TPU v7x, 256 devices: a whole 4x4x8 slice. The times are simulated.
256 devices in a mesh: wide: 64 (over y, z, core), narrow: 4 (over x).
Axes of the slice: x: 4, y: 4, z: 8, core: 2. Of those that a mesh axis runs over, the one named last changes fastest.
Arguments:
- embedding: float32 [131072, 128], P(('wide', 'narrow'))
- tile_blocks: bfloat16 [64, 4, 22, 512, 512], P('wide', 'narrow'), may hold values from -0.125 to 0.125
- tile_row: int32 [64, 4, 22], P('wide', 'narrow'), may hold values from 0 to 3
- tile_col: int32 [64, 4, 22], P('wide', 'narrow'), may hold values from 0 to 63
- counts: int32 [64, 4], P('wide', 'narrow'), may hold values from 1 to 22, as said below
Outputs:
- orthonormal: float32 [131072, 128], P(('wide', 'narrow'))
Inputs may be any that keep to these rules, and one draw needn't show every extreme that they name: Slots 0 to counts[w, n] - 1 of device (w, n) hold its tiles, the others are unused; some device has all 22 slots live.
All inputs are finite; a program needn't handle non-finite values.
Results may differ from a plain program's by a relative error of at most 0.0036.
Values may be sent and summed in bfloat16 or wider, within the bound.
No kernel may reach another device: no remote copies, remote signals or barrier semaphores. Data moves between devices by JAX's collectives and lax.ppermute only.
A program may use at most 64 MiB of HBM per device.

v0:
```python
import functools

import jax
import jax.numpy as jnp
import numpy as np
from jax import lax
from jax.experimental import pallas as pl
from jax.experimental.pallas import tpu as pltpu
from jax.sharding import Mesh, PartitionSpec as P

NY, NZ, NC, NX = 4, 8, 2, 4
PLANE = ("y", "z", "c")


def plane_index(y, z, c):
    return ((y % NY) * NZ + z % NZ) * NC + c


def step_pairs(hop):
    first = []
    for y in range(NY):
        for z in range(NZ):
            first.append((plane_index(y, z, 0), plane_index(y, z + hop, 0)))
            first.append((plane_index(y, z, 1), plane_index(y + hop, z, 1)))
    return first


def bundle_pairs(hop):
    second = []
    for y in range(NY):
        for z in range(NZ):
            second.append((plane_index(y, z, 0), plane_index(y + hop, z, 0)))
            second.append((plane_index(y, z, 1), plane_index(y, z + hop, 1)))
    return second


def axis_shift(value, axis, hop):
    n = lax.axis_size(axis)
    return lax.ppermute(value, axis, [(i, (i + hop) % n) for i in range(n)])


def axis_swap(value, axis, bit):
    n = lax.axis_size(axis)
    return lax.ppermute(value, axis, [(i, i ^ bit) for i in range(n)])


def stack_blocks(parts):
    which = lax.broadcasted_iota(jnp.int32, (len(parts), 1, 1), 0)
    shape = (len(parts),) + parts[0].shape
    out = jnp.broadcast_to(parts[-1][None], shape)
    for i in range(len(parts) - 2, -1, -1):
        out = jnp.where(which == i, parts[i][None], out)
    return out


def far_pairs():
    pairs = []
    for y in range(NY):
        for z in range(NZ):
            pairs.append((plane_index(y, z, 0), plane_index(y, z - 2, 0)))
            pairs.append((plane_index(y, z, 1), plane_index(y, z + 4, 1)))
    return pairs


def send(value, pairs):
    return lax.ppermute(value, PLANE, pairs)


def swap(value):
    return axis_shift(value, "c", 1)


def gather_blocks(block, core):
    zero = core == 0
    plus1, minus1, plus2 = step_pairs(1), step_pairs(-1), step_pairs(2)
    bplus, bminus = bundle_pairs(1), bundle_pairs(-1)
    a1 = send(block, plus1)
    a2 = send(block, minus1)
    a3 = send(block, plus2)
    a4 = send(block, far_pairs())
    lo = stack_blocks([block, a1, a2, a3])
    g1p = send(lo, bplus)
    g1m = send(lo, bminus)
    onward = jnp.where(zero, a3, a4)
    a5 = send(onward, plus1)
    a6 = send(a4, minus1)
    a7 = send(onward, plus2)
    hi = stack_blocks([a4, a5, a6, a7])
    g2p = send(g1p, bplus)
    second_minus, hi_kept = lax.optimization_barrier((jnp.where(zero, hi, g1m), hi))
    g2m = send(second_minus, bminus)
    g3p = send(jnp.where(zero, hi_kept, g2p), bplus)
    g3m = send(g2m, bminus)
    mine = [lo, hi_kept, g1p, g1m, g2p, g2m, g3p, g3m]
    theirs = [swap(v) for v in mine]
    return mine + theirs


def place_table():
    table = np.zeros((NC, NY, NZ), np.int32)
    lo_z, hi_z, col_y = [0, -1, 1, -2], [2, -3, 3, -4], [0, -1, 1, -2]
    rows = ((0, 0, lo_z), (1, 0, hi_z), (2, -1, lo_z), (3, 1, lo_z), (4, -2, lo_z), (5, 1, hi_z), (6, -1, hi_z), (7, 2, hi_z))
    columns = ((0, 0), (1, 4), (2, -1), (3, 1), (4, -2), (5, 2), (6, -3), (7, 3))
    for off in range(4):
        for piece, dy, offsets in rows:
            table[0, dy % NY, offsets[off] % NZ] = piece * 4 + off
        for piece, dz in columns:
            table[1, col_y[off] % NY, dz % NZ] = piece * 4 + off
    assert all(sorted(t.reshape(-1)) == list(range(NY * NZ)) for t in table)
    return table.reshape(-1)


def tile_kernel(rows, cols, counts, table, tiles, *refs):
    *pieces, own_ref, one_ref, two_ref, three_ref, acc, picked, held, sems = refs
    span = pieces[0].shape[0]
    slots = tiles.shape[0]
    live = counts[0]
    y, z, core, x = (lax.axis_index(a) for a in ("y", "z", "c", "x"))

    def place_of(s):
        col = cols[s]
        from_y, from_z, from_c = (col // (NZ * NC)) & (NY - 1), (col // NC) & (NZ - 1), col & (NC - 1)
        dy, dz = (from_y - y) & (NY - 1), (from_z - z) & (NZ - 1)
        place = table[(from_c * NY + dy) * NZ + dz]
        return place + jnp.where(from_c == core, 0, NY * NZ)

    def load(pair):
        return pltpu.make_async_copy(tiles.at[pl.ds(2 * pair, 2)], held.at[pl.ds(2 * pair, 2)], sems.at[pair])

    for pair in range(slots // 2):

        @pl.when(2 * pair < live)
        def _():
            load(pair).start()

    acc[...] = jnp.zeros_like(acc)

    def work(pair, carry):
        both = (2 * pair, 2 * pair + 1)
        for i, s in enumerate(both):
            place = place_of(s)
            for p, piece in enumerate(pieces):

                @pl.when(place // span == p)
                def _():
                    picked[i] = piece[place % span]

        load(pair).wait()
        products = [
            jnp.dot(held[s], picked[i], preferred_element_type=jnp.float32) for i, s in enumerate(both)
        ]
        for i, s in enumerate(both):
            row = jnp.where(s < live, (rows[s] - x) & (NX - 1), NX)
            acc[row] += products[i]
        return carry

    lax.fori_loop(0, (live + 1) // 2, work, 0)
    own_ref[...] = acc[0]
    one_ref[...] = acc[1].astype(jnp.bfloat16)
    two_ref[...] = acc[2].astype(jnp.bfloat16)
    three_ref[...] = acc[3].astype(jnp.bfloat16)


def apply_operator(block, tiles, lists, core):
    slots, tile, _ = tiles.shape
    assert slots % 2 == 0
    width = block.shape[1]
    pieces = gather_blocks(block, core)
    vmem = pl.BlockSpec(memory_space=pltpu.VMEM)
    shape = lambda t: jax.ShapeDtypeStruct((tile, width), t)
    own, one, two, three = pl.pallas_call(
        tile_kernel,
        out_shape=[shape(jnp.float32)] + [shape(jnp.bfloat16)] * 3,
        in_specs=[pl.BlockSpec(memory_space=pltpu.SMEM)] * 4 + [pl.BlockSpec(memory_space=pl.ANY)] + [vmem] * len(pieces),
        out_specs=[vmem] * 4,
        scratch_shapes=[
            pltpu.VMEM((NX + 1, tile, width), jnp.float32),
            pltpu.VMEM((2, tile, width), jnp.bfloat16),
            pltpu.VMEM((slots, tile, tile), jnp.bfloat16),
            pltpu.SemaphoreType.DMA((slots // 2,)),
        ],
        compiler_params=pltpu.CompilerParams(vmem_limit_bytes=40 << 20),
        cost_estimate=pl.CostEstimate(
            flops=2 * slots * tile * tile * width, bytes_accessed=slots * tile * (tile + width) * 2, transcendentals=0
        ),
        name="tile_products",
    )(*lists, tiles, *pieces)
    f32 = jnp.float32
    one = axis_shift(one, "x", 1)
    three = axis_shift(three, "x", 3)
    two = axis_shift(two, "x", 2)
    return own + one.astype(f32) + three.astype(f32) + two.astype(f32)


def sum_over_devices(gram):
    gram = gram + axis_swap(gram, "c", 1)
    for axis in ("x", "y"):
        gram = gram + axis_shift(gram, axis, 1) + axis_shift(gram, axis, 3) + axis_shift(gram, axis, 2)
    gram = gram + axis_shift(gram, "z", 2) + axis_shift(gram, "z", 6) + axis_shift(gram, "z", 4)
    return gram + axis_swap(gram, "z", 1)


STEP = 8


def finish_kernel(scale, gram_ref, spectral_ref, out_ref, work):
    n = gram_ref.shape[0]
    row_id = lax.broadcasted_iota(jnp.int32, (n, n), 0)
    col_id = lax.broadcasted_iota(jnp.int32, (n, n), 1)
    work[:, :n] = gram_ref[...]
    work[:, n:] = jnp.where(row_id == col_id, 1.0, 0.0)
    sub = lax.broadcasted_iota(jnp.int32, (STEP, n), 0)
    for k in range(n // STEP):
        lo = k * STEP
        left = work[lo : lo + STEP, :n]
        right = work[lo : lo + STEP, n:]
        columns = [jnp.broadcast_to(left[:, lo + j : lo + j + 1], (STEP, n)) for j in range(STEP)]
        for j in range(STEP):
            inv = lax.rsqrt(columns[j][j : j + 1, :])
            inv = inv * (1.5 - 0.5 * columns[j][j : j + 1, :] * inv * inv)
            row_l, row_r = left[j : j + 1, :] * inv, right[j : j + 1, :] * inv
            factor = jnp.where(sub > j, columns[j] * inv, 0.0)
            here = sub == j
            left = jnp.where(here, row_l, left - factor * row_l)
            right = jnp.where(here, row_r, right - factor * row_r)
            for i in range(j + 1, STEP):
                columns[i] = columns[i] - factor * (columns[i][j : j + 1, :] * inv)
        work[lo : lo + STEP, :n] = left
        work[lo : lo + STEP, n:] = right
        hi = lo + STEP
        if hi < n:
            panel = left[:, hi:]
            both = jnp.concatenate([left, right], axis=1)
            work[hi:, :] = work[hi:, :] - lax.dot_general(
                panel, both, (((0,), (0,)), ((), ())), precision=lax.Precision.HIGHEST,
                preferred_element_type=jnp.float32)
    out_ref[...] = lax.dot_general(
        spectral_ref[...], work[:, n:] * scale, (((1,), (1,)), ((), ())), precision=lax.Precision.HIGHEST,
        preferred_element_type=jnp.float32)


def finish(gram, spectral, scale):
    n = gram.shape[0]
    vmem = pl.BlockSpec(memory_space=pltpu.VMEM)
    return pl.pallas_call(functools.partial(finish_kernel, scale),
        out_shape=jax.ShapeDtypeStruct(spectral.shape, jnp.float32),
        in_specs=[vmem, vmem], out_specs=vmem,
        scratch_shapes=[pltpu.VMEM((n, 2*n), jnp.float32)], name="orthonormalize")(gram, spectral)


def local(embedding, tile_blocks, tile_row, tile_col, counts):
    tiles = tile_blocks.reshape(tile_blocks.shape[-3:])
    slots = tiles.shape[0]
    core = lax.axis_index("c")
    lists = (tile_row.reshape(slots), tile_col.reshape(slots), counts.reshape(1), jnp.asarray(place_table()))

    def apply_once(_, carry):
        block, _, latest = carry
        applied = apply_operator(block, tiles, lists, core)
        return applied.astype(jnp.bfloat16), latest, applied

    start = (embedding.astype(jnp.bfloat16), jnp.zeros_like(embedding), embedding)
    _, first_order, applied = lax.fori_loop(0, 2, apply_once, start)
    second = 2.0 * applied - embedding
    spectral = 1.2661 * embedding - 1.1303 * first_order + 0.2715 * second
    gram = lax.dot_general(
        spectral, spectral, (((0,), (0,)), ((), ())), precision=lax.Precision.HIGHEST
    )
    node_total = embedding.shape[0] * NY * NZ * NC * NX
    return finish(sum_over_devices(gram), spectral, float(np.sqrt(node_total)))


def solution(mesh):
    fine = Mesh(mesh.devices.reshape(NY, NZ, NC, NX), ("y", "z", "c", "x"))
    wide = ("y", "z", "c")
    placed = (
        P(("y", "z", "c", "x"), None),
        P(wide, "x", None, None, None),
        P(wide, "x", None),
        P(wide, "x", None),
        P(wide, "x"),
    )
    return jax.shard_map(
        local, mesh=fine, in_specs=placed, out_specs=P(("y", "z", "c", "x"), None), check_vma=False
    )
```

profile of v0, /device:TPU:1, one launch (start us, length us, event | category | flops | bytes accessed | tf_op | source)
XLA Modules:
  0.0 197.5 jit_solution(3616549695815340836)
XLA Ops:
  1.9 154.1 %while.17 = (s32[]{:T(128)}, bf16[512,128]{1,0:T(8,128)(2,1)S(1)}, f32[512,128]{1,0:T(8,128)}, f32[512,128]{1,0:T(8,128)S(1)}, pred[]{:T(512)}, /*index=5*/s32[2...) while((s32[]{:T(128)}, bf16[512,128]{1,0:T(8,128)(2,1)S(1)}, ...), condition=%wide.region_1.2_spmd.clone, body=%wide.region_0.1_spmd.sunk.clone.sunk | while | flops 1479016448 | bytes 55706708 | solution.py:263
  1.9 3.6 %collective-permute-start.1 = (bf16[512,128]{1,0:T(8,128)(2,1)S(1)}, bf16[512,128]{1,0:T(8,128)(2,1)S(1)}, u32[]{:S(2)}, u32[]{:S(2)}) collective-permute-start(bf16[512,128]{1,0:T(8,128)(2,1)S(1)} %get-tuple-element.271), channel_id=1, source_target_pairs={{0,56},{4,196},{8,0},{12,204},{16,8},{20,212},{24,16},{28,220},{32... | collective-permute-start | bytes 393224 | tf_op jit(solution)/shard_map/while/body/eval_jaxpr/ppermute | solution.py:66
  6.5 2.3 %collective-permute-done.1 = bf16[512,128]{1,0:T(8,128)(2,1)S(1)} collective-permute-done((bf16[512,128]{1,0:T(8,128)(2,1)S(1)}, bf16[512,128]{1,0:T(8,128)(2,1)S(1)}, u32[]{:S(2)}, u32[]{:S(2)}) %collective-permute-start.1) | collective-permute-done | bytes 131104 | tf_op jit(solution)/shard_map/while/body/eval_jaxpr/ppermute | solution.py:66
  8.8 2.1 %collective-permute-done = bf16[512,128]{1,0:T(8,128)(2,1)S(1)} collective-permute-done((bf16[512,128]{1,0:T(8,128)(2,1)S(1)}, bf16[512,128]{1,0:T(8,128)(2,1)S(1)}, u32[]{:S(2)}, u32[]{:S(2)}) %collective-permute-start) | collective-permute-done | bytes 131104 | tf_op jit(solution)/shard_map/while/body/eval_jaxpr/ppermute | solution.py:66
  12.4 1.9 collective-permute-start.8
  14.3 3.9 %collective-permute-start.3 = (bf16[4,512,128]{2,1,0:T(8,128)(2,1)S(1)}, bf16[4,512,128]{2,1,0:T(8,128)(2,1)S(1)}, u32[]{:S(2)}, u32[]{:S(2)}) collective-permute-start(bf16[4,512,128]{2,1,0:T(8,128)(2,1)S(1)} %select_select_fusion.4.refs_0_), channel_id=1, source_target_pairs={{0,192},{4,60},{8,200},{12,4},{16,208},{20,12},{24,216},{28,20},{3... | collective-permute-start | bytes 1572872 | tf_op jit(solution)/shard_map/while/body/eval_jaxpr/ppermute | solution.py:66
  18.1 4.2 %collective-permute-start.4 = (bf16[512,128]{1,0:T(8,128)(2,1)S(1)}, bf16[512,128]{1,0:T(8,128)(2,1)S(1)}, u32[]{:S(2)}, u32[]{:S(2)}) collective-permute-start(bf16[512,128]{1,0:T(8,128)(2,1)S(1)} %get-tuple-element.271), channel_id=1, source_target_pairs={{0,48},{4,36},{8,56},{12,44},{16,0},{20,52},{24,8},{28,60},{32,16}... | collective-permute-start | bytes 393224 | tf_op jit(solution)/shard_map/while/body/eval_jaxpr/ppermute | solution.py:66
  22.3 7.1 %collective-permute-done.4 = bf16[512,128]{1,0:T(8,128)(2,1)S(1)} collective-permute-done((bf16[512,128]{1,0:T(8,128)(2,1)S(1)}, bf16[512,128]{1,0:T(8,128)(2,1)S(1)}, u32[]{:S(2)}, u32[]{:S(2)}) %collective-permute-start.4) | collective-permute-done | bytes 131104 | tf_op jit(solution)/shard_map/while/body/eval_jaxpr/ppermute | solution.py:66
  29.6 1.7 collective-permute-start.5
  32.3 2.4 %collective-permute-start.9 = (bf16[4,512,128]{2,1,0:T(8,128)(2,1)S(1)}, bf16[4,512,128]{2,1,0:T(8,128)(2,1)S(1)}, u32[]{:S(2)}, u32[]{:S(2)}) collective-permute-start(bf16[4,512,128]{2,1,0:T(8,128)(2,1)S(1)} %collective-permute-done.8.refs_2_), channel_id=1, source_target_pairs={{0,64},{4,12},{8,72},{12,20},{16,80},{20,28},{24,88},{28,36},{32,9... | collective-permute-start | bytes 1572872 | tf_op jit(solution)/shard_map/while/body/eval_jaxpr/ppermute | solution.py:66
  37.1 5.4 %collective-permute-start.10 = (bf16[4,512,128]{2,1,0:T(8,128)(2,1)S(1)}, bf16[4,512,128]{2,1,0:T(8,128)(2,1)S(1)}, u32[]{:S(2)}, u32[]{:S(2)}) collective-permute-start(bf16[4,512,128]{2,1,0:T(8,128)(2,1)S(1)} %get-tuple-element.252), channel_id=1, source_target_pairs={{0,192},{4,60},{8,200},{12,4},{16,208},{20,12},{24,216},{28,20},{3... | collective-permute-start | bytes 1572872 | tf_op jit(solution)/shard_map/while/body/eval_jaxpr/ppermute | solution.py:66
  44.4 4.3 %collective-permute-done.10.refs_5_ = bf16[4,512,128]{2,1,0:T(8,128)(2,1)S(1)} collective-permute-done((bf16[4,512,128]{2,1,0:T(8,128)(2,1)S(1)}, bf16[4,512,128]{2,1,0:T(8,128)(2,1)S(1)}, u32[]{:S(2)}, u32[]{:S(2)}) %collective-permute-start.10) | collective-permute-done | bytes 524320 | tf_op jit(solution)/shard_map/while/body/eval_jaxpr/ppermute | solution.py:66
  48.7 3.4 %collective-permute-start.12 = (bf16[4,512,128]{2,1,0:T(8,128)(2,1)S(1)}, bf16[4,512,128]{2,1,0:T(8,128)(2,1)S(1)}, u32[]{:S(2)}, u32[]{:S(2)}) collective-permute-start(bf16[4,512,128]{2,1,0:T(8,128)(2,1)S(1)} %collective-permute-done.10.refs_5_), channel_id=1, source_target_pairs={{0,192},{4,60},{8,200},{12,4},{16,208},{20,12},{24,216},{28,20},{3... | collective-permute-start | bytes 1572872 | tf_op jit(solution)/shard_map/while/body/eval_jaxpr/ppermute | solution.py:66
  55.0 3.2 %collective-permute-done.12.refs_7_ = bf16[4,512,128]{2,1,0:T(8,128)(2,1)S(1)} collective-permute-done((bf16[4,512,128]{2,1,0:T(8,128)(2,1)S(1)}, bf16[4,512,128]{2,1,0:T(8,128)(2,1)S(1)}, u32[]{:S(2)}, u32[]{:S(2)}) %collective-permute-start.12) | collective-permute-done | bytes 524320 | tf_op jit(solution)/shard_map/while/body/eval_jaxpr/ppermute | solution.py:66
  58.5 1.6 collective-permute-done.20.refs_15_
  60.1 6.5 %tile_products.3 = (f32[512,128]{1,0:T(8,128)S(1)}, bf16[512,128]{1,0:T(8,128)(2,1)S(1)}, bf16[512,128]{1,0:T(8,128)(2,1)S(1)}, bf16[512,128]{1,0:T(8,128)(2,1)S(1)}) custom-call(s32[22]{0:T(128)} %get-tuple-element.286.rows, s32[22]{0:T(128)} %get-tuple-element.287.cols, s32[1]{0:T(128)} %get-tuple-element.288.counts, s32[64]{0:T(128)} %get-tuple-element.291.table, ...), custom_call_target="tpu_custom_call" | custom-call | flops 1476395008 | bytes 14417920 | tf_op jit(solution)/shard_map/while/body/eval_jaxpr/tile_products/pallas_call | solution.py:171
  66.8 3.6 %collective-permute-start.22 = (bf16[512,128]{1,0:T(8,128)(2,1)S(1)}, bf16[512,128]{1,0:T(8,128)(2,1)S(1)}, u32[]{:S(2)}, u32[]{:S(2)}) collective-permute-start(bf16[512,128]{1,0:T(8,128)(2,1)S(1)} %get-tuple-element.254), channel_id=1, source_target_pairs={{0,3},{1,0},{2,1},{3,2},{4,7},{5,4},{6,5},{7,6},{8,11},{9,8},{10,9... | collective-permute-start | bytes 393224 | tf_op jit(solution)/shard_map/while/body/eval_jaxpr/ppermute | solution.py:39
  72.3 3.1 %collective-permute-done.23 = bf16[512,128]{1,0:T(8,128)(2,1)S(1)} collective-permute-done((bf16[512,128]{1,0:T(8,128)(2,1)S(1)}, bf16[512,128]{1,0:T(8,128)(2,1)S(1)}, u32[]{:S(2)}, u32[]{:S(2)}) %collective-permute-start.23) | collective-permute-done | bytes 131104 | tf_op jit(solution)/shard_map/while/body/eval_jaxpr/ppermute | solution.py:39
  75.5 6.6 %collective-permute-start.1 = (bf16[512,128]{1,0:T(8,128)(2,1)S(1)}, bf16[512,128]{1,0:T(8,128)(2,1)S(1)}, u32[]{:S(2)}, u32[]{:S(2)}) collective-permute-start(bf16[512,128]{1,0:T(8,128)(2,1)S(1)} %get-tuple-element.271), channel_id=1, source_target_pairs={{0,56},{4,196},{8,0},{12,204},{16,8},{20,212},{24,16},{28,220},{32... | collective-permute-start | bytes 393224 | tf_op jit(solution)/shard_map/while/body/eval_jaxpr/ppermute | solution.py:66
  82.7 2.6 %collective-permute-done.1 = bf16[512,128]{1,0:T(8,128)(2,1)S(1)} collective-permute-done((bf16[512,128]{1,0:T(8,128)(2,1)S(1)}, bf16[512,128]{1,0:T(8,128)(2,1)S(1)}, u32[]{:S(2)}, u32[]{:S(2)}) %collective-permute-start.1) | collective-permute-done | bytes 131104 | tf_op jit(solution)/shard_map/while/body/eval_jaxpr/ppermute | solution.py:66
  85.4 2.1 %collective-permute-done = bf16[512,128]{1,0:T(8,128)(2,1)S(1)} collective-permute-done((bf16[512,128]{1,0:T(8,128)(2,1)S(1)}, bf16[512,128]{1,0:T(8,128)(2,1)S(1)}, u32[]{:S(2)}, u32[]{:S(2)}) %collective-permute-start) | collective-permute-done | bytes 131104 | tf_op jit(solution)/shard_map/while/body/eval_jaxpr/ppermute | solution.py:66
  89.0 3.9 %collective-permute-start.8 = (bf16[4,512,128]{2,1,0:T(8,128)(2,1)S(1)}, bf16[4,512,128]{2,1,0:T(8,128)(2,1)S(1)}, u32[]{:S(2)}, u32[]{:S(2)}) collective-permute-start(bf16[4,512,128]{2,1,0:T(8,128)(2,1)S(1)} %select_select_fusion.4.refs_0_), channel_id=1, source_target_pairs={{0,64},{4,12},{8,72},{12,20},{16,80},{20,28},{24,88},{28,36},{32,9... | collective-permute-start | bytes 1572872 | tf_op jit(solution)/shard_map/while/body/eval_jaxpr/ppermute | solution.py:66
  93.2 1.8 collective-permute-start.4
  95.0 6.0 %collective-permute-done.4 = bf16[512,128]{1,0:T(8,128)(2,1)S(1)} collective-permute-done((bf16[512,128]{1,0:T(8,128)(2,1)S(1)}, bf16[512,128]{1,0:T(8,128)(2,1)S(1)}, u32[]{:S(2)}, u32[]{:S(2)}) %collective-permute-start.4) | collective-permute-done | bytes 131104 | tf_op jit(solution)/shard_map/while/body/eval_jaxpr/ppermute | solution.py:66
  101.2 2.7 %collective-permute-start.5 = (bf16[512,128]{1,0:T(8,128)(2,1)S(1)}, bf16[512,128]{1,0:T(8,128)(2,1)S(1)}, u32[]{:S(2)}, u32[]{:S(2)}) collective-permute-start(bf16[512,128]{1,0:T(8,128)(2,1)S(1)} %broadcast_select_fusion.6), channel_id=1, source_target_pairs={{0,16},{4,132},{8,24},{12,140},{16,32},{20,148},{24,40},{28,156},{... | collective-permute-start | bytes 393224 | tf_op jit(solution)/shard_map/while/body/eval_jaxpr/ppermute | solution.py:66
  103.9 3.6 %collective-permute-start.9 = (bf16[4,512,128]{2,1,0:T(8,128)(2,1)S(1)}, bf16[4,512,128]{2,1,0:T(8,128)(2,1)S(1)}, u32[]{:S(2)}, u32[]{:S(2)}) collective-permute-start(bf16[4,512,128]{2,1,0:T(8,128)(2,1)S(1)} %collective-permute-done.8.refs_2_), channel_id=1, source_target_pairs={{0,64},{4,12},{8,72},{12,20},{16,80},{20,28},{24,88},{28,36},{32,9... | collective-permute-start | bytes 1572872 | tf_op jit(solution)/shard_map/while/body/eval_jaxpr/ppermute | solution.py:66
  108.5 6.7 %collective-permute-start.10 = (bf16[4,512,128]{2,1,0:T(8,128)(2,1)S(1)}, bf16[4,512,128]{2,1,0:T(8,128)(2,1)S(1)}, u32[]{:S(2)}, u32[]{:S(2)}) collective-permute-start(bf16[4,512,128]{2,1,0:T(8,128)(2,1)S(1)} %get-tuple-element.252), channel_id=1, source_target_pairs={{0,192},{4,60},{8,200},{12,4},{16,208},{20,12},{24,216},{28,20},{3... | collective-permute-start | bytes 1572872 | tf_op jit(solution)/shard_map/while/body/eval_jaxpr/ppermute | solution.py:66
  115.3 6.7 %collective-permute-start.13 = (bf16[4,512,128]{2,1,0:T(8,128)(2,1)S(1)}, bf16[4,512,128]{2,1,0:T(8,128)(2,1)S(1)}, u32[]{:S(2)}, u32[]{:S(2)}) collective-permute-start(bf16[4,512,128]{2,1,0:T(8,128)(2,1)S(1)} %select_select_fusion.4.refs_0_), channel_id=1, source_target_pairs={{0,4},{4,0},{1,5},{5,1},{2,6},{6,2},{3,7},{7,3},{8,12},{12,8},{9,1... | collective-permute-start | bytes 1572872 | tf_op jit(solution)/shard_map/while/body/eval_jaxpr/ppermute | solution.py:39
  122.6 2.7 %collective-permute-start.12 = (bf16[4,512,128]{2,1,0:T(8,128)(2,1)S(1)}, bf16[4,512,128]{2,1,0:T(8,128)(2,1)S(1)}, u32[]{:S(2)}, u32[]{:S(2)}) collective-permute-start(bf16[4,512,128]{2,1,0:T(8,128)(2,1)S(1)} %collective-permute-done.10.refs_5_), channel_id=1, source_target_pairs={{0,192},{4,60},{8,200},{12,4},{16,208},{20,12},{24,216},{28,20},{3... | collective-permute-start | bytes 1572872 | tf_op jit(solution)/shard_map/while/body/eval_jaxpr/ppermute | solution.py:66
  125.3 7.1 %collective-permute-start.16 = (bf16[4,512,128]{2,1,0:T(8,128)(2,1)S(1)}, bf16[4,512,128]{2,1,0:T(8,128)(2,1)S(1)}, u32[]{:S(2)}, u32[]{:S(2)}) collective-permute-start(bf16[4,512,128]{2,1,0:T(8,128)(2,1)S(1)} %collective-permute-done.3.refs_3_), channel_id=1, source_target_pairs={{0,4},{4,0},{1,5},{5,1},{2,6},{6,2},{3,7},{7,3},{8,12},{12,8},{9,1... | collective-permute-start | bytes 1572872 | tf_op jit(solution)/shard_map/while/body/eval_jaxpr/ppermute | solution.py:39
  133.0 6.0 %collective-permute-start.20 = (bf16[4,512,128]{2,1,0:T(8,128)(2,1)S(1)}, bf16[4,512,128]{2,1,0:T(8,128)(2,1)S(1)}, u32[]{:S(2)}, u32[]{:S(2)}) collective-permute-start(bf16[4,512,128]{2,1,0:T(8,128)(2,1)S(1)} %collective-permute-done.12.refs_7_), channel_id=1, source_target_pairs={{0,4},{4,0},{1,5},{5,1},{2,6},{6,2},{3,7},{7,3},{8,12},{12,8},{9,1... | collective-permute-start | bytes 1572872 | tf_op jit(solution)/shard_map/while/body/eval_jaxpr/ppermute | solution.py:39
  139.1 1.5 collective-permute-done.20.refs_15_
  140.6 6.5 %tile_products.3 = (f32[512,128]{1,0:T(8,128)S(1)}, bf16[512,128]{1,0:T(8,128)(2,1)S(1)}, bf16[512,128]{1,0:T(8,128)(2,1)S(1)}, bf16[512,128]{1,0:T(8,128)(2,1)S(1)}) custom-call(s32[22]{0:T(128)} %get-tuple-element.286.rows, s32[22]{0:T(128)} %get-tuple-element.287.cols, s32[1]{0:T(128)} %get-tuple-element.288.counts, s32[64]{0:T(128)} %get-tuple-element.291.table, ...), custom_call_target="tpu_custom_call" | custom-call | flops 1476395008 | bytes 14417920 | tf_op jit(solution)/shard_map/while/body/eval_jaxpr/tile_products/pallas_call | solution.py:171
  147.3 1.5 collective-permute-start.23
  149.5 4.4 %collective-permute-done.21 = bf16[512,128]{1,0:T(8,128)(2,1)S(1)} collective-permute-done((bf16[512,128]{1,0:T(8,128)(2,1)S(1)}, bf16[512,128]{1,0:T(8,128)(2,1)S(1)}, u32[]{:S(2)}, u32[]{:S(2)}) %collective-permute-start.21) | collective-permute-done | bytes 131104 | tf_op jit(solution)/shard_map/while/body/eval_jaxpr/ppermute | solution.py:39
  153.9 1.8 collective-permute-done.23
  160.7 3.1 %collective-permute-done.27 = f32[128,128]{1,0:T(8,128)S(1)} collective-permute-done((f32[128,128]{1,0:T(8,128)S(1)}, f32[128,128]{1,0:T(8,128)S(1)}, u32[]{:S(2)}, u32[]{:S(2)}) %collective-permute-start.27) | collective-permute-done | bytes 65568 | tf_op jit(solution)/shard_map/ppermute | solution.py:39
  163.8 2.2 %collective-permute-done.25 = f32[128,128]{1,0:T(8,128)S(1)} collective-permute-done((f32[128,128]{1,0:T(8,128)S(1)}, f32[128,128]{1,0:T(8,128)S(1)}, u32[]{:S(2)}, u32[]{:S(2)}) %collective-permute-start.25) | collective-permute-done | bytes 65568 | tf_op jit(solution)/shard_map/ppermute | solution.py:39
  166.0 2.6 %collective-permute-start.30 = (f32[128,128]{1,0:T(8,128)S(1)}, f32[128,128]{1,0:T(8,128)S(1)}, u32[]{:S(2)}, u32[]{:S(2)}) collective-permute-start(f32[128,128]{1,0:T(8,128)S(1)} %add_add_fusion.2), channel_id=1, source_target_pairs={{0,128},{64,192},{128,0},{192,64},{1,129},{65,193},{129,1},{193,65... | collective-permute-start | bytes 196616 | tf_op jit(solution)/shard_map/ppermute | solution.py:39
  168.6 1.6 collective-permute-start.29
  170.8 2.3 %collective-permute-done.29 = f32[128,128]{1,0:T(8,128)S(1)} collective-permute-done((f32[128,128]{1,0:T(8,128)S(1)}, f32[128,128]{1,0:T(8,128)S(1)}, u32[]{:S(2)}, u32[]{:S(2)}) %collective-permute-start.29) | collective-permute-done | bytes 65568 | tf_op jit(solution)/shard_map/ppermute | solution.py:39
  173.0 1.5 collective-permute-done.28
  174.7 1.6 collective-permute-start.32
  176.2 2.0 %collective-permute-start.31 = (f32[128,128]{1,0:T(8,128)S(1)}, f32[128,128]{1,0:T(8,128)S(1)}, u32[]{:S(2)}, u32[]{:S(2)}) collective-permute-start(f32[128,128]{1,0:T(8,128)S(1)} %add_add_fusion.1), channel_id=1, source_target_pairs={{0,16},{8,24},{16,32},{24,40},{32,48},{40,56},{48,0},{56,8},{1,17}... | collective-permute-start | bytes 196616 | tf_op jit(solution)/shard_map/ppermute | solution.py:39
  178.2 3.5 %collective-permute-done.33 = f32[128,128]{1,0:T(8,128)S(1)} collective-permute-done((f32[128,128]{1,0:T(8,128)S(1)}, f32[128,128]{1,0:T(8,128)S(1)}, u32[]{:S(2)}, u32[]{:S(2)}) %collective-permute-start.33) | collective-permute-done | bytes 65568 | tf_op jit(solution)/shard_map/ppermute | solution.py:39
  182.4 2.7 %collective-permute-start.34 = (f32[128,128]{1,0:T(8,128)S(1)}, f32[128,128]{1,0:T(8,128)S(1)}, u32[]{:S(2)}, u32[]{:S(2)}) collective-permute-start(f32[128,128]{1,0:T(8,128)S(1)} %add_add_fusion), channel_id=1, source_target_pairs={{0,8},{8,0},{16,24},{24,16},{32,40},{40,32},{48,56},{56,48},{1,9},... | collective-permute-start | bytes 196616 | tf_op jit(solution)/shard_map/ppermute | solution.py:44
  185.1 1.7 collective-permute-done.34
  187.4 10.1 %orthonormalize.1 = f32[512,128]{1,0:T(8,128)} custom-call(f32[128,128]{1,0:T(8,128)} %add.67.gram_ref, f32[512,128]{1,0:T(8,128)} %copy-done), custom_call_target="tpu_custom_call" | custom-call | tf_op jit(solution)/shard_map/orthonormalize/pallas_call | solution.py:245
  (104 shorter events, 27.6 us)
Async XLA Ops:
  1.9 6.9 %collective-permute-start.1 = (bf16[512,128]{1,0:T(8,128)(2,1)S(1)}, bf16[512,128]{1,0:T(8,128)(2,1)S(1)}, u32[]{:S(2)}, u32[]{:S(2)}) collective-permute-start(bf16[512,128]{1,0:T(8,128)(2,1)S(1)} %get-tuple-element.271), channel_id=1, source_target_pairs={{0,56},{4,196},{8,0},{12,204},{16,8},{20,212},{24,16},{28,220},{32... | collective-permute-start | bytes 393224 | tf_op jit(solution)/shard_map/while/body/eval_jaxpr/ppermute | solution.py:66
  5.5 5.4 %collective-permute-start = (bf16[512,128]{1,0:T(8,128)(2,1)S(1)}, bf16[512,128]{1,0:T(8,128)(2,1)S(1)}, u32[]{:S(2)}, u32[]{:S(2)}) collective-permute-start(bf16[512,128]{1,0:T(8,128)(2,1)S(1)} %get-tuple-element.271), channel_id=1, source_target_pairs={{0,16},{4,132},{8,24},{12,140},{16,32},{20,148},{24,40},{28,156},{... | collective-permute-start | bytes 393224 | tf_op jit(solution)/shard_map/while/body/eval_jaxpr/ppermute | solution.py:66
  5.8 6.4 %collective-permute-start.2 = (bf16[512,128]{1,0:T(8,128)(2,1)S(1)}, bf16[512,128]{1,0:T(8,128)(2,1)S(1)}, u32[]{:S(2)}, u32[]{:S(2)}) collective-permute-start(bf16[512,128]{1,0:T(8,128)(2,1)S(1)} %get-tuple-element.271), channel_id=1, source_target_pairs={{0,8},{4,68},{8,16},{12,76},{16,24},{20,84},{24,32},{28,92},{32,40... | collective-permute-start | bytes 393224 | tf_op jit(solution)/shard_map/while/body/eval_jaxpr/ppermute | solution.py:66
  12.4 19.9 %collective-permute-start.8 = (bf16[4,512,128]{2,1,0:T(8,128)(2,1)S(1)}, bf16[4,512,128]{2,1,0:T(8,128)(2,1)S(1)}, u32[]{:S(2)}, u32[]{:S(2)}) collective-permute-start(bf16[4,512,128]{2,1,0:T(8,128)(2,1)S(1)} %select_select_fusion.4.refs_0_), channel_id=1, source_target_pairs={{0,64},{4,12},{8,72},{12,20},{16,80},{20,28},{24,88},{28,36},{32,9... | collective-permute-start | bytes 1572872 | tf_op jit(solution)/shard_map/while/body/eval_jaxpr/ppermute | solution.py:66
  14.3 22.7 %collective-permute-start.3 = (bf16[4,512,128]{2,1,0:T(8,128)(2,1)S(1)}, bf16[4,512,128]{2,1,0:T(8,128)(2,1)S(1)}, u32[]{:S(2)}, u32[]{:S(2)}) collective-permute-start(bf16[4,512,128]{2,1,0:T(8,128)(2,1)S(1)} %select_select_fusion.4.refs_0_), channel_id=1, source_target_pairs={{0,192},{4,60},{8,200},{12,4},{16,208},{20,12},{24,216},{28,20},{3... | collective-permute-start | bytes 1572872 | tf_op jit(solution)/shard_map/while/body/eval_jaxpr/ppermute | solution.py:66
  18.1 11.4 %collective-permute-start.4 = (bf16[512,128]{1,0:T(8,128)(2,1)S(1)}, bf16[512,128]{1,0:T(8,128)(2,1)S(1)}, u32[]{:S(2)}, u32[]{:S(2)}) collective-permute-start(bf16[512,128]{1,0:T(8,128)(2,1)S(1)} %get-tuple-element.271), channel_id=1, source_target_pairs={{0,48},{4,36},{8,56},{12,44},{16,0},{20,52},{24,8},{28,60},{32,16}... | collective-permute-start | bytes 393224 | tf_op jit(solution)/shard_map/while/body/eval_jaxpr/ppermute | solution.py:66
  29.5 6.5 %collective-permute-start.7 = (bf16[512,128]{1,0:T(8,128)(2,1)S(1)}, bf16[512,128]{1,0:T(8,128)(2,1)S(1)}, u32[]{:S(2)}, u32[]{:S(2)}) collective-permute-start(bf16[512,128]{1,0:T(8,128)(2,1)S(1)} %broadcast_select_fusion.6), channel_id=1, source_target_pairs={{0,8},{4,68},{8,16},{12,76},{16,24},{20,84},{24,32},{28,92},{32,40... | collective-permute-start | bytes 393224 | tf_op jit(solution)/shard_map/while/body/eval_jaxpr/ppermute | solution.py:66
  29.6 6.4 %collective-permute-start.5 = (bf16[512,128]{1,0:T(8,128)(2,1)S(1)}, bf16[512,128]{1,0:T(8,128)(2,1)S(1)}, u32[]{:S(2)}, u32[]{:S(2)}) collective-permute-start(bf16[512,128]{1,0:T(8,128)(2,1)S(1)} %broadcast_select_fusion.6), channel_id=1, source_target_pairs={{0,16},{4,132},{8,24},{12,140},{16,32},{20,148},{24,40},{28,156},{... | collective-permute-start | bytes 393224 | tf_op jit(solution)/shard_map/while/body/eval_jaxpr/ppermute | solution.py:66
  31.3 5.6 %collective-permute-start.6 = (bf16[512,128]{1,0:T(8,128)(2,1)S(1)}, bf16[512,128]{1,0:T(8,128)(2,1)S(1)}, u32[]{:S(2)}, u32[]{:S(2)}) collective-permute-start(bf16[512,128]{1,0:T(8,128)(2,1)S(1)} %collective-permute-done.4), channel_id=1, source_target_pairs={{0,56},{4,196},{8,0},{12,204},{16,8},{20,212},{24,16},{28,220},{32... | collective-permute-start | bytes 393224 | tf_op jit(solution)/shard_map/while/body/eval_jaxpr/ppermute | solution.py:66
  32.3 11.8 %collective-permute-start.9 = (bf16[4,512,128]{2,1,0:T(8,128)(2,1)S(1)}, bf16[4,512,128]{2,1,0:T(8,128)(2,1)S(1)}, u32[]{:S(2)}, u32[]{:S(2)}) collective-permute-start(bf16[4,512,128]{2,1,0:T(8,128)(2,1)S(1)} %collective-permute-done.8.refs_2_), channel_id=1, source_target_pairs={{0,64},{4,12},{8,72},{12,20},{16,80},{20,28},{24,88},{28,36},{32,9... | collective-permute-start | bytes 1572872 | tf_op jit(solution)/shard_map/while/body/eval_jaxpr/ppermute | solution.py:66
  37.1 11.6 %collective-permute-start.10 = (bf16[4,512,128]{2,1,0:T(8,128)(2,1)S(1)}, bf16[4,512,128]{2,1,0:T(8,128)(2,1)S(1)}, u32[]{:S(2)}, u32[]{:S(2)}) collective-permute-start(bf16[4,512,128]{2,1,0:T(8,128)(2,1)S(1)} %get-tuple-element.252), channel_id=1, source_target_pairs={{0,192},{4,60},{8,200},{12,4},{16,208},{20,12},{24,216},{28,20},{3... | collective-permute-start | bytes 1572872 | tf_op jit(solution)/shard_map/while/body/eval_jaxpr/ppermute | solution.py:66
  42.5 9.5 %collective-permute-start.13 = (bf16[4,512,128]{2,1,0:T(8,128)(2,1)S(1)}, bf16[4,512,128]{2,1,0:T(8,128)(2,1)S(1)}, u32[]{:S(2)}, u32[]{:S(2)}) collective-permute-start(bf16[4,512,128]{2,1,0:T(8,128)(2,1)S(1)} %select_select_fusion.4.refs_0_), channel_id=1, source_target_pairs={{0,4},{4,0},{1,5},{5,1},{2,6},{6,2},{3,7},{7,3},{8,12},{12,8},{9,1... | collective-permute-start | bytes 1572872 | tf_op jit(solution)/shard_map/while/body/eval_jaxpr/ppermute | solution.py:39
  42.5 10.1 %collective-permute-start.14 = (bf16[4,512,128]{2,1,0:T(8,128)(2,1)S(1)}, bf16[4,512,128]{2,1,0:T(8,128)(2,1)S(1)}, u32[]{:S(2)}, u32[]{:S(2)}) collective-permute-start(bf16[4,512,128]{2,1,0:T(8,128)(2,1)S(1)} %get-tuple-element.251.refs_1_), channel_id=1, source_target_pairs={{0,4},{4,0},{1,5},{5,1},{2,6},{6,2},{3,7},{7,3},{8,12},{12,8},{9,1... | collective-permute-start | bytes 1572872 | tf_op jit(solution)/shard_map/while/body/eval_jaxpr/ppermute | solution.py:39
  43.1 9.0 %collective-permute-start.15 = (bf16[4,512,128]{2,1,0:T(8,128)(2,1)S(1)}, bf16[4,512,128]{2,1,0:T(8,128)(2,1)S(1)}, u32[]{:S(2)}, u32[]{:S(2)}) collective-permute-start(bf16[4,512,128]{2,1,0:T(8,128)(2,1)S(1)} %collective-permute-done.8.refs_2_), channel_id=1, source_target_pairs={{0,4},{4,0},{1,5},{5,1},{2,6},{6,2},{3,7},{7,3},{8,12},{12,8},{9,1... | collective-permute-start | bytes 1572872 | tf_op jit(solution)/shard_map/while/body/eval_jaxpr/ppermute | solution.py:39
  44.2 9.6 %collective-permute-start.11 = (bf16[4,512,128]{2,1,0:T(8,128)(2,1)S(1)}, bf16[4,512,128]{2,1,0:T(8,128)(2,1)S(1)}, u32[]{:S(2)}, u32[]{:S(2)}) collective-permute-start(bf16[4,512,128]{2,1,0:T(8,128)(2,1)S(1)} %broadcast_select_fusion.8), channel_id=1, source_target_pairs={{0,64},{4,12},{8,72},{12,20},{16,80},{20,28},{24,88},{28,36},{32,9... | collective-permute-start | bytes 1572872 | tf_op jit(solution)/shard_map/while/body/eval_jaxpr/ppermute | solution.py:66
  48.7 9.5 %collective-permute-start.12 = (bf16[4,512,128]{2,1,0:T(8,128)(2,1)S(1)}, bf16[4,512,128]{2,1,0:T(8,128)(2,1)S(1)}, u32[]{:S(2)}, u32[]{:S(2)}) collective-permute-start(bf16[4,512,128]{2,1,0:T(8,128)(2,1)S(1)} %collective-permute-done.10.refs_5_), channel_id=1, source_target_pairs={{0,192},{4,60},{8,200},{12,4},{16,208},{20,12},{24,216},{28,20},{3... | collective-permute-start | bytes 1572872 | tf_op jit(solution)/shard_map/while/body/eval_jaxpr/ppermute | solution.py:66
  52.1 6.4 %collective-permute-start.16 = (bf16[4,512,128]{2,1,0:T(8,128)(2,1)S(1)}, bf16[4,512,128]{2,1,0:T(8,128)(2,1)S(1)}, u32[]{:S(2)}, u32[]{:S(2)}) collective-permute-start(bf16[4,512,128]{2,1,0:T(8,128)(2,1)S(1)} %collective-permute-done.3.refs_3_), channel_id=1, source_target_pairs={{0,4},{4,0},{1,5},{5,1},{2,6},{6,2},{3,7},{7,3},{8,12},{12,8},{9,1... | collective-permute-start | bytes 1572872 | tf_op jit(solution)/shard_map/while/body/eval_jaxpr/ppermute | solution.py:39
  52.1 6.4 %collective-permute-start.17 = (bf16[4,512,128]{2,1,0:T(8,128)(2,1)S(1)}, bf16[4,512,128]{2,1,0:T(8,128)(2,1)S(1)}, u32[]{:S(2)}, u32[]{:S(2)}) collective-permute-start(bf16[4,512,128]{2,1,0:T(8,128)(2,1)S(1)} %collective-permute-done.9.refs_4_), channel_id=1, source_target_pairs={{0,4},{4,0},{1,5},{5,1},{2,6},{6,2},{3,7},{7,3},{8,12},{12,8},{9,1... | collective-permute-start | bytes 1572872 | tf_op jit(solution)/shard_map/while/body/eval_jaxpr/ppermute | solution.py:39
  52.6 5.9 %collective-permute-start.18 = (bf16[4,512,128]{2,1,0:T(8,128)(2,1)S(1)}, bf16[4,512,128]{2,1,0:T(8,128)(2,1)S(1)}, u32[]{:S(2)}, u32[]{:S(2)}) collective-permute-start(bf16[4,512,128]{2,1,0:T(8,128)(2,1)S(1)} %collective-permute-done.10.refs_5_), channel_id=1, source_target_pairs={{0,4},{4,0},{1,5},{5,1},{2,6},{6,2},{3,7},{7,3},{8,12},{12,8},{9,1... | collective-permute-start | bytes 1572872 | tf_op jit(solution)/shard_map/while/body/eval_jaxpr/ppermute | solution.py:39
  66.7 5.4 %collective-permute-start.21 = (bf16[512,128]{1,0:T(8,128)(2,1)S(1)}, bf16[512,128]{1,0:T(8,128)(2,1)S(1)}, u32[]{:S(2)}, u32[]{:S(2)}) collective-permute-start(bf16[512,128]{1,0:T(8,128)(2,1)S(1)} %get-tuple-element.253), channel_id=1, source_target_pairs={{0,2},{1,3},{2,0},{3,1},{4,6},{5,7},{6,4},{7,5},{8,10},{9,11},{10,... | collective-permute-start | bytes 393224 | tf_op jit(solution)/shard_map/while/body/eval_jaxpr/ppermute | solution.py:39
  66.8 5.5 %collective-permute-start.22 = (bf16[512,128]{1,0:T(8,128)(2,1)S(1)}, bf16[512,128]{1,0:T(8,128)(2,1)S(1)}, u32[]{:S(2)}, u32[]{:S(2)}) collective-permute-start(bf16[512,128]{1,0:T(8,128)(2,1)S(1)} %get-tuple-element.254), channel_id=1, source_target_pairs={{0,3},{1,0},{2,1},{3,2},{4,7},{5,4},{6,5},{7,6},{8,11},{9,8},{10,9... | collective-permute-start | bytes 393224 | tf_op jit(solution)/shard_map/while/body/eval_jaxpr/ppermute | solution.py:39
  75.5 9.9 %collective-permute-start.1 = (bf16[512,128]{1,0:T(8,128)(2,1)S(1)}, bf16[512,128]{1,0:T(8,128)(2,1)S(1)}, u32[]{:S(2)}, u32[]{:S(2)}) collective-permute-start(bf16[512,128]{1,0:T(8,128)(2,1)S(1)} %get-tuple-element.271), channel_id=1, source_target_pairs={{0,56},{4,196},{8,0},{12,204},{16,8},{20,212},{24,16},{28,220},{32... | collective-permute-start | bytes 393224 | tf_op jit(solution)/shard_map/while/body/eval_jaxpr/ppermute | solution.py:66
  82.1 5.4 %collective-permute-start = (bf16[512,128]{1,0:T(8,128)(2,1)S(1)}, bf16[512,128]{1,0:T(8,128)(2,1)S(1)}, u32[]{:S(2)}, u32[]{:S(2)}) collective-permute-start(bf16[512,128]{1,0:T(8,128)(2,1)S(1)} %get-tuple-element.271), channel_id=1, source_target_pairs={{0,16},{4,132},{8,24},{12,140},{16,32},{20,148},{24,40},{28,156},{... | collective-permute-start | bytes 393224 | tf_op jit(solution)/shard_map/while/body/eval_jaxpr/ppermute | solution.py:66
  82.1 6.7 %collective-permute-start.2 = (bf16[512,128]{1,0:T(8,128)(2,1)S(1)}, bf16[512,128]{1,0:T(8,128)(2,1)S(1)}, u32[]{:S(2)}, u32[]{:S(2)}) collective-permute-start(bf16[512,128]{1,0:T(8,128)(2,1)S(1)} %get-tuple-element.271), channel_id=1, source_target_pairs={{0,8},{4,68},{8,16},{12,76},{16,24},{20,84},{24,32},{28,92},{32,40... | collective-permute-start | bytes 393224 | tf_op jit(solution)/shard_map/while/body/eval_jaxpr/ppermute | solution.py:66
  89.0 14.9 %collective-permute-start.8 = (bf16[4,512,128]{2,1,0:T(8,128)(2,1)S(1)}, bf16[4,512,128]{2,1,0:T(8,128)(2,1)S(1)}, u32[]{:S(2)}, u32[]{:S(2)}) collective-permute-start(bf16[4,512,128]{2,1,0:T(8,128)(2,1)S(1)} %select_select_fusion.4.refs_0_), channel_id=1, source_target_pairs={{0,64},{4,12},{8,72},{12,20},{16,80},{20,28},{24,88},{28,36},{32,9... | collective-permute-start | bytes 1572872 | tf_op jit(solution)/shard_map/while/body/eval_jaxpr/ppermute | solution.py:66
  92.8 15.5 %collective-permute-start.3 = (bf16[4,512,128]{2,1,0:T(8,128)(2,1)S(1)}, bf16[4,512,128]{2,1,0:T(8,128)(2,1)S(1)}, u32[]{:S(2)}, u32[]{:S(2)}) collective-permute-start(bf16[4,512,128]{2,1,0:T(8,128)(2,1)S(1)} %select_select_fusion.4.refs_0_), channel_id=1, source_target_pairs={{0,192},{4,60},{8,200},{12,4},{16,208},{20,12},{24,216},{28,20},{3... | collective-permute-start | bytes 1572872 | tf_op jit(solution)/shard_map/while/body/eval_jaxpr/ppermute | solution.py:66
  93.2 7.8 %collective-permute-start.4 = (bf16[512,128]{1,0:T(8,128)(2,1)S(1)}, bf16[512,128]{1,0:T(8,128)(2,1)S(1)}, u32[]{:S(2)}, u32[]{:S(2)}) collective-permute-start(bf16[512,128]{1,0:T(8,128)(2,1)S(1)} %get-tuple-element.271), channel_id=1, source_target_pairs={{0,48},{4,36},{8,56},{12,44},{16,0},{20,52},{24,8},{28,60},{32,16}... | collective-permute-start | bytes 393224 | tf_op jit(solution)/shard_map/while/body/eval_jaxpr/ppermute | solution.py:66
  101.1 6.4 %collective-permute-start.7 = (bf16[512,128]{1,0:T(8,128)(2,1)S(1)}, bf16[512,128]{1,0:T(8,128)(2,1)S(1)}, u32[]{:S(2)}, u32[]{:S(2)}) collective-permute-start(bf16[512,128]{1,0:T(8,128)(2,1)S(1)} %broadcast_select_fusion.6), channel_id=1, source_target_pairs={{0,8},{4,68},{8,16},{12,76},{16,24},{20,84},{24,32},{28,92},{32,40... | collective-permute-start | bytes 393224 | tf_op jit(solution)/shard_map/while/body/eval_jaxpr/ppermute | solution.py:66
  101.2 7.2 %collective-permute-start.5 = (bf16[512,128]{1,0:T(8,128)(2,1)S(1)}, bf16[512,128]{1,0:T(8,128)(2,1)S(1)}, u32[]{:S(2)}, u32[]{:S(2)}) collective-permute-start(bf16[512,128]{1,0:T(8,128)(2,1)S(1)} %broadcast_select_fusion.6), channel_id=1, source_target_pairs={{0,16},{4,132},{8,24},{12,140},{16,32},{20,148},{24,40},{28,156},{... | collective-permute-start | bytes 393224 | tf_op jit(solution)/shard_map/while/body/eval_jaxpr/ppermute | solution.py:66
  103.9 18.6 %collective-permute-start.9 = (bf16[4,512,128]{2,1,0:T(8,128)(2,1)S(1)}, bf16[4,512,128]{2,1,0:T(8,128)(2,1)S(1)}, u32[]{:S(2)}, u32[]{:S(2)}) collective-permute-start(bf16[4,512,128]{2,1,0:T(8,128)(2,1)S(1)} %collective-permute-done.8.refs_2_), channel_id=1, source_target_pairs={{0,64},{4,12},{8,72},{12,20},{16,80},{20,28},{24,88},{28,36},{32,9... | collective-permute-start | bytes 1572872 | tf_op jit(solution)/shard_map/while/body/eval_jaxpr/ppermute | solution.py:66
  108.5 14.1 %collective-permute-start.10 = (bf16[4,512,128]{2,1,0:T(8,128)(2,1)S(1)}, bf16[4,512,128]{2,1,0:T(8,128)(2,1)S(1)}, u32[]{:S(2)}, u32[]{:S(2)}) collective-permute-start(bf16[4,512,128]{2,1,0:T(8,128)(2,1)S(1)} %get-tuple-element.252), channel_id=1, source_target_pairs={{0,192},{4,60},{8,200},{12,4},{16,208},{20,12},{24,216},{28,20},{3... | collective-permute-start | bytes 1572872 | tf_op jit(solution)/shard_map/while/body/eval_jaxpr/ppermute | solution.py:66
  115.3 10.0 %collective-permute-start.13 = (bf16[4,512,128]{2,1,0:T(8,128)(2,1)S(1)}, bf16[4,512,128]{2,1,0:T(8,128)(2,1)S(1)}, u32[]{:S(2)}, u32[]{:S(2)}) collective-permute-start(bf16[4,512,128]{2,1,0:T(8,128)(2,1)S(1)} %select_select_fusion.4.refs_0_), channel_id=1, source_target_pairs={{0,4},{4,0},{1,5},{5,1},{2,6},{6,2},{3,7},{7,3},{8,12},{12,8},{9,1... | collective-permute-start | bytes 1572872 | tf_op jit(solution)/shard_map/while/body/eval_jaxpr/ppermute | solution.py:39
  122.0 10.5 %collective-permute-start.14 = (bf16[4,512,128]{2,1,0:T(8,128)(2,1)S(1)}, bf16[4,512,128]{2,1,0:T(8,128)(2,1)S(1)}, u32[]{:S(2)}, u32[]{:S(2)}) collective-permute-start(bf16[4,512,128]{2,1,0:T(8,128)(2,1)S(1)} %get-tuple-element.251.refs_1_), channel_id=1, source_target_pairs={{0,4},{4,0},{1,5},{5,1},{2,6},{6,2},{3,7},{7,3},{8,12},{12,8},{9,1... | collective-permute-start | bytes 1572872 | tf_op jit(solution)/shard_map/while/body/eval_jaxpr/ppermute | solution.py:39
  122.0 10.4 %collective-permute-start.15 = (bf16[4,512,128]{2,1,0:T(8,128)(2,1)S(1)}, bf16[4,512,128]{2,1,0:T(8,128)(2,1)S(1)}, u32[]{:S(2)}, u32[]{:S(2)}) collective-permute-start(bf16[4,512,128]{2,1,0:T(8,128)(2,1)S(1)} %collective-permute-done.8.refs_2_), channel_id=1, source_target_pairs={{0,4},{4,0},{1,5},{5,1},{2,6},{6,2},{3,7},{7,3},{8,12},{12,8},{9,1... | collective-permute-start | bytes 1572872 | tf_op jit(solution)/shard_map/while/body/eval_jaxpr/ppermute | solution.py:39
  122.5 10.3 %collective-permute-start.11 = (bf16[4,512,128]{2,1,0:T(8,128)(2,1)S(1)}, bf16[4,512,128]{2,1,0:T(8,128)(2,1)S(1)}, u32[]{:S(2)}, u32[]{:S(2)}) collective-permute-start(bf16[4,512,128]{2,1,0:T(8,128)(2,1)S(1)} %broadcast_select_fusion.8), channel_id=1, source_target_pairs={{0,64},{4,12},{8,72},{12,20},{16,80},{20,28},{24,88},{28,36},{32,9... | collective-permute-start | bytes 1572872 | tf_op jit(solution)/shard_map/while/body/eval_jaxpr/ppermute | solution.py:66
  122.6 10.4 %collective-permute-start.12 = (bf16[4,512,128]{2,1,0:T(8,128)(2,1)S(1)}, bf16[4,512,128]{2,1,0:T(8,128)(2,1)S(1)}, u32[]{:S(2)}, u32[]{:S(2)}) collective-permute-start(bf16[4,512,128]{2,1,0:T(8,128)(2,1)S(1)} %collective-permute-done.10.refs_5_), channel_id=1, source_target_pairs={{0,192},{4,60},{8,200},{12,4},{16,208},{20,12},{24,216},{28,20},{3... | collective-permute-start | bytes 1572872 | tf_op jit(solution)/shard_map/while/body/eval_jaxpr/ppermute | solution.py:66
  125.3 13.8 %collective-permute-start.16 = (bf16[4,512,128]{2,1,0:T(8,128)(2,1)S(1)}, bf16[4,512,128]{2,1,0:T(8,128)(2,1)S(1)}, u32[]{:S(2)}, u32[]{:S(2)}) collective-permute-start(bf16[4,512,128]{2,1,0:T(8,128)(2,1)S(1)} %collective-permute-done.3.refs_3_), channel_id=1, source_target_pairs={{0,4},{4,0},{1,5},{5,1},{2,6},{6,2},{3,7},{7,3},{8,12},{12,8},{9,1... | collective-permute-start | bytes 1572872 | tf_op jit(solution)/shard_map/while/body/eval_jaxpr/ppermute | solution.py:39
  132.4 6.7 %collective-permute-start.17 = (bf16[4,512,128]{2,1,0:T(8,128)(2,1)S(1)}, bf16[4,512,128]{2,1,0:T(8,128)(2,1)S(1)}, u32[]{:S(2)}, u32[]{:S(2)}) collective-permute-start(bf16[4,512,128]{2,1,0:T(8,128)(2,1)S(1)} %collective-permute-done.9.refs_4_), channel_id=1, source_target_pairs={{0,4},{4,0},{1,5},{5,1},{2,6},{6,2},{3,7},{7,3},{8,12},{12,8},{9,1... | collective-permute-start | bytes 1572872 | tf_op jit(solution)/shard_map/while/body/eval_jaxpr/ppermute | solution.py:39
  132.4 6.6 %collective-permute-start.18 = (bf16[4,512,128]{2,1,0:T(8,128)(2,1)S(1)}, bf16[4,512,128]{2,1,0:T(8,128)(2,1)S(1)}, u32[]{:S(2)}, u32[]{:S(2)}) collective-permute-start(bf16[4,512,128]{2,1,0:T(8,128)(2,1)S(1)} %collective-permute-done.10.refs_5_), channel_id=1, source_target_pairs={{0,4},{4,0},{1,5},{5,1},{2,6},{6,2},{3,7},{7,3},{8,12},{12,8},{9,1... | collective-permute-start | bytes 1572872 | tf_op jit(solution)/shard_map/while/body/eval_jaxpr/ppermute | solution.py:39
  132.9 6.2 %collective-permute-start.19 = (bf16[4,512,128]{2,1,0:T(8,128)(2,1)S(1)}, bf16[4,512,128]{2,1,0:T(8,128)(2,1)S(1)}, u32[]{:S(2)}, u32[]{:S(2)}) collective-permute-start(bf16[4,512,128]{2,1,0:T(8,128)(2,1)S(1)} %collective-permute-done.11.refs_6_), channel_id=1, source_target_pairs={{0,4},{4,0},{1,5},{5,1},{2,6},{6,2},{3,7},{7,3},{8,12},{12,8},{9,1... | collective-permute-start | bytes 1572872 | tf_op jit(solution)/shard_map/while/body/eval_jaxpr/ppermute | solution.py:39
  133.0 7.6 %collective-permute-start.20 = (bf16[4,512,128]{2,1,0:T(8,128)(2,1)S(1)}, bf16[4,512,128]{2,1,0:T(8,128)(2,1)S(1)}, u32[]{:S(2)}, u32[]{:S(2)}) collective-permute-start(bf16[4,512,128]{2,1,0:T(8,128)(2,1)S(1)} %collective-permute-done.12.refs_7_), channel_id=1, source_target_pairs={{0,4},{4,0},{1,5},{5,1},{2,6},{6,2},{3,7},{7,3},{8,12},{12,8},{9,1... | collective-permute-start | bytes 1572872 | tf_op jit(solution)/shard_map/while/body/eval_jaxpr/ppermute | solution.py:39
  147.1 6.8 %collective-permute-start.21 = (bf16[512,128]{1,0:T(8,128)(2,1)S(1)}, bf16[512,128]{1,0:T(8,128)(2,1)S(1)}, u32[]{:S(2)}, u32[]{:S(2)}) collective-permute-start(bf16[512,128]{1,0:T(8,128)(2,1)S(1)} %get-tuple-element.253), channel_id=1, source_target_pairs={{0,2},{1,3},{2,0},{3,1},{4,6},{5,7},{6,4},{7,5},{8,10},{9,11},{10,... | collective-permute-start | bytes 393224 | tf_op jit(solution)/shard_map/while/body/eval_jaxpr/ppermute | solution.py:39
  147.2 6.7 %collective-permute-start.22 = (bf16[512,128]{1,0:T(8,128)(2,1)S(1)}, bf16[512,128]{1,0:T(8,128)(2,1)S(1)}, u32[]{:S(2)}, u32[]{:S(2)}) collective-permute-start(bf16[512,128]{1,0:T(8,128)(2,1)S(1)} %get-tuple-element.254), channel_id=1, source_target_pairs={{0,3},{1,0},{2,1},{3,2},{4,7},{5,4},{6,5},{7,6},{8,11},{9,8},{10,9... | collective-permute-start | bytes 393224 | tf_op jit(solution)/shard_map/while/body/eval_jaxpr/ppermute | solution.py:39
  147.3 8.4 %collective-permute-start.23 = (bf16[512,128]{1,0:T(8,128)(2,1)S(1)}, bf16[512,128]{1,0:T(8,128)(2,1)S(1)}, u32[]{:S(2)}, u32[]{:S(2)}) collective-permute-start(bf16[512,128]{1,0:T(8,128)(2,1)S(1)} %get-tuple-element.256), channel_id=1, source_target_pairs={{0,1},{1,2},{2,3},{3,0},{4,5},{5,6},{6,7},{7,4},{8,9},{9,10},{10,1... | collective-permute-start | bytes 393224 | tf_op jit(solution)/shard_map/while/body/eval_jaxpr/ppermute | solution.py:39
  159.6 6.5 %collective-permute-start.25 = (f32[128,128]{1,0:T(8,128)S(1)}, f32[128,128]{1,0:T(8,128)S(1)}, u32[]{:S(2)}, u32[]{:S(2)}) collective-permute-start(f32[128,128]{1,0:T(8,128)S(1)} %add.57), channel_id=1, source_target_pairs={{0,1},{1,2},{2,3},{3,0},{4,5},{5,6},{6,7},{7,4},{8,9},{9,10},{10,1... | collective-permute-start | bytes 196616 | tf_op jit(solution)/shard_map/ppermute | solution.py:39
  174.6 7.2 %collective-permute-start.33 = (f32[128,128]{1,0:T(8,128)S(1)}, f32[128,128]{1,0:T(8,128)S(1)}, u32[]{:S(2)}, u32[]{:S(2)}) collective-permute-start(f32[128,128]{1,0:T(8,128)S(1)} %add_add_fusion.1), channel_id=1, source_target_pairs={{0,32},{8,40},{16,48},{24,56},{32,0},{40,8},{48,16},{56,24},{1,33}... | collective-permute-start | bytes 196616 | tf_op jit(solution)/shard_map/ppermute | solution.py:39
  174.7 7.1 %collective-permute-start.32 = (f32[128,128]{1,0:T(8,128)S(1)}, f32[128,128]{1,0:T(8,128)S(1)}, u32[]{:S(2)}, u32[]{:S(2)}) collective-permute-start(f32[128,128]{1,0:T(8,128)S(1)} %add_add_fusion.1), channel_id=1, source_target_pairs={{0,48},{8,56},{16,0},{24,8},{32,16},{40,24},{48,32},{56,40},{1,49}... | collective-permute-start | bytes 196616 | tf_op jit(solution)/shard_map/ppermute | solution.py:39
  176.2 6.1 %collective-permute-start.31 = (f32[128,128]{1,0:T(8,128)S(1)}, f32[128,128]{1,0:T(8,128)S(1)}, u32[]{:S(2)}, u32[]{:S(2)}) collective-permute-start(f32[128,128]{1,0:T(8,128)S(1)} %add_add_fusion.1), channel_id=1, source_target_pairs={{0,16},{8,24},{16,32},{24,40},{32,48},{40,56},{48,0},{56,8},{1,17}... | collective-permute-start | bytes 196616 | tf_op jit(solution)/shard_map/ppermute | solution.py:39
  (13 other events, 229.1 us)
where the time goes:
time: 201 us; the launch traced here: 198 us
  starting transfers between devices  100 us (50%)
  waiting for transfers between devices  67.2 us (33%)
  Pallas kernels  23.2 us (12%)
  other arithmetic  3.67 us (2%)
  local copies, waits for them, and re-layouts  2.37 us (1%)
    ppermute x26, starting transfers between devices, send(): return lax.ppermute(value, PLANE, pairs)  58 us
    ppermute x31, starting transfers between devices, axis_shift(): return lax.ppermute(value, axis, [(i, (i + hop) % n) for i in range(n)])  38.9 us
    ppermute x26, waiting for transfers between devices, send(): return lax.ppermute(value, PLANE, pairs)  37.5 us
    ppermute x31, waiting for transfers between devices, axis_shift(): return lax.ppermute(value, axis, [(i, (i + hop) % n) for i in range(n)])  27.1 us
    pallas_call x2, Pallas kernels, apply_operator(): pl.pallas_call(tile_kernel, out_shape=[shape(jnp.float32)] + [shape(jnp.b...  13.1 us
    pallas_call x1, Pallas kernels, finish(): pl.pallas_call(functools.partial(finish_kernel, scale), out_shape=jax.Sha...  10.1 us
  transfers between devices with their start and end apart: 59, of which 31 were waited for; matrix products, arithmetic and copies ran while one was open for 1% of the time, Pallas kernels for 0%

commit v1 on v0

--- a/solution.py
+++ b/solution.py
@@ -110,12 +110,17 @@
     return table.reshape(-1)
 
 
-def tile_kernel(rows, cols, counts, table, tiles, *refs):
-    *pieces, own_ref, one_ref, two_ref, three_ref, acc, picked, held, sems = refs
+def tile_kernel(ids, final, rows, cols, counts, table, tiles, *refs):
+    pieces, refs = refs[: len(ids)], refs[len(ids) :]
+    if final:
+        acc_in, own_ref, one_ref, two_ref, three_ref, acc, *refs = refs
+    else:
+        acc, *refs = refs
+    picked, held, todo, sems = refs
     span = pieces[0].shape[0]
-    slots = tiles.shape[0]
     live = counts[0]
     y, z, core, x = (lax.axis_index(a) for a in ("y", "z", "c", "x"))
+    here = sum(1 << p for p in ids)
 
     def place_of(s):
         col = cols[s]
@@ -124,67 +129,108 @@
         place = table[(from_c * NY + dy) * NZ + dz]
         return place + jnp.where(from_c == core, 0, NY * NZ)
 
-    def load(pair):
-        return pltpu.make_async_copy(tiles.at[pl.ds(2 * pair, 2)], held.at[pl.ds(2 * pair, 2)], sems.at[pair])
-
-    for pair in range(slots // 2):
-
-        @pl.when(2 * pair < live)
+    def load(s, k):
+        return pltpu.make_async_copy(tiles.at[s], held.at[k], sems.at[k])
+
+    def enlist(s, n):
+        found = (here >> (place_of(s) // span)) & 1
+
+        @pl.when(found == 1)
         def _():
-            load(pair).start()
-
-    acc[...] = jnp.zeros_like(acc)
+            todo[n] = s
+            load(s, n).start()
+
+        return n + found
+
+    total = lax.fori_loop(0, live, enlist, 0)
+    if final:
+        acc[:NX] = acc_in[:NX]
+    else:
+        acc[...] = jnp.zeros_like(acc)
+
+    def pick(i, piece, offset, first, last):
+        if last - first == 1:
+            picked[i] = pieces[first][offset]
+            return
+        middle = (first + last) // 2
+
+        @pl.when(piece < ids[middle])
+        def _():
+            pick(i, piece, offset, first, middle)
+
+        @pl.when(piece >= ids[middle])
+        def _():
+            pick(i, piece, offset, middle, last)
 
     def work(pair, carry):
-        both = (2 * pair, 2 * pair + 1)
-        for i, s in enumerate(both):
+        targets, products = [], []
+        for i in range(2):
+            k = 2 * pair + i
+            at = jnp.minimum(k, total - 1)
+            s = todo[at]
             place = place_of(s)
-            for p, piece in enumerate(pieces):
-
-                @pl.when(place // span == p)
-                def _():
-                    picked[i] = piece[place % span]
-
-        load(pair).wait()
-        products = [
-            jnp.dot(held[s], picked[i], preferred_element_type=jnp.float32) for i, s in enumerate(both)
-        ]
-        for i, s in enumerate(both):
-            row = jnp.where(s < live, (rows[s] - x) & (NX - 1), NX)
-            acc[row] += products[i]
+            pick(i, place // span, place % span, 0, len(ids))
+
+            @pl.when(k < total)
+            def _():
+                load(s, at).wait()
+
+            targets.append((at, jnp.where(k < total, (rows[s] - x) & (NX - 1), NX)))
+        for i in range(2):
+            products.append(jnp.dot(held[targets[i][0]], picked[i], preferred_element_type=jnp.float32))
+        for i in range(2):
+            acc[targets[i][1]] += products[i]
         return carry
 
-    lax.fori_loop(0, (live + 1) // 2, work, 0)
-    own_ref[...] = acc[0]
-    one_ref[...] = acc[1].astype(jnp.bfloat16)
-    two_ref[...] = acc[2].astype(jnp.bfloat16)
-    three_ref[...] = acc[3].astype(jnp.bfloat16)
-
-
-def apply_operator(block, tiles, lists, core):
+    lax.fori_loop(0, (total + 1) // 2, work, 0)
+    if final:
+        own_ref[...] = acc[0]
+        one_ref[...] = acc[1].astype(jnp.bfloat16)
+        two_ref[...] = acc[2].astype(jnp.bfloat16)
+        three_ref[...] = acc[3].astype(jnp.bfloat16)
+
+
+LATE = (6, 7, 14, 15)
+
+
+def tile_products(pieces, tiles, lists):
     slots, tile, _ = tiles.shape
-    assert slots % 2 == 0
-    width = block.shape[1]
-    pieces = gather_blocks(block, core)
+    width = pieces[0].shape[-1]
+    early = tuple(p for p in range(len(pieces)) if p not in LATE)
     vmem = pl.BlockSpec(memory_space=pltpu.VMEM)
     shape = lambda t: jax.ShapeDtypeStruct((tile, width), t)
-    own, one, two, three = pl.pallas_call(
-        tile_kernel,
-        out_shape=[shape(jnp.float32)] + [shape(jnp.bfloat16)] * 3,
-        in_specs=[pl.BlockSpec(memory_space=pltpu.SMEM)] * 4 + [pl.BlockSpec(memory_space=pl.ANY)] + [vmem] * len(pieces),
-        out_specs=[vmem] * 4,
-        scratch_shapes=[
-            pltpu.VMEM((NX + 1, tile, width), jnp.float32),
-            pltpu.VMEM((2, tile, width), jnp.bfloat16),
-            pltpu.VMEM((slots, tile, tile), jnp.bfloat16),
-            pltpu.SemaphoreType.DMA((slots // 2,)),
-        ],
-        compiler_params=pltpu.CompilerParams(vmem_limit_bytes=40 << 20),
-        cost_estimate=pl.CostEstimate(
-            flops=2 * slots * tile * tile * width, bytes_accessed=slots * tile * (tile + width) * 2, transcendentals=0
-        ),
-        name="tile_products",
-    )(*lists, tiles, *pieces)
+    sums = jax.ShapeDtypeStruct((NX + 1, tile, width), jnp.float32)
+    scratch = [
+        pltpu.VMEM((2, tile, width), jnp.bfloat16),
+        pltpu.VMEM((slots, tile, tile), jnp.bfloat16),
+        pltpu.SMEM((slots,), jnp.int32),
+        pltpu.SemaphoreType.DMA((slots,)),
+    ]
+
+    def call(ids, final, out_shape, extra):
+        share = len(ids) / len(pieces)
+        return pl.pallas_call(
+            functools.partial(tile_kernel, ids, final),
+            out_shape=out_shape,
+            in_specs=[pl.BlockSpec(memory_space=pltpu.SMEM)] * 4
+            + [pl.BlockSpec(memory_space=pl.ANY)]
+            + [vmem] * (len(ids) + len(extra)),
+            out_specs=[vmem] * len(out_shape),
+            scratch_shapes=([pltpu.VMEM(sums.shape, sums.dtype)] if final else []) + scratch,
+            compiler_params=pltpu.CompilerParams(vmem_limit_bytes=40 << 20),
+            cost_estimate=pl.CostEstimate(
+                flops=int(share * 2 * slots * tile * tile * width),
+                bytes_accessed=int(share * slots * tile * (tile + width) * 2),
+                transcendentals=0,
+            ),
+        )(*lists, tiles, *(pieces[p] for p in ids), *extra)
+
+    (partial,) = call(early, False, [sums], ())
+    return call(LATE, True, [shape(jnp.float32)] + [shape(jnp.bfloat16)] * 3, (partial,))
+
+
+def apply_operator(block, tiles, lists, core):
+    own, one, two, three = tile_products(gather_blocks(block, core), tiles, lists)
     f32 = jnp.float32
     one = axis_shift(one, "x", 1)
     three = axis_shift(three, "x", 3)
@@ -200,42 +246,42 @@
     return gram + axis_swap(gram, "z", 1)
 
 
-STEP = 8
+STEP = 16
 
 
 def finish_kernel(scale, gram_ref, spectral_ref, out_ref, work):
+    step = STEP
     n = gram_ref.shape[0]
-    row_id = lax.broadcasted_iota(jnp.int32, (n, n), 0)
-    col_id = lax.broadcasted_iota(jnp.int32, (n, n), 1)
-    work[:, :n] = gram_ref[...]
-    work[:, n:] = jnp.where(row_id == col_id, 1.0, 0.0)
-    sub = lax.broadcasted_iota(jnp.int32, (STEP, n), 0)
-    for k in range(n // STEP):
-        lo = k * STEP
-        left = work[lo : lo + STEP, :n]
-        right = work[lo : lo + STEP, n:]
-        columns = [jnp.broadcast_to(left[:, lo + j : lo + j + 1], (STEP, n)) for j in range(STEP)]
-        for j in range(STEP):
-            inv = lax.rsqrt(columns[j][j : j + 1, :])
-            inv = inv * (1.5 - 0.5 * columns[j][j : j + 1, :] * inv * inv)
-            row_l, row_r = left[j : j + 1, :] * inv, right[j : j + 1, :] * inv
+    work[...] = gram_ref[...]
+    sub = lax.broadcasted_iota(jnp.int32, (step, n), 0)
+    lane = lax.broadcasted_iota(jnp.int32, (step, n), 1)
+    for k in range(n // step):
+        lo = k * step
+        hi = lo + step
+        slab = work[lo:hi, :]
+        columns = [jnp.broadcast_to(slab[:, lo + j : lo + j + 1], (step, n)) for j in range(step)]
+        slab = jnp.where((lane >= lo) & (lane < hi), jnp.where(lane - lo == sub, 1.0, 0.0), slab)
+        for j in range(step):
+            pivot = columns[j][j : j + 1, :]
+            inv = lax.rsqrt(pivot)
+            inv = inv * (1.5 - 0.5 * pivot * inv * inv)
+            row = slab[j : j + 1, :] * inv
             factor = jnp.where(sub > j, columns[j] * inv, 0.0)
-            here = sub == j
-            left = jnp.where(here, row_l, left - factor * row_l)
-            right = jnp.where(here, row_r, right - factor * row_r)
-            for i in range(j + 1, STEP):
+            slab = jnp.where(sub == j, row, slab - factor * row)
+            for i in range(j + 1, step):
                 columns[i] = columns[i] - factor * (columns[i][j : j + 1, :] * inv)
-        work[lo : lo + STEP, :n] = left
-        work[lo : lo + STEP, n:] = right
-        hi = lo + STEP
+        work[lo:hi, :] = slab
         if hi < n:
-            panel = left[:, hi:]
-            both = jnp.concatenate([left, right], axis=1)
-            work[hi:, :] = work[hi:, :] - lax.dot_general(
-                panel, both, (((0,), (0,)), ((), ())), precision=lax.Precision.HIGHEST,
+            rest = work[hi:, :]
+            spot = lax.broadcasted_iota(jnp.int32, rest.shape, 1)
+            rest = jnp.where((spot >= lo) & (spot < hi), 0.0, rest)
+            work[hi:, :] = rest - lax.dot_general(
+                slab[:, hi:], slab, (((0,), (0,)), ((), ())), precision=lax.Precision.HIGHEST,
                 preferred_element_type=jnp.float32)
+    upper = lax.broadcasted_iota(jnp.int32, (n, n), 1) > lax.broadcasted_iota(jnp.int32, (n, n), 0)
+    inverse = jnp.where(upper, 0.0, work[...]) * scale
     out_ref[...] = lax.dot_general(
-        spectral_ref[...], work[:, n:] * scale, (((1,), (1,)), ((), ())), precision=lax.Precision.HIGHEST,
+        spectral_ref[...], inverse, (((1,), (1,)), ((), ())), precision=lax.Precision.HIGHEST,
         preferred_element_type=jnp.float32)
 
 
@@ -245,7 +291,7 @@
     return pl.pallas_call(functools.partial(finish_kernel, scale),
         out_shape=jax.ShapeDtypeStruct(spectral.shape, jnp.float32),
         in_specs=[vmem, vmem], out_specs=vmem,
-        scratch_shapes=[pltpu.VMEM((n, 2*n), jnp.float32)], name="orthonormalize")(gram, spectral)
+        scratch_shapes=[pltpu.VMEM((n, n), jnp.float32)], name="orthonormalize")(gram, spectral)
 
 
 def local(embedding, tile_blocks, tile_row, tile_col, counts):

time: 201 us -> 200 us (level)
  waiting for transfers between devices: 67.2 us -> 58.1 us
  starting transfers between devices: 100 us -> 107 us
    ppermute x31, waiting for transfers between devices: 27.1 us -> 21.7 us  [axis_shift(): return lax.ppermute(value, axis, [(i, (i + hop) % n) for i in range(n)])]
    pallas_call x2 -> x4, Pallas kernels: 13.1 us -> 17.6 us  [call(): pl.pallas_call(functools.partial(tile_kernel, ids, final), out_shape=out_...]
    ppermute x26, waiting for transfers between devices: 37.5 us -> 33.8 us  [send(): return lax.ppermute(value, PLANE, pairs)]
    ppermute x26, starting transfers between devices: 58 us -> 61.6 us  [send(): return lax.ppermute(value, PLANE, pairs)]
    pallas_call x1, Pallas kernels: 10.1 us -> 6.67 us  [finish(): pl.pallas_call(functools.partial(finish_kernel, scale), out_shape=jax.Sha...]
    ppermute x2, starting transfers between devices: 3.2 us -> 5.65 us  [axis_swap(): return lax.ppermute(value, axis, [(i, i ^ bit) for i in range(n)])]
  transfers between devices with their start and end apart: 59 -> 59, of which waited for: 31 -> 28; matrix products, arithmetic and copies ran while one was open for 1% -> 1% of each run, Pallas kernels for 0% -> 6%
where the time goes in v1:
time: 200 us; the launch traced here: 197 us
  starting transfers between devices  107 us (54%)
  waiting for transfers between devices  58.1 us (29%)
  Pallas kernels  24.3 us (12%)
  other arithmetic  3.66 us (2%)
  local copies, waits for them, and re-layouts  2.42 us (1%)
    ppermute x26, starting transfers between devices, send(): return lax.ppermute(value, PLANE, pairs)  61.6 us
    ppermute x31, starting transfers between devices, axis_shift(): return lax.ppermute(value, axis, [(i, (i + hop) % n) for i in range(n)])  39.8 us
    ppermute x26, waiting for transfers between devices, send(): return lax.ppermute(value, PLANE, pairs)  33.8 us
    ppermute x31, waiting for transfers between devices, axis_shift(): return lax.ppermute(value, axis, [(i, (i + hop) % n) for i in range(n)])  21.7 us
    pallas_call x4, Pallas kernels, call(): pl.pallas_call(functools.partial(tile_kernel, ids, final), out_shape=out_...  17.6 us
    pallas_call x1, Pallas kernels, finish(): pl.pallas_call(functools.partial(finish_kernel, scale), out_shape=jax.Sha...  6.67 us
    ppermute x2, starting transfers between devices, axis_swap(): return lax.ppermute(value, axis, [(i, i ^ bit) for i in range(n)])  5.65 us
  transfers between devices with their start and end apart: 59, of which 28 were waited for; matrix products, arithmetic and copies ran while one was open for 1% of the time, Pallas kernels for 6%

profile of v1, /device:TPU:1, one launch (start us, length us, event | category | flops | bytes accessed | tf_op | source)
XLA Modules:
  0.0 196.7 jit_solution(17137622998971040426)
XLA Ops:
  1.9 149.6 %while.17 = (s32[]{:T(128)}, bf16[512,128]{1,0:T(8,128)(2,1)S(1)}, f32[512,128]{1,0:T(8,128)}, f32[512,128]{1,0:T(8,128)S(1)}, pred[]{:T(512)}, /*index=5*/s32[2...) while((s32[]{:T(128)}, bf16[512,128]{1,0:T(8,128)(2,1)S(1)}, ...), condition=%wide.region_1.2_spmd.clone, body=%wide.region_0.1_spmd.sunk.clone.sunk | while | flops 1479016448 | bytes 90311592 | solution.py:309
  1.9 3.8 %collective-permute-start = (bf16[512,128]{1,0:T(8,128)(2,1)S(1)}, bf16[512,128]{1,0:T(8,128)(2,1)S(1)}, u32[]{:S(2)}, u32[]{:S(2)}) collective-permute-start(bf16[512,128]{1,0:T(8,128)(2,1)S(1)} %get-tuple-element.271), channel_id=1, source_target_pairs={{0,16},{4,132},{8,24},{12,140},{16,32},{20,148},{24,40},{28,156},{... | collective-permute-start | bytes 393224 | tf_op jit(solution)/shard_map/while/body/eval_jaxpr/ppermute | solution.py:66
  8.1 2.1 %collective-permute-done.1 = bf16[512,128]{1,0:T(8,128)(2,1)S(1)} collective-permute-done((bf16[512,128]{1,0:T(8,128)(2,1)S(1)}, bf16[512,128]{1,0:T(8,128)(2,1)S(1)}, u32[]{:S(2)}, u32[]{:S(2)}) %collective-permute-start.1) | collective-permute-done | bytes 131104 | tf_op jit(solution)/shard_map/while/body/eval_jaxpr/ppermute | solution.py:66
  10.2 1.7 collective-permute-done.2
  12.0 1.7 collective-permute-start.8
  13.7 3.7 %collective-permute-start.3 = (bf16[4,512,128]{2,1,0:T(8,128)(2,1)S(1)}, bf16[4,512,128]{2,1,0:T(8,128)(2,1)S(1)}, u32[]{:S(2)}, u32[]{:S(2)}) collective-permute-start(bf16[4,512,128]{2,1,0:T(8,128)(2,1)S(1)} %select_select_fusion.4.refs_0_), channel_id=1, source_target_pairs={{0,192},{4,60},{8,200},{12,4},{16,208},{20,12},{24,216},{28,20},{3... | collective-permute-start | bytes 1572872 | tf_op jit(solution)/shard_map/while/body/eval_jaxpr/ppermute | solution.py:66
  17.5 4.2 %collective-permute-start.4 = (bf16[512,128]{1,0:T(8,128)(2,1)S(1)}, bf16[512,128]{1,0:T(8,128)(2,1)S(1)}, u32[]{:S(2)}, u32[]{:S(2)}) collective-permute-start(bf16[512,128]{1,0:T(8,128)(2,1)S(1)} %get-tuple-element.271), channel_id=1, source_target_pairs={{0,48},{4,36},{8,56},{12,44},{16,0},{20,52},{24,8},{28,60},{32,16}... | collective-permute-start | bytes 393224 | tf_op jit(solution)/shard_map/while/body/eval_jaxpr/ppermute | solution.py:66
  21.7 7.2 %collective-permute-done.4 = bf16[512,128]{1,0:T(8,128)(2,1)S(1)} collective-permute-done((bf16[512,128]{1,0:T(8,128)(2,1)S(1)}, bf16[512,128]{1,0:T(8,128)(2,1)S(1)}, u32[]{:S(2)}, u32[]{:S(2)}) %collective-permute-start.4) | collective-permute-done | bytes 131104 | tf_op jit(solution)/shard_map/while/body/eval_jaxpr/ppermute | solution.py:66
  30.6 2.3 %collective-permute-start.6 = (bf16[512,128]{1,0:T(8,128)(2,1)S(1)}, bf16[512,128]{1,0:T(8,128)(2,1)S(1)}, u32[]{:S(2)}, u32[]{:S(2)}) collective-permute-start(bf16[512,128]{1,0:T(8,128)(2,1)S(1)} %collective-permute-done.4), channel_id=1, source_target_pairs={{0,56},{4,196},{8,0},{12,204},{16,8},{20,212},{24,16},{28,220},{32... | collective-permute-start | bytes 393224 | tf_op jit(solution)/shard_map/while/body/eval_jaxpr/ppermute | solution.py:66
  32.8 2.9 %collective-permute-start.9 = (bf16[4,512,128]{2,1,0:T(8,128)(2,1)S(1)}, bf16[4,512,128]{2,1,0:T(8,128)(2,1)S(1)}, u32[]{:S(2)}, u32[]{:S(2)}) collective-permute-start(bf16[4,512,128]{2,1,0:T(8,128)(2,1)S(1)} %collective-permute-done.8.refs_2_), channel_id=1, source_target_pairs={{0,64},{4,12},{8,72},{12,20},{16,80},{20,28},{24,88},{28,36},{32,9... | collective-permute-start | bytes 1572872 | tf_op jit(solution)/shard_map/while/body/eval_jaxpr/ppermute | solution.py:66
  36.2 6.5 %collective-permute-start.11 = (bf16[4,512,128]{2,1,0:T(8,128)(2,1)S(1)}, bf16[4,512,128]{2,1,0:T(8,128)(2,1)S(1)}, u32[]{:S(2)}, u32[]{:S(2)}) collective-permute-start(bf16[4,512,128]{2,1,0:T(8,128)(2,1)S(1)} %get-tuple-element.252), channel_id=1, source_target_pairs={{0,192},{4,60},{8,200},{12,4},{16,208},{20,12},{24,216},{28,20},{3... | collective-permute-start | bytes 1572872 | tf_op jit(solution)/shard_map/while/body/eval_jaxpr/ppermute | solution.py:66
  44.4 4.4 %collective-permute-done.11.refs_5_ = bf16[4,512,128]{2,1,0:T(8,128)(2,1)S(1)} collective-permute-done((bf16[4,512,128]{2,1,0:T(8,128)(2,1)S(1)}, bf16[4,512,128]{2,1,0:T(8,128)(2,1)S(1)}, u32[]{:S(2)}, u32[]{:S(2)}) %collective-permute-start.11) | collective-permute-done | bytes 524320 | tf_op jit(solution)/shard_map/while/body/eval_jaxpr/ppermute | solution.py:66
  48.8 3.4 %collective-permute-start.12 = (bf16[4,512,128]{2,1,0:T(8,128)(2,1)S(1)}, bf16[4,512,128]{2,1,0:T(8,128)(2,1)S(1)}, u32[]{:S(2)}, u32[]{:S(2)}) collective-permute-start(bf16[4,512,128]{2,1,0:T(8,128)(2,1)S(1)} %collective-permute-done.11.refs_5_), channel_id=1, source_target_pairs={{0,192},{4,60},{8,200},{12,4},{16,208},{20,12},{24,216},{28,20},{3... | collective-permute-start | bytes 1572872 | tf_op jit(solution)/shard_map/while/body/eval_jaxpr/ppermute | solution.py:66
  55.5 2.9 %collective-permute-done.12.refs_1_ = bf16[4,512,128]{2,1,0:T(8,128)(2,1)S(1)} collective-permute-done((bf16[4,512,128]{2,1,0:T(8,128)(2,1)S(1)}, bf16[4,512,128]{2,1,0:T(8,128)(2,1)S(1)}, u32[]{:S(2)}, u32[]{:S(2)}) %collective-permute-start.12) | collective-permute-done | bytes 524320 | tf_op jit(solution)/shard_map/while/body/eval_jaxpr/ppermute | solution.py:66
  58.4 6.3 %eval_jaxpr.4.refs_4_ = f32[5,512,128]{2,1,0:T(8,128)S(1)} custom-call(s32[22]{0:T(128)} %get-tuple-element.286.rows, s32[22]{0:T(128)} %get-tuple-element.287.cols, s32[1]{0:T(128)} %get-tuple-element.288.counts, s32[64]{0:T(128)} %get-tuple-element.291.table, bf16[22,512,512]{2,1,0:T(8,128)(2,1)} %get-tuple-element.289.tiles, ...), custom_call_target="tpu_custom_call" | custom-call | flops 1107296256 | bytes 10813440 | tf_op jit(solution)/shard_map/while/body/eval_jaxpr/pallas_call | solution.py:212
  64.8 2.5 %eval_jaxpr.5 = (f32[512,128]{1,0:T(8,128)S(1)}, bf16[512,128]{1,0:T(8,128)(2,1)S(1)}, bf16[512,128]{1,0:T(8,128)(2,1)S(1)}, bf16[512,128]{1,0:T(8,128)(2,1)S(1)}) custom-call(s32[22]{0:T(128)S(1)} %copy-done.2, s32[22]{0:T(128)S(1)} %copy-done.3, s32[1]{0:T(128)} %get-tuple-element.288.counts, s32[64]{0:T(128)S(1)} %copy-done.4, ...), custom_call_target="tpu_custom_call" | custom-call | flops 369098752 | bytes 3604480 | tf_op jit(solution)/shard_map/while/body/eval_jaxpr/pallas_call | solution.py:212
  67.4 3.7 %collective-permute-start.22 = (bf16[512,128]{1,0:T(8,128)(2,1)S(1)}, bf16[512,128]{1,0:T(8,128)(2,1)S(1)}, u32[]{:S(2)}, u32[]{:S(2)}) collective-permute-start(bf16[512,128]{1,0:T(8,128)(2,1)S(1)} %get-tuple-element.254), channel_id=1, source_target_pairs={{0,3},{1,0},{2,1},{3,2},{4,7},{5,4},{6,5},{7,6},{8,11},{9,8},{10,9... | collective-permute-start | bytes 393224 | tf_op jit(solution)/shard_map/while/body/eval_jaxpr/ppermute | solution.py:39
  73.0 3.1 %collective-permute-done.23 = bf16[512,128]{1,0:T(8,128)(2,1)S(1)} collective-permute-done((bf16[512,128]{1,0:T(8,128)(2,1)S(1)}, bf16[512,128]{1,0:T(8,128)(2,1)S(1)}, u32[]{:S(2)}, u32[]{:S(2)}) %collective-permute-start.23) | collective-permute-done | bytes 131104 | tf_op jit(solution)/shard_map/while/body/eval_jaxpr/ppermute | solution.py:39
  76.2 2.5 %collective-permute-start = (bf16[512,128]{1,0:T(8,128)(2,1)S(1)}, bf16[512,128]{1,0:T(8,128)(2,1)S(1)}, u32[]{:S(2)}, u32[]{:S(2)}) collective-permute-start(bf16[512,128]{1,0:T(8,128)(2,1)S(1)} %get-tuple-element.271), channel_id=1, source_target_pairs={{0,16},{4,132},{8,24},{12,140},{16,32},{20,148},{24,40},{28,156},{... | collective-permute-start | bytes 393224 | tf_op jit(solution)/shard_map/while/body/eval_jaxpr/ppermute | solution.py:66
  78.7 2.8 %collective-permute-start.1 = (bf16[512,128]{1,0:T(8,128)(2,1)S(1)}, bf16[512,128]{1,0:T(8,128)(2,1)S(1)}, u32[]{:S(2)}, u32[]{:S(2)}) collective-permute-start(bf16[512,128]{1,0:T(8,128)(2,1)S(1)} %get-tuple-element.271), channel_id=1, source_target_pairs={{0,56},{4,196},{8,0},{12,204},{16,8},{20,212},{24,16},{28,220},{32... | collective-permute-start | bytes 393224 | tf_op jit(solution)/shard_map/while/body/eval_jaxpr/ppermute | solution.py:66
  82.0 4.1 %collective-permute-done.1 = bf16[512,128]{1,0:T(8,128)(2,1)S(1)} collective-permute-done((bf16[512,128]{1,0:T(8,128)(2,1)S(1)}, bf16[512,128]{1,0:T(8,128)(2,1)S(1)}, u32[]{:S(2)}, u32[]{:S(2)}) %collective-permute-start.1) | collective-permute-done | bytes 131104 | tf_op jit(solution)/shard_map/while/body/eval_jaxpr/ppermute | solution.py:66
  88.2 2.2 %collective-permute-start.3 = (bf16[4,512,128]{2,1,0:T(8,128)(2,1)S(1)}, bf16[4,512,128]{2,1,0:T(8,128)(2,1)S(1)}, u32[]{:S(2)}, u32[]{:S(2)}) collective-permute-start(bf16[4,512,128]{2,1,0:T(8,128)(2,1)S(1)} %select_select_fusion.4.refs_0_), channel_id=1, source_target_pairs={{0,192},{4,60},{8,200},{12,4},{16,208},{20,12},{24,216},{28,20},{3... | collective-permute-start | bytes 1572872 | tf_op jit(solution)/shard_map/while/body/eval_jaxpr/ppermute | solution.py:66
  90.4 4.0 %collective-permute-start.4 = (bf16[512,128]{1,0:T(8,128)(2,1)S(1)}, bf16[512,128]{1,0:T(8,128)(2,1)S(1)}, u32[]{:S(2)}, u32[]{:S(2)}) collective-permute-start(bf16[512,128]{1,0:T(8,128)(2,1)S(1)} %get-tuple-element.271), channel_id=1, source_target_pairs={{0,48},{4,36},{8,56},{12,44},{16,0},{20,52},{24,8},{28,60},{32,16}... | collective-permute-start | bytes 393224 | tf_op jit(solution)/shard_map/while/body/eval_jaxpr/ppermute | solution.py:66
  94.4 5.5 %collective-permute-done.4 = bf16[512,128]{1,0:T(8,128)(2,1)S(1)} collective-permute-done((bf16[512,128]{1,0:T(8,128)(2,1)S(1)}, bf16[512,128]{1,0:T(8,128)(2,1)S(1)}, u32[]{:S(2)}, u32[]{:S(2)}) %collective-permute-start.4) | collective-permute-done | bytes 131104 | tf_op jit(solution)/shard_map/while/body/eval_jaxpr/ppermute | solution.py:66
  103.6 1.9 collective-permute-start.9
  106.9 6.7 %collective-permute-start.11 = (bf16[4,512,128]{2,1,0:T(8,128)(2,1)S(1)}, bf16[4,512,128]{2,1,0:T(8,128)(2,1)S(1)}, u32[]{:S(2)}, u32[]{:S(2)}) collective-permute-start(bf16[4,512,128]{2,1,0:T(8,128)(2,1)S(1)} %get-tuple-element.252), channel_id=1, source_target_pairs={{0,192},{4,60},{8,200},{12,4},{16,208},{20,12},{24,216},{28,20},{3... | collective-permute-start | bytes 1572872 | tf_op jit(solution)/shard_map/while/body/eval_jaxpr/ppermute | solution.py:66
  113.7 3.6 %collective-permute-start.15 = (bf16[4,512,128]{2,1,0:T(8,128)(2,1)S(1)}, bf16[4,512,128]{2,1,0:T(8,128)(2,1)S(1)}, u32[]{:S(2)}, u32[]{:S(2)}) collective-permute-start(bf16[4,512,128]{2,1,0:T(8,128)(2,1)S(1)} %select_select_fusion.4.refs_0_), channel_id=1, source_target_pairs={{0,4},{4,0},{1,5},{5,1},{2,6},{6,2},{3,7},{7,3},{8,12},{12,8},{9,1... | collective-permute-start | bytes 1572872 | tf_op jit(solution)/shard_map/while/body/eval_jaxpr/ppermute | solution.py:39
  119.8 3.1 %collective-permute-start.12 = (bf16[4,512,128]{2,1,0:T(8,128)(2,1)S(1)}, bf16[4,512,128]{2,1,0:T(8,128)(2,1)S(1)}, u32[]{:S(2)}, u32[]{:S(2)}) collective-permute-start(bf16[4,512,128]{2,1,0:T(8,128)(2,1)S(1)} %collective-permute-done.11.refs_5_), channel_id=1, source_target_pairs={{0,192},{4,60},{8,200},{12,4},{16,208},{20,12},{24,216},{28,20},{3... | collective-permute-start | bytes 1572872 | tf_op jit(solution)/shard_map/while/body/eval_jaxpr/ppermute | solution.py:66
  122.9 4.7 %collective-permute-start.18 = (bf16[4,512,128]{2,1,0:T(8,128)(2,1)S(1)}, bf16[4,512,128]{2,1,0:T(8,128)(2,1)S(1)}, u32[]{:S(2)}, u32[]{:S(2)}) collective-permute-start(bf16[4,512,128]{2,1,0:T(8,128)(2,1)S(1)} %collective-permute-done.3.refs_3_), channel_id=1, source_target_pairs={{0,4},{4,0},{1,5},{5,1},{2,6},{6,2},{3,7},{7,3},{8,12},{12,8},{9,1... | collective-permute-start | bytes 1572872 | tf_op jit(solution)/shard_map/while/body/eval_jaxpr/ppermute | solution.py:39
  128.2 3.5 %collective-permute-start.13 = (bf16[4,512,128]{2,1,0:T(8,128)(2,1)S(1)}, bf16[4,512,128]{2,1,0:T(8,128)(2,1)S(1)}, u32[]{:S(2)}, u32[]{:S(2)}) collective-permute-start(bf16[4,512,128]{2,1,0:T(8,128)(2,1)S(1)} %collective-permute-done.10.refs_0_), channel_id=1, source_target_pairs={{0,4},{4,0},{1,5},{5,1},{2,6},{6,2},{3,7},{7,3},{8,12},{12,8},{9,1... | collective-permute-start | bytes 1572872 | tf_op jit(solution)/shard_map/while/body/eval_jaxpr/ppermute | solution.py:39
  131.6 2.7 %collective-permute-start.14 = (bf16[4,512,128]{2,1,0:T(8,128)(2,1)S(1)}, bf16[4,512,128]{2,1,0:T(8,128)(2,1)S(1)}, u32[]{:S(2)}, u32[]{:S(2)}) collective-permute-start(bf16[4,512,128]{2,1,0:T(8,128)(2,1)S(1)} %collective-permute-done.12.refs_1_), channel_id=1, source_target_pairs={{0,4},{4,0},{1,5},{5,1},{2,6},{6,2},{3,7},{7,3},{8,12},{12,8},{9,1... | collective-permute-start | bytes 1572872 | tf_op jit(solution)/shard_map/while/body/eval_jaxpr/ppermute | solution.py:39
  134.4 6.3 %eval_jaxpr.4.refs_4_ = f32[5,512,128]{2,1,0:T(8,128)S(1)} custom-call(s32[22]{0:T(128)} %get-tuple-element.286.rows, s32[22]{0:T(128)} %get-tuple-element.287.cols, s32[1]{0:T(128)} %get-tuple-element.288.counts, s32[64]{0:T(128)} %get-tuple-element.291.table, bf16[22,512,512]{2,1,0:T(8,128)(2,1)} %get-tuple-element.289.tiles, ...), custom_call_target="tpu_custom_call" | custom-call | flops 1107296256 | bytes 10813440 | tf_op jit(solution)/shard_map/while/body/eval_jaxpr/pallas_call | solution.py:212
  140.7 2.5 %eval_jaxpr.5 = (f32[512,128]{1,0:T(8,128)S(1)}, bf16[512,128]{1,0:T(8,128)(2,1)S(1)}, bf16[512,128]{1,0:T(8,128)(2,1)S(1)}, bf16[512,128]{1,0:T(8,128)(2,1)S(1)}) custom-call(s32[22]{0:T(128)S(1)} %copy-done.2, s32[22]{0:T(128)S(1)} %copy-done.3, s32[1]{0:T(128)} %get-tuple-element.288.counts, s32[64]{0:T(128)S(1)} %copy-done.4, ...), custom_call_target="tpu_custom_call" | custom-call | flops 369098752 | bytes 3604480 | tf_op jit(solution)/shard_map/while/body/eval_jaxpr/pallas_call | solution.py:212
  143.4 2.9 %collective-permute-start.22 = (bf16[512,128]{1,0:T(8,128)(2,1)S(1)}, bf16[512,128]{1,0:T(8,128)(2,1)S(1)}, u32[]{:S(2)}, u32[]{:S(2)}) collective-permute-start(bf16[512,128]{1,0:T(8,128)(2,1)S(1)} %get-tuple-element.254), channel_id=1, source_target_pairs={{0,3},{1,0},{2,1},{3,2},{4,7},{5,4},{6,5},{7,6},{8,11},{9,8},{10,9... | collective-permute-start | bytes 393224 | tf_op jit(solution)/shard_map/while/body/eval_jaxpr/ppermute | solution.py:39
  147.0 1.7 collective-permute-done.21
  148.7 2.6 %collective-permute-done.23 = bf16[512,128]{1,0:T(8,128)(2,1)S(1)} collective-permute-done((bf16[512,128]{1,0:T(8,128)(2,1)S(1)}, bf16[512,128]{1,0:T(8,128)(2,1)S(1)}, u32[]{:S(2)}, u32[]{:S(2)}) %collective-permute-start.23) | collective-permute-done | bytes 131104 | tf_op jit(solution)/shard_map/while/body/eval_jaxpr/ppermute | solution.py:39
  153.2 3.2 %collective-permute-start.24 = (f32[128,128]{1,0:T(8,128)S(1)}, f32[128,128]{1,0:T(8,128)S(1)}, u32[]{:S(2)}, u32[]{:S(2)}) collective-permute-start(f32[128,128]{1,0:T(8,128)S(1)} %fusion.1), channel_id=1, source_target_pairs={{0,4},{4,0},{1,5},{5,1},{2,6},{6,2},{3,7},{7,3},{8,12},{12,8},{9,1... | collective-permute-start | bytes 196616 | tf_op jit(solution)/shard_map/ppermute | solution.py:44
  157.4 2.7 %collective-permute-start.26 = (f32[128,128]{1,0:T(8,128)S(1)}, f32[128,128]{1,0:T(8,128)S(1)}, u32[]{:S(2)}, u32[]{:S(2)}) collective-permute-start(f32[128,128]{1,0:T(8,128)S(1)} %add.57), channel_id=1, source_target_pairs={{0,3},{1,0},{2,1},{3,2},{4,7},{5,4},{6,5},{7,6},{8,11},{9,8},{10,9... | collective-permute-start | bytes 196616 | tf_op jit(solution)/shard_map/ppermute | solution.py:39
  160.2 1.5 collective-permute-done.25
  162.1 2.5 %collective-permute-done.27 = f32[128,128]{1,0:T(8,128)S(1)} collective-permute-done((f32[128,128]{1,0:T(8,128)S(1)}, f32[128,128]{1,0:T(8,128)S(1)}, u32[]{:S(2)}, u32[]{:S(2)}) %collective-permute-start.27) | collective-permute-done | bytes 65568 | tf_op jit(solution)/shard_map/ppermute | solution.py:39
  164.8 3.9 %collective-permute-start.29 = (f32[128,128]{1,0:T(8,128)S(1)}, f32[128,128]{1,0:T(8,128)S(1)}, u32[]{:S(2)}, u32[]{:S(2)}) collective-permute-start(f32[128,128]{1,0:T(8,128)S(1)} %add_add_fusion.2), channel_id=1, source_target_pairs={{0,192},{64,0},{128,64},{192,128},{1,193},{65,1},{129,65},{193,129... | collective-permute-start | bytes 196616 | tf_op jit(solution)/shard_map/ppermute | solution.py:39
  170.2 3.1 %collective-permute-done.30 = f32[128,128]{1,0:T(8,128)S(1)} collective-permute-done((f32[128,128]{1,0:T(8,128)S(1)}, f32[128,128]{1,0:T(8,128)S(1)}, u32[]{:S(2)}, u32[]{:S(2)}) %collective-permute-start.30) | collective-permute-done | bytes 65568 | tf_op jit(solution)/shard_map/ppermute | solution.py:39
  174.6 2.4 %collective-permute-start.32 = (f32[128,128]{1,0:T(8,128)S(1)}, f32[128,128]{1,0:T(8,128)S(1)}, u32[]{:S(2)}, u32[]{:S(2)}) collective-permute-start(f32[128,128]{1,0:T(8,128)S(1)} %add_add_fusion.1), channel_id=1, source_target_pairs={{0,48},{8,56},{16,0},{24,8},{32,16},{40,24},{48,32},{56,40},{1,49}... | collective-permute-start | bytes 196616 | tf_op jit(solution)/shard_map/ppermute | solution.py:39
  177.0 3.3 %collective-permute-start.33 = (f32[128,128]{1,0:T(8,128)S(1)}, f32[128,128]{1,0:T(8,128)S(1)}, u32[]{:S(2)}, u32[]{:S(2)}) collective-permute-start(f32[128,128]{1,0:T(8,128)S(1)} %add_add_fusion.1), channel_id=1, source_target_pairs={{0,32},{8,40},{16,48},{24,56},{32,0},{40,8},{48,16},{56,24},{1,33}... | collective-permute-start | bytes 196616 | tf_op jit(solution)/shard_map/ppermute | solution.py:39
  180.3 5.0 %collective-permute-done.33 = f32[128,128]{1,0:T(8,128)S(1)} collective-permute-done((f32[128,128]{1,0:T(8,128)S(1)}, f32[128,128]{1,0:T(8,128)S(1)}, u32[]{:S(2)}, u32[]{:S(2)}) %collective-permute-start.33) | collective-permute-done | bytes 65568 | tf_op jit(solution)/shard_map/ppermute | solution.py:39
  185.3 2.5 %collective-permute-start.34 = (f32[128,128]{1,0:T(8,128)S(1)}, f32[128,128]{1,0:T(8,128)S(1)}, u32[]{:S(2)}, u32[]{:S(2)}) collective-permute-start(f32[128,128]{1,0:T(8,128)S(1)} %add_add_fusion), channel_id=1, source_target_pairs={{0,8},{8,0},{16,24},{24,16},{32,40},{40,32},{48,56},{56,48},{1,9},... | collective-permute-start | bytes 196616 | tf_op jit(solution)/shard_map/ppermute | solution.py:44
  187.8 1.7 collective-permute-done.34
  190.1 6.7 %orthonormalize.1 = f32[512,128]{1,0:T(8,128)} custom-call(f32[128,128]{1,0:T(8,128)} %add.67.gram_ref, f32[512,128]{1,0:T(8,128)} %copy-done), custom_call_target="tpu_custom_call" | custom-call | tf_op jit(solution)/shard_map/orthonormalize/pallas_call | solution.py:291
  (132 shorter events, 32.1 us)
Async XLA Ops:
  1.9 6.2 %collective-permute-start = (bf16[512,128]{1,0:T(8,128)(2,1)S(1)}, bf16[512,128]{1,0:T(8,128)(2,1)S(1)}, u32[]{:S(2)}, u32[]{:S(2)}) collective-permute-start(bf16[512,128]{1,0:T(8,128)(2,1)S(1)} %get-tuple-element.271), channel_id=1, source_target_pairs={{0,16},{4,132},{8,24},{12,140},{16,32},{20,148},{24,40},{28,156},{... | collective-permute-start | bytes 393224 | tf_op jit(solution)/shard_map/while/body/eval_jaxpr/ppermute | solution.py:66
  6.5 5.3 %collective-permute-start.2 = (bf16[512,128]{1,0:T(8,128)(2,1)S(1)}, bf16[512,128]{1,0:T(8,128)(2,1)S(1)}, u32[]{:S(2)}, u32[]{:S(2)}) collective-permute-start(bf16[512,128]{1,0:T(8,128)(2,1)S(1)} %get-tuple-element.271), channel_id=1, source_target_pairs={{0,8},{4,68},{8,16},{12,76},{16,24},{20,84},{24,32},{28,92},{32,40... | collective-permute-start | bytes 393224 | tf_op jit(solution)/shard_map/while/body/eval_jaxpr/ppermute | solution.py:66
  12.0 20.8 %collective-permute-start.8 = (bf16[4,512,128]{2,1,0:T(8,128)(2,1)S(1)}, bf16[4,512,128]{2,1,0:T(8,128)(2,1)S(1)}, u32[]{:S(2)}, u32[]{:S(2)}) collective-permute-start(bf16[4,512,128]{2,1,0:T(8,128)(2,1)S(1)} %select_select_fusion.4.refs_0_), channel_id=1, source_target_pairs={{0,64},{4,12},{8,72},{12,20},{16,80},{20,28},{24,88},{28,36},{32,9... | collective-permute-start | bytes 1572872 | tf_op jit(solution)/shard_map/while/body/eval_jaxpr/ppermute | solution.py:66
  13.7 22.3 %collective-permute-start.3 = (bf16[4,512,128]{2,1,0:T(8,128)(2,1)S(1)}, bf16[4,512,128]{2,1,0:T(8,128)(2,1)S(1)}, u32[]{:S(2)}, u32[]{:S(2)}) collective-permute-start(bf16[4,512,128]{2,1,0:T(8,128)(2,1)S(1)} %select_select_fusion.4.refs_0_), channel_id=1, source_target_pairs={{0,192},{4,60},{8,200},{12,4},{16,208},{20,12},{24,216},{28,20},{3... | collective-permute-start | bytes 1572872 | tf_op jit(solution)/shard_map/while/body/eval_jaxpr/ppermute | solution.py:66
  17.5 11.4 %collective-permute-start.4 = (bf16[512,128]{1,0:T(8,128)(2,1)S(1)}, bf16[512,128]{1,0:T(8,128)(2,1)S(1)}, u32[]{:S(2)}, u32[]{:S(2)}) collective-permute-start(bf16[512,128]{1,0:T(8,128)(2,1)S(1)} %get-tuple-element.271), channel_id=1, source_target_pairs={{0,48},{4,36},{8,56},{12,44},{16,0},{20,52},{24,8},{28,60},{32,16}... | collective-permute-start | bytes 393224 | tf_op jit(solution)/shard_map/while/body/eval_jaxpr/ppermute | solution.py:66
  28.9 6.8 %collective-permute-start.5 = (bf16[512,128]{1,0:T(8,128)(2,1)S(1)}, bf16[512,128]{1,0:T(8,128)(2,1)S(1)}, u32[]{:S(2)}, u32[]{:S(2)}) collective-permute-start(bf16[512,128]{1,0:T(8,128)(2,1)S(1)} %broadcast_select_fusion.6), channel_id=1, source_target_pairs={{0,16},{4,132},{8,24},{12,140},{16,32},{20,148},{24,40},{28,156},{... | collective-permute-start | bytes 393224 | tf_op jit(solution)/shard_map/while/body/eval_jaxpr/ppermute | solution.py:66
  30.2 5.8 %collective-permute-start.7 = (bf16[512,128]{1,0:T(8,128)(2,1)S(1)}, bf16[512,128]{1,0:T(8,128)(2,1)S(1)}, u32[]{:S(2)}, u32[]{:S(2)}) collective-permute-start(bf16[512,128]{1,0:T(8,128)(2,1)S(1)} %broadcast_select_fusion.6), channel_id=1, source_target_pairs={{0,8},{4,68},{8,16},{12,76},{16,24},{20,84},{24,32},{28,92},{32,40... | collective-permute-start | bytes 393224 | tf_op jit(solution)/shard_map/while/body/eval_jaxpr/ppermute | solution.py:66
  30.6 5.5 %collective-permute-start.6 = (bf16[512,128]{1,0:T(8,128)(2,1)S(1)}, bf16[512,128]{1,0:T(8,128)(2,1)S(1)}, u32[]{:S(2)}, u32[]{:S(2)}) collective-permute-start(bf16[512,128]{1,0:T(8,128)(2,1)S(1)} %collective-permute-done.4), channel_id=1, source_target_pairs={{0,56},{4,196},{8,0},{12,204},{16,8},{20,212},{24,16},{28,220},{32... | collective-permute-start | bytes 393224 | tf_op jit(solution)/shard_map/while/body/eval_jaxpr/ppermute | solution.py:66
  32.8 11.4 %collective-permute-start.9 = (bf16[4,512,128]{2,1,0:T(8,128)(2,1)S(1)}, bf16[4,512,128]{2,1,0:T(8,128)(2,1)S(1)}, u32[]{:S(2)}, u32[]{:S(2)}) collective-permute-start(bf16[4,512,128]{2,1,0:T(8,128)(2,1)S(1)} %collective-permute-done.8.refs_2_), channel_id=1, source_target_pairs={{0,64},{4,12},{8,72},{12,20},{16,80},{20,28},{24,88},{28,36},{32,9... | collective-permute-start | bytes 1572872 | tf_op jit(solution)/shard_map/while/body/eval_jaxpr/ppermute | solution.py:66
  36.2 12.6 %collective-permute-start.11 = (bf16[4,512,128]{2,1,0:T(8,128)(2,1)S(1)}, bf16[4,512,128]{2,1,0:T(8,128)(2,1)S(1)}, u32[]{:S(2)}, u32[]{:S(2)}) collective-permute-start(bf16[4,512,128]{2,1,0:T(8,128)(2,1)S(1)} %get-tuple-element.252), channel_id=1, source_target_pairs={{0,192},{4,60},{8,200},{12,4},{16,208},{20,12},{24,216},{28,20},{3... | collective-permute-start | bytes 1572872 | tf_op jit(solution)/shard_map/while/body/eval_jaxpr/ppermute | solution.py:66
  42.7 9.5 %collective-permute-start.15 = (bf16[4,512,128]{2,1,0:T(8,128)(2,1)S(1)}, bf16[4,512,128]{2,1,0:T(8,128)(2,1)S(1)}, u32[]{:S(2)}, u32[]{:S(2)}) collective-permute-start(bf16[4,512,128]{2,1,0:T(8,128)(2,1)S(1)} %select_select_fusion.4.refs_0_), channel_id=1, source_target_pairs={{0,4},{4,0},{1,5},{5,1},{2,6},{6,2},{3,7},{7,3},{8,12},{12,8},{9,1... | collective-permute-start | bytes 1572872 | tf_op jit(solution)/shard_map/while/body/eval_jaxpr/ppermute | solution.py:39
  42.7 9.5 %collective-permute-start.16 = (bf16[4,512,128]{2,1,0:T(8,128)(2,1)S(1)}, bf16[4,512,128]{2,1,0:T(8,128)(2,1)S(1)}, u32[]{:S(2)}, u32[]{:S(2)}) collective-permute-start(bf16[4,512,128]{2,1,0:T(8,128)(2,1)S(1)} %get-tuple-element.251.refs_1_), channel_id=1, source_target_pairs={{0,4},{4,0},{1,5},{5,1},{2,6},{6,2},{3,7},{7,3},{8,12},{12,8},{9,1... | collective-permute-start | bytes 1572872 | tf_op jit(solution)/shard_map/while/body/eval_jaxpr/ppermute | solution.py:39
  43.2 9.5 %collective-permute-start.17 = (bf16[4,512,128]{2,1,0:T(8,128)(2,1)S(1)}, bf16[4,512,128]{2,1,0:T(8,128)(2,1)S(1)}, u32[]{:S(2)}, u32[]{:S(2)}) collective-permute-start(bf16[4,512,128]{2,1,0:T(8,128)(2,1)S(1)} %collective-permute-done.8.refs_2_), channel_id=1, source_target_pairs={{0,4},{4,0},{1,5},{5,1},{2,6},{6,2},{3,7},{7,3},{8,12},{12,8},{9,1... | collective-permute-start | bytes 1572872 | tf_op jit(solution)/shard_map/while/body/eval_jaxpr/ppermute | solution.py:39
  44.3 9.6 %collective-permute-start.10 = (bf16[4,512,128]{2,1,0:T(8,128)(2,1)S(1)}, bf16[4,512,128]{2,1,0:T(8,128)(2,1)S(1)}, u32[]{:S(2)}, u32[]{:S(2)}) collective-permute-start(bf16[4,512,128]{2,1,0:T(8,128)(2,1)S(1)} %broadcast_select_fusion.8), channel_id=1, source_target_pairs={{0,64},{4,12},{8,72},{12,20},{16,80},{20,28},{24,88},{28,36},{32,9... | collective-permute-start | bytes 1572872 | tf_op jit(solution)/shard_map/while/body/eval_jaxpr/ppermute | solution.py:66
  48.8 9.5 %collective-permute-start.12 = (bf16[4,512,128]{2,1,0:T(8,128)(2,1)S(1)}, bf16[4,512,128]{2,1,0:T(8,128)(2,1)S(1)}, u32[]{:S(2)}, u32[]{:S(2)}) collective-permute-start(bf16[4,512,128]{2,1,0:T(8,128)(2,1)S(1)} %collective-permute-done.11.refs_5_), channel_id=1, source_target_pairs={{0,192},{4,60},{8,200},{12,4},{16,208},{20,12},{24,216},{28,20},{3... | collective-permute-start | bytes 1572872 | tf_op jit(solution)/shard_map/while/body/eval_jaxpr/ppermute | solution.py:66
  52.2 6.1 %collective-permute-start.18 = (bf16[4,512,128]{2,1,0:T(8,128)(2,1)S(1)}, bf16[4,512,128]{2,1,0:T(8,128)(2,1)S(1)}, u32[]{:S(2)}, u32[]{:S(2)}) collective-permute-start(bf16[4,512,128]{2,1,0:T(8,128)(2,1)S(1)} %collective-permute-done.3.refs_3_), channel_id=1, source_target_pairs={{0,4},{4,0},{1,5},{5,1},{2,6},{6,2},{3,7},{7,3},{8,12},{12,8},{9,1... | collective-permute-start | bytes 1572872 | tf_op jit(solution)/shard_map/while/body/eval_jaxpr/ppermute | solution.py:39
  52.2 6.1 %collective-permute-start.20 = (bf16[4,512,128]{2,1,0:T(8,128)(2,1)S(1)}, bf16[4,512,128]{2,1,0:T(8,128)(2,1)S(1)}, u32[]{:S(2)}, u32[]{:S(2)}) collective-permute-start(bf16[4,512,128]{2,1,0:T(8,128)(2,1)S(1)} %collective-permute-done.11.refs_5_), channel_id=1, source_target_pairs={{0,4},{4,0},{1,5},{5,1},{2,6},{6,2},{3,7},{7,3},{8,12},{12,8},{9,1... | collective-permute-start | bytes 1572872 | tf_op jit(solution)/shard_map/while/body/eval_jaxpr/ppermute | solution.py:39
  52.8 5.6 %collective-permute-start.19 = (bf16[4,512,128]{2,1,0:T(8,128)(2,1)S(1)}, bf16[4,512,128]{2,1,0:T(8,128)(2,1)S(1)}, u32[]{:S(2)}, u32[]{:S(2)}) collective-permute-start(bf16[4,512,128]{2,1,0:T(8,128)(2,1)S(1)} %collective-permute-done.9.refs_4_), channel_id=1, source_target_pairs={{0,4},{4,0},{1,5},{5,1},{2,6},{6,2},{3,7},{7,3},{8,12},{12,8},{9,1... | collective-permute-start | bytes 1572872 | tf_op jit(solution)/shard_map/while/body/eval_jaxpr/ppermute | solution.py:39
  53.9 10.7 %collective-permute-start.13 = (bf16[4,512,128]{2,1,0:T(8,128)(2,1)S(1)}, bf16[4,512,128]{2,1,0:T(8,128)(2,1)S(1)}, u32[]{:S(2)}, u32[]{:S(2)}) collective-permute-start(bf16[4,512,128]{2,1,0:T(8,128)(2,1)S(1)} %collective-permute-done.10.refs_0_), channel_id=1, source_target_pairs={{0,4},{4,0},{1,5},{5,1},{2,6},{6,2},{3,7},{7,3},{8,12},{12,8},{9,1... | collective-permute-start | bytes 1572872 | tf_op jit(solution)/shard_map/while/body/eval_jaxpr/ppermute | solution.py:39
  58.4 6.3 %collective-permute-start.14 = (bf16[4,512,128]{2,1,0:T(8,128)(2,1)S(1)}, bf16[4,512,128]{2,1,0:T(8,128)(2,1)S(1)}, u32[]{:S(2)}, u32[]{:S(2)}) collective-permute-start(bf16[4,512,128]{2,1,0:T(8,128)(2,1)S(1)} %collective-permute-done.12.refs_1_), channel_id=1, source_target_pairs={{0,4},{4,0},{1,5},{5,1},{2,6},{6,2},{3,7},{7,3},{8,12},{12,8},{9,1... | collective-permute-start | bytes 1572872 | tf_op jit(solution)/shard_map/while/body/eval_jaxpr/ppermute | solution.py:39
  67.3 5.4 %collective-permute-start.21 = (bf16[512,128]{1,0:T(8,128)(2,1)S(1)}, bf16[512,128]{1,0:T(8,128)(2,1)S(1)}, u32[]{:S(2)}, u32[]{:S(2)}) collective-permute-start(bf16[512,128]{1,0:T(8,128)(2,1)S(1)} %get-tuple-element.253), channel_id=1, source_target_pairs={{0,2},{1,3},{2,0},{3,1},{4,6},{5,7},{6,4},{7,5},{8,10},{9,11},{10,... | collective-permute-start | bytes 393224 | tf_op jit(solution)/shard_map/while/body/eval_jaxpr/ppermute | solution.py:39
  67.4 5.6 %collective-permute-start.22 = (bf16[512,128]{1,0:T(8,128)(2,1)S(1)}, bf16[512,128]{1,0:T(8,128)(2,1)S(1)}, u32[]{:S(2)}, u32[]{:S(2)}) collective-permute-start(bf16[512,128]{1,0:T(8,128)(2,1)S(1)} %get-tuple-element.254), channel_id=1, source_target_pairs={{0,3},{1,0},{2,1},{3,2},{4,7},{5,4},{6,5},{7,6},{8,11},{9,8},{10,9... | collective-permute-start | bytes 393224 | tf_op jit(solution)/shard_map/while/body/eval_jaxpr/ppermute | solution.py:39
  76.2 5.8 %collective-permute-start = (bf16[512,128]{1,0:T(8,128)(2,1)S(1)}, bf16[512,128]{1,0:T(8,128)(2,1)S(1)}, u32[]{:S(2)}, u32[]{:S(2)}) collective-permute-start(bf16[512,128]{1,0:T(8,128)(2,1)S(1)} %get-tuple-element.271), channel_id=1, source_target_pairs={{0,16},{4,132},{8,24},{12,140},{16,32},{20,148},{24,40},{28,156},{... | collective-permute-start | bytes 393224 | tf_op jit(solution)/shard_map/while/body/eval_jaxpr/ppermute | solution.py:66
  78.7 7.4 %collective-permute-start.1 = (bf16[512,128]{1,0:T(8,128)(2,1)S(1)}, bf16[512,128]{1,0:T(8,128)(2,1)S(1)}, u32[]{:S(2)}, u32[]{:S(2)}) collective-permute-start(bf16[512,128]{1,0:T(8,128)(2,1)S(1)} %get-tuple-element.271), channel_id=1, source_target_pairs={{0,56},{4,196},{8,0},{12,204},{16,8},{20,212},{24,16},{28,220},{32... | collective-permute-start | bytes 393224 | tf_op jit(solution)/shard_map/while/body/eval_jaxpr/ppermute | solution.py:66
  81.5 5.3 %collective-permute-start.2 = (bf16[512,128]{1,0:T(8,128)(2,1)S(1)}, bf16[512,128]{1,0:T(8,128)(2,1)S(1)}, u32[]{:S(2)}, u32[]{:S(2)}) collective-permute-start(bf16[512,128]{1,0:T(8,128)(2,1)S(1)} %get-tuple-element.271), channel_id=1, source_target_pairs={{0,8},{4,68},{8,16},{12,76},{16,24},{20,84},{24,32},{28,92},{32,40... | collective-permute-start | bytes 393224 | tf_op jit(solution)/shard_map/while/body/eval_jaxpr/ppermute | solution.py:66
  87.0 16.6 %collective-permute-start.8 = (bf16[4,512,128]{2,1,0:T(8,128)(2,1)S(1)}, bf16[4,512,128]{2,1,0:T(8,128)(2,1)S(1)}, u32[]{:S(2)}, u32[]{:S(2)}) collective-permute-start(bf16[4,512,128]{2,1,0:T(8,128)(2,1)S(1)} %select_select_fusion.4.refs_0_), channel_id=1, source_target_pairs={{0,64},{4,12},{8,72},{12,20},{16,80},{20,28},{24,88},{28,36},{32,9... | collective-permute-start | bytes 1572872 | tf_op jit(solution)/shard_map/while/body/eval_jaxpr/ppermute | solution.py:66
  88.2 18.5 %collective-permute-start.3 = (bf16[4,512,128]{2,1,0:T(8,128)(2,1)S(1)}, bf16[4,512,128]{2,1,0:T(8,128)(2,1)S(1)}, u32[]{:S(2)}, u32[]{:S(2)}) collective-permute-start(bf16[4,512,128]{2,1,0:T(8,128)(2,1)S(1)} %select_select_fusion.4.refs_0_), channel_id=1, source_target_pairs={{0,192},{4,60},{8,200},{12,4},{16,208},{20,12},{24,216},{28,20},{3... | collective-permute-start | bytes 1572872 | tf_op jit(solution)/shard_map/while/body/eval_jaxpr/ppermute | solution.py:66
  90.4 9.5 %collective-permute-start.4 = (bf16[512,128]{1,0:T(8,128)(2,1)S(1)}, bf16[512,128]{1,0:T(8,128)(2,1)S(1)}, u32[]{:S(2)}, u32[]{:S(2)}) collective-permute-start(bf16[512,128]{1,0:T(8,128)(2,1)S(1)} %get-tuple-element.271), channel_id=1, source_target_pairs={{0,48},{4,36},{8,56},{12,44},{16,0},{20,52},{24,8},{28,60},{32,16}... | collective-permute-start | bytes 393224 | tf_op jit(solution)/shard_map/while/body/eval_jaxpr/ppermute | solution.py:66
  99.9 5.6 %collective-permute-start.5 = (bf16[512,128]{1,0:T(8,128)(2,1)S(1)}, bf16[512,128]{1,0:T(8,128)(2,1)S(1)}, u32[]{:S(2)}, u32[]{:S(2)}) collective-permute-start(bf16[512,128]{1,0:T(8,128)(2,1)S(1)} %broadcast_select_fusion.6), channel_id=1, source_target_pairs={{0,16},{4,132},{8,24},{12,140},{16,32},{20,148},{24,40},{28,156},{... | collective-permute-start | bytes 393224 | tf_op jit(solution)/shard_map/while/body/eval_jaxpr/ppermute | solution.py:66
  100.9 5.8 %collective-permute-start.7 = (bf16[512,128]{1,0:T(8,128)(2,1)S(1)}, bf16[512,128]{1,0:T(8,128)(2,1)S(1)}, u32[]{:S(2)}, u32[]{:S(2)}) collective-permute-start(bf16[512,128]{1,0:T(8,128)(2,1)S(1)} %broadcast_select_fusion.6), channel_id=1, source_target_pairs={{0,8},{4,68},{8,16},{12,76},{16,24},{20,84},{24,32},{28,92},{32,40... | collective-permute-start | bytes 393224 | tf_op jit(solution)/shard_map/while/body/eval_jaxpr/ppermute | solution.py:66
  103.6 14.4 %collective-permute-start.9 = (bf16[4,512,128]{2,1,0:T(8,128)(2,1)S(1)}, bf16[4,512,128]{2,1,0:T(8,128)(2,1)S(1)}, u32[]{:S(2)}, u32[]{:S(2)}) collective-permute-start(bf16[4,512,128]{2,1,0:T(8,128)(2,1)S(1)} %collective-permute-done.8.refs_2_), channel_id=1, source_target_pairs={{0,64},{4,12},{8,72},{12,20},{16,80},{20,28},{24,88},{28,36},{32,9... | collective-permute-start | bytes 1572872 | tf_op jit(solution)/shard_map/while/body/eval_jaxpr/ppermute | solution.py:66
  106.9 12.8 %collective-permute-start.11 = (bf16[4,512,128]{2,1,0:T(8,128)(2,1)S(1)}, bf16[4,512,128]{2,1,0:T(8,128)(2,1)S(1)}, u32[]{:S(2)}, u32[]{:S(2)}) collective-permute-start(bf16[4,512,128]{2,1,0:T(8,128)(2,1)S(1)} %get-tuple-element.252), channel_id=1, source_target_pairs={{0,192},{4,60},{8,200},{12,4},{16,208},{20,12},{24,216},{28,20},{3... | collective-permute-start | bytes 1572872 | tf_op jit(solution)/shard_map/while/body/eval_jaxpr/ppermute | solution.py:66
  113.7 9.2 %collective-permute-start.15 = (bf16[4,512,128]{2,1,0:T(8,128)(2,1)S(1)}, bf16[4,512,128]{2,1,0:T(8,128)(2,1)S(1)}, u32[]{:S(2)}, u32[]{:S(2)}) collective-permute-start(bf16[4,512,128]{2,1,0:T(8,128)(2,1)S(1)} %select_select_fusion.4.refs_0_), channel_id=1, source_target_pairs={{0,4},{4,0},{1,5},{5,1},{2,6},{6,2},{3,7},{7,3},{8,12},{12,8},{9,1... | collective-permute-start | bytes 1572872 | tf_op jit(solution)/shard_map/while/body/eval_jaxpr/ppermute | solution.py:39
  117.2 10.4 %collective-permute-start.16 = (bf16[4,512,128]{2,1,0:T(8,128)(2,1)S(1)}, bf16[4,512,128]{2,1,0:T(8,128)(2,1)S(1)}, u32[]{:S(2)}, u32[]{:S(2)}) collective-permute-start(bf16[4,512,128]{2,1,0:T(8,128)(2,1)S(1)} %get-tuple-element.251.refs_1_), channel_id=1, source_target_pairs={{0,4},{4,0},{1,5},{5,1},{2,6},{6,2},{3,7},{7,3},{8,12},{12,8},{9,1... | collective-permute-start | bytes 1572872 | tf_op jit(solution)/shard_map/while/body/eval_jaxpr/ppermute | solution.py:39
  117.2 10.5 %collective-permute-start.17 = (bf16[4,512,128]{2,1,0:T(8,128)(2,1)S(1)}, bf16[4,512,128]{2,1,0:T(8,128)(2,1)S(1)}, u32[]{:S(2)}, u32[]{:S(2)}) collective-permute-start(bf16[4,512,128]{2,1,0:T(8,128)(2,1)S(1)} %collective-permute-done.8.refs_2_), channel_id=1, source_target_pairs={{0,4},{4,0},{1,5},{5,1},{2,6},{6,2},{3,7},{7,3},{8,12},{12,8},{9,1... | collective-permute-start | bytes 1572872 | tf_op jit(solution)/shard_map/while/body/eval_jaxpr/ppermute | solution.py:39
  118.0 10.1 %collective-permute-start.10 = (bf16[4,512,128]{2,1,0:T(8,128)(2,1)S(1)}, bf16[4,512,128]{2,1,0:T(8,128)(2,1)S(1)}, u32[]{:S(2)}, u32[]{:S(2)}) collective-permute-start(bf16[4,512,128]{2,1,0:T(8,128)(2,1)S(1)} %broadcast_select_fusion.8), channel_id=1, source_target_pairs={{0,64},{4,12},{8,72},{12,20},{16,80},{20,28},{24,88},{28,36},{32,9... | collective-permute-start | bytes 1572872 | tf_op jit(solution)/shard_map/while/body/eval_jaxpr/ppermute | solution.py:66
  119.8 11.9 %collective-permute-start.12 = (bf16[4,512,128]{2,1,0:T(8,128)(2,1)S(1)}, bf16[4,512,128]{2,1,0:T(8,128)(2,1)S(1)}, u32[]{:S(2)}, u32[]{:S(2)}) collective-permute-start(bf16[4,512,128]{2,1,0:T(8,128)(2,1)S(1)} %collective-permute-done.11.refs_5_), channel_id=1, source_target_pairs={{0,192},{4,60},{8,200},{12,4},{16,208},{20,12},{24,216},{28,20},{3... | collective-permute-start | bytes 1572872 | tf_op jit(solution)/shard_map/while/body/eval_jaxpr/ppermute | solution.py:66
  122.9 11.4 %collective-permute-start.18 = (bf16[4,512,128]{2,1,0:T(8,128)(2,1)S(1)}, bf16[4,512,128]{2,1,0:T(8,128)(2,1)S(1)}, u32[]{:S(2)}, u32[]{:S(2)}) collective-permute-start(bf16[4,512,128]{2,1,0:T(8,128)(2,1)S(1)} %collective-permute-done.3.refs_3_), channel_id=1, source_target_pairs={{0,4},{4,0},{1,5},{5,1},{2,6},{6,2},{3,7},{7,3},{8,12},{12,8},{9,1... | collective-permute-start | bytes 1572872 | tf_op jit(solution)/shard_map/while/body/eval_jaxpr/ppermute | solution.py:39
  127.6 6.7 %collective-permute-start.20 = (bf16[4,512,128]{2,1,0:T(8,128)(2,1)S(1)}, bf16[4,512,128]{2,1,0:T(8,128)(2,1)S(1)}, u32[]{:S(2)}, u32[]{:S(2)}) collective-permute-start(bf16[4,512,128]{2,1,0:T(8,128)(2,1)S(1)} %collective-permute-done.11.refs_5_), channel_id=1, source_target_pairs={{0,4},{4,0},{1,5},{5,1},{2,6},{6,2},{3,7},{7,3},{8,12},{12,8},{9,1... | collective-permute-start | bytes 1572872 | tf_op jit(solution)/shard_map/while/body/eval_jaxpr/ppermute | solution.py:39
  127.7 6.6 %collective-permute-start.19 = (bf16[4,512,128]{2,1,0:T(8,128)(2,1)S(1)}, bf16[4,512,128]{2,1,0:T(8,128)(2,1)S(1)}, u32[]{:S(2)}, u32[]{:S(2)}) collective-permute-start(bf16[4,512,128]{2,1,0:T(8,128)(2,1)S(1)} %collective-permute-done.9.refs_4_), channel_id=1, source_target_pairs={{0,4},{4,0},{1,5},{5,1},{2,6},{6,2},{3,7},{7,3},{8,12},{12,8},{9,1... | collective-permute-start | bytes 1572872 | tf_op jit(solution)/shard_map/while/body/eval_jaxpr/ppermute | solution.py:39
  128.2 12.5 %collective-permute-start.13 = (bf16[4,512,128]{2,1,0:T(8,128)(2,1)S(1)}, bf16[4,512,128]{2,1,0:T(8,128)(2,1)S(1)}, u32[]{:S(2)}, u32[]{:S(2)}) collective-permute-start(bf16[4,512,128]{2,1,0:T(8,128)(2,1)S(1)} %collective-permute-done.10.refs_0_), channel_id=1, source_target_pairs={{0,4},{4,0},{1,5},{5,1},{2,6},{6,2},{3,7},{7,3},{8,12},{12,8},{9,1... | collective-permute-start | bytes 1572872 | tf_op jit(solution)/shard_map/while/body/eval_jaxpr/ppermute | solution.py:39
  131.6 9.0 %collective-permute-start.14 = (bf16[4,512,128]{2,1,0:T(8,128)(2,1)S(1)}, bf16[4,512,128]{2,1,0:T(8,128)(2,1)S(1)}, u32[]{:S(2)}, u32[]{:S(2)}) collective-permute-start(bf16[4,512,128]{2,1,0:T(8,128)(2,1)S(1)} %collective-permute-done.12.refs_1_), channel_id=1, source_target_pairs={{0,4},{4,0},{1,5},{5,1},{2,6},{6,2},{3,7},{7,3},{8,12},{12,8},{9,1... | collective-permute-start | bytes 1572872 | tf_op jit(solution)/shard_map/while/body/eval_jaxpr/ppermute | solution.py:39
  143.3 5.4 %collective-permute-start.21 = (bf16[512,128]{1,0:T(8,128)(2,1)S(1)}, bf16[512,128]{1,0:T(8,128)(2,1)S(1)}, u32[]{:S(2)}, u32[]{:S(2)}) collective-permute-start(bf16[512,128]{1,0:T(8,128)(2,1)S(1)} %get-tuple-element.253), channel_id=1, source_target_pairs={{0,2},{1,3},{2,0},{3,1},{4,6},{5,7},{6,4},{7,5},{8,10},{9,11},{10,... | collective-permute-start | bytes 393224 | tf_op jit(solution)/shard_map/while/body/eval_jaxpr/ppermute | solution.py:39
  164.7 5.5 %collective-permute-start.28 = (f32[128,128]{1,0:T(8,128)S(1)}, f32[128,128]{1,0:T(8,128)S(1)}, u32[]{:S(2)}, u32[]{:S(2)}) collective-permute-start(f32[128,128]{1,0:T(8,128)S(1)} %add_add_fusion.2), channel_id=1, source_target_pairs={{0,64},{64,128},{128,192},{192,0},{1,65},{65,129},{129,193},{193,1... | collective-permute-start | bytes 196616 | tf_op jit(solution)/shard_map/ppermute | solution.py:39
  164.8 5.5 %collective-permute-start.29 = (f32[128,128]{1,0:T(8,128)S(1)}, f32[128,128]{1,0:T(8,128)S(1)}, u32[]{:S(2)}, u32[]{:S(2)}) collective-permute-start(f32[128,128]{1,0:T(8,128)S(1)} %add_add_fusion.2), channel_id=1, source_target_pairs={{0,192},{64,0},{128,64},{192,128},{1,193},{65,1},{129,65},{193,129... | collective-permute-start | bytes 196616 | tf_op jit(solution)/shard_map/ppermute | solution.py:39
  173.4 6.9 %collective-permute-start.31 = (f32[128,128]{1,0:T(8,128)S(1)}, f32[128,128]{1,0:T(8,128)S(1)}, u32[]{:S(2)}, u32[]{:S(2)}) collective-permute-start(f32[128,128]{1,0:T(8,128)S(1)} %add_add_fusion.1), channel_id=1, source_target_pairs={{0,16},{8,24},{16,32},{24,40},{32,48},{40,56},{48,0},{56,8},{1,17}... | collective-permute-start | bytes 196616 | tf_op jit(solution)/shard_map/ppermute | solution.py:39
  174.6 5.7 %collective-permute-start.32 = (f32[128,128]{1,0:T(8,128)S(1)}, f32[128,128]{1,0:T(8,128)S(1)}, u32[]{:S(2)}, u32[]{:S(2)}) collective-permute-start(f32[128,128]{1,0:T(8,128)S(1)} %add_add_fusion.1), channel_id=1, source_target_pairs={{0,48},{8,56},{16,0},{24,8},{32,16},{40,24},{48,32},{56,40},{1,49}... | collective-permute-start | bytes 196616 | tf_op jit(solution)/shard_map/ppermute | solution.py:39
  177.0 8.3 %collective-permute-start.33 = (f32[128,128]{1,0:T(8,128)S(1)}, f32[128,128]{1,0:T(8,128)S(1)}, u32[]{:S(2)}, u32[]{:S(2)}) collective-permute-start(f32[128,128]{1,0:T(8,128)S(1)} %add_add_fusion.1), channel_id=1, source_target_pairs={{0,32},{8,40},{16,48},{24,56},{32,0},{40,8},{48,16},{56,24},{1,33}... | collective-permute-start | bytes 196616 | tf_op jit(solution)/shard_map/ppermute | solution.py:39
  (25 other events, 570.1 us)

commit v2 on v1

--- a/solution.py
+++ b/solution.py
@@ -16,22 +16,21 @@
     return ((y % NY) * NZ + z % NZ) * NC + c
 
 
-def step_pairs(hop):
-    first = []
+def moves(first, second):
+    pairs = []
     for y in range(NY):
         for z in range(NZ):
-            first.append((plane_index(y, z, 0), plane_index(y, z + hop, 0)))
-            first.append((plane_index(y, z, 1), plane_index(y + hop, z, 1)))
-    return first
+            for c, (dy, dz) in enumerate((first, second)):
+                pairs.append((plane_index(y, z, c), plane_index(y + dy, z + dz, c)))
+    return pairs
+
+
+def step_pairs(hop):
+    return moves((0, hop), (hop, 0))
 
 
 def bundle_pairs(hop):
-    second = []
-    for y in range(NY):
-        for z in range(NZ):
-            second.append((plane_index(y, z, 0), plane_index(y + hop, z, 0)))
-            second.append((plane_index(y, z, 1), plane_index(y, z + hop, 1)))
-    return second
+    return moves((hop, 0), (0, hop))
 
 
 def axis_shift(value, axis, hop):
@@ -53,15 +52,6 @@
     return out
 
 
-def far_pairs():
-    pairs = []
-    for y in range(NY):
-        for z in range(NZ):
-            pairs.append((plane_index(y, z, 0), plane_index(y, z - 2, 0)))
-            pairs.append((plane_index(y, z, 1), plane_index(y, z + 4, 1)))
-    return pairs
-
-
 def send(value, pairs):
     return lax.ppermute(value, PLANE, pairs)
 
@@ -72,28 +62,28 @@
 
 def gather_blocks(block, core):
     zero = core == 0
-    plus1, minus1, plus2 = step_pairs(1), step_pairs(-1), step_pairs(2)
+    plus, minus, plus_two = step_pairs(1), step_pairs(-1), step_pairs(2)
     bplus, bminus = bundle_pairs(1), bundle_pairs(-1)
-    a1 = send(block, plus1)
-    a2 = send(block, minus1)
-    a3 = send(block, plus2)
-    a4 = send(block, far_pairs())
+    a3 = send(block, plus_two)
+    a1 = send(block, plus)
+    a2 = send(block, minus)
+    a4 = send(block, moves((0, -2), (0, -2)))
     lo = stack_blocks([block, a1, a2, a3])
     g1p = send(lo, bplus)
     g1m = send(lo, bminus)
-    onward = jnp.where(zero, a3, a4)
-    a5 = send(onward, plus1)
-    a6 = send(a4, minus1)
-    a7 = send(onward, plus2)
-    hi = stack_blocks([a4, a5, a6, a7])
+    a5 = send(jnp.where(zero, a3, a4), moves((0, 1), (0, -2)))
+    a6 = send(jnp.where(zero, a4, a5), minus)
+    a7 = send(jnp.where(zero, a3, a5), plus_two)
+    a8 = send(a5, plus)
+    rest = stack_blocks([a4, a5, a6, a7])
     g2p = send(g1p, bplus)
-    second_minus, hi_kept = lax.optimization_barrier((jnp.where(zero, hi, g1m), hi))
+    second_minus, rest = lax.optimization_barrier((jnp.where(zero, rest, g1m), rest))
     g2m = send(second_minus, bminus)
-    g3p = send(jnp.where(zero, hi_kept, g2p), bplus)
+    hi = jnp.where(zero, rest, stack_blocks([a5, a8, a6, a7]))
+    g3p = send(jnp.where(zero, rest, g2p), bplus)
     g3m = send(g2m, bminus)
-    mine = [lo, hi_kept, g1p, g1m, g2p, g2m, g3p, g3m]
-    theirs = [swap(v) for v in mine]
-    return mine + theirs
+    mine = [lo, hi, g1p, g1m, g2p, g2m, g3p, g3m]
+    return mine + [swap(v) for v in mine]
 
 
 def place_table():
@@ -305,7 +295,7 @@
         applied = apply_operator(block, tiles, lists, core)
         return applied.astype(jnp.bfloat16), latest, applied
 
-    start = (embedding.astype(jnp.bfloat16), jnp.zeros_like(embedding), embedding)
+    start = (embedding.astype(jnp.bfloat16), jnp.zeros_like(embedding), jnp.zeros_like(embedding))
     _, first_order, applied = lax.fori_loop(0, 2, apply_once, start)
     second = 2.0 * applied - embedding
     spectral = 1.2661 * embedding - 1.1303 * first_order + 0.2715 * second

time: 200 us -> 206 us (1.030)
  starting transfers between devices: 107 us -> 94.1 us
  local copies, waits for them, and re-layouts: 2.42 us -> 11.1 us
  waiting for transfers between devices: 58.1 us -> 63.6 us
  Pallas kernels: 24.3 us -> 27.2 us
    ppermute x26 -> x28, starting transfers between devices: 61.6 us -> 40.2 us  [send(): return lax.ppermute(value, PLANE, pairs)]
    ppermute x31, starting transfers between devices: 39.8 us -> 50.4 us  [axis_shift(): return lax.ppermute(value, axis, [(i, (i + hop) % n) for i in range(n)])]
    while x26 -> x36, local copies, waits for them, and re-layouts: 1.46 us -> 11.1 us
    ppermute x26 -> x28, waiting for transfers between devices: 33.8 us -> 38.8 us  [send(): return lax.ppermute(value, PLANE, pairs)]
    pallas_call x4, Pallas kernels: 17.6 us -> 20.5 us  [call(): pl.pallas_call(functools.partial(tile_kernel, ids, final), out_shape=out_...]
    ppermute x2, starting transfers between devices: 5.65 us -> 3.54 us  [axis_swap(): return lax.ppermute(value, axis, [(i, i ^ bit) for i in range(n)])]
  transfers between devices with their start and end apart: 59 -> 61, of which waited for: 28 -> 25; matrix products, arithmetic and copies ran while one was open for 1% -> 1% of each run, Pallas kernels for 6% -> 6%
where the time goes in v2:
time: 206 us; the launch traced here: 203 us
  starting transfers between devices  94.1 us (46%)
  waiting for transfers between devices  63.6 us (31%)
  Pallas kernels  27.2 us (13%)
  local copies, waits for them, and re-layouts  11.1 us (5%)
  other arithmetic  5.7 us (3%)
    ppermute x31, starting transfers between devices, axis_shift(): return lax.ppermute(value, axis, [(i, (i + hop) % n) for i in range(n)])  50.4 us
    ppermute x28, starting transfers between devices, send(): return lax.ppermute(value, PLANE, pairs)  40.2 us
    ppermute x28, waiting for transfers between devices, send(): return lax.ppermute(value, PLANE, pairs)  38.8 us
    pallas_call x4, Pallas kernels, call(): pl.pallas_call(functools.partial(tile_kernel, ids, final), out_shape=out_...  20.5 us
    ppermute x31, waiting for transfers between devices, axis_shift(): return lax.ppermute(value, axis, [(i, (i + hop) % n) for i in range(n)])  20.5 us
    while x36, local copies, waits for them, and re-layouts  11.1 us
    pallas_call x1, Pallas kernels, finish(): pl.pallas_call(functools.partial(finish_kernel, scale), out_shape=jax.Sha...  6.67 us
    ppermute x2, waiting for transfers between devices, axis_swap(): return lax.ppermute(value, axis, [(i, i ^ bit) for i in range(n)])  4.4 us
  transfers between devices with their start and end apart: 61, of which 25 were waited for; matrix products, arithmetic and copies ran while one was open for 1% of the time, Pallas kernels for 6%

profile of v2, /device:TPU:1, one launch (start us, length us, event | category | flops | bytes accessed | tf_op | source)
XLA Modules:
  0.0 202.9 jit_solution(14344524497736217195)
XLA Ops:
  1.0 157.1 %while.18 = (s32[]{:T(128)}, bf16[512,128]{1,0:T(8,128)(2,1)S(1)}, f32[512,128]{1,0:T(8,128)}, f32[512,128]{1,0:T(8,128)S(1)}, pred[]{:T(512)}, /*index=5*/s32[2...) while((s32[]{:T(128)}, bf16[512,128]{1,0:T(8,128)(2,1)S(1)}, ...), condition=%wide.region_1.2_spmd.clone.clone, body=%wide.region_0.1_spmd.sunk.clone.clone.sunk | while | flops 1480261632 | bytes 70519896 | solution.py:299
  1.0 3.8 %collective-permute-start = (bf16[512,128]{1,0:T(8,128)(2,1)S(1)}, bf16[512,128]{1,0:T(8,128)(2,1)S(1)}, u32[]{:S(2)}, u32[]{:S(2)}) collective-permute-start(bf16[512,128]{1,0:T(8,128)(2,1)S(1)} %get-tuple-element.319), channel_id=1, source_target_pairs={{0,16},{4,132},{8,24},{12,140},{16,32},{20,148},{24,40},{28,156},{... | collective-permute-start | bytes 393224 | tf_op jit(solution)/shard_map/while/body/eval_jaxpr/ppermute | solution.py:56
  4.8 6.0 %collective-permute-start.4 = (bf16[512,128]{1,0:T(8,128)(2,1)S(1)}, bf16[512,128]{1,0:T(8,128)(2,1)S(1)}, u32[]{:S(2)}, u32[]{:S(2)}) collective-permute-start(bf16[512,128]{1,0:T(8,128)(2,1)S(1)} %get-tuple-element.319), channel_id=1, source_target_pairs={{0,48},{4,52},{8,56},{12,60},{16,0},{20,4},{24,8},{28,12},{32,16},... | collective-permute-start | bytes 393224 | tf_op jit(solution)/shard_map/while/body/eval_jaxpr/ppermute | solution.py:56
  12.3 2.6 %collective-permute-done.1 = bf16[512,128]{1,0:T(8,128)(2,1)S(1)} collective-permute-done((bf16[512,128]{1,0:T(8,128)(2,1)S(1)}, bf16[512,128]{1,0:T(8,128)(2,1)S(1)}, u32[]{:S(2)}, u32[]{:S(2)}) %collective-permute-start.1) | collective-permute-done | bytes 131104 | tf_op jit(solution)/shard_map/while/body/eval_jaxpr/ppermute | solution.py:56
  14.9 2.0 collective-permute-done.2
  18.7 1.3 collective-permute-start.5
  19.9 8.5 %collective-permute-done.5 = bf16[512,128]{1,0:T(8,128)(2,1)S(1)} collective-permute-done((bf16[512,128]{1,0:T(8,128)(2,1)S(1)}, bf16[512,128]{1,0:T(8,128)(2,1)S(1)}, u32[]{:S(2)}, u32[]{:S(2)}) %collective-permute-start.5) | collective-permute-done | bytes 131104 | tf_op jit(solution)/shard_map/while/body/eval_jaxpr/ppermute | solution.py:56
  29.1 1.7 collective-permute-start.7
  30.7 3.1 %collective-permute-done.6 = bf16[512,128]{1,0:T(8,128)(2,1)S(1)} collective-permute-done((bf16[512,128]{1,0:T(8,128)(2,1)S(1)}, bf16[512,128]{1,0:T(8,128)(2,1)S(1)}, u32[]{:S(2)}, u32[]{:S(2)}) %collective-permute-start.6) | collective-permute-done | bytes 131104 | tf_op jit(solution)/shard_map/while/body/eval_jaxpr/ppermute | solution.py:56
  36.0 5.0 %collective-permute-start.16 = (bf16[4,512,128]{2,1,0:T(8,128)(2,1)S(1)}, bf16[4,512,128]{2,1,0:T(8,128)(2,1)S(1)}, u32[]{:S(2)}, u32[]{:S(2)}) collective-permute-start(bf16[4,512,128]{2,1,0:T(8,128)(2,1)S(1)} %select_select_fusion.4.refs_0_), channel_id=1, source_target_pairs={{0,4},{4,0},{1,5},{5,1},{2,6},{6,2},{3,7},{7,3},{8,12},{12,8},{9,1... | collective-permute-start | bytes 1572872 | tf_op jit(solution)/shard_map/while/body/eval_jaxpr/ppermute | solution.py:38
  41.6 5.6 %collective-permute-start.19 = (bf16[4,512,128]{2,1,0:T(8,128)(2,1)S(1)}, bf16[4,512,128]{2,1,0:T(8,128)(2,1)S(1)}, u32[]{:S(2)}, u32[]{:S(2)}) collective-permute-start(bf16[4,512,128]{2,1,0:T(8,128)(2,1)S(1)} %collective-permute-done.3.refs_3_), channel_id=1, source_target_pairs={{0,4},{4,0},{1,5},{5,1},{2,6},{6,2},{3,7},{7,3},{8,12},{12,8},{9,1... | collective-permute-start | bytes 1572872 | tf_op jit(solution)/shard_map/while/body/eval_jaxpr/ppermute | solution.py:38
  47.6 2.7 %collective-permute-start.13 = (bf16[4,512,128]{2,1,0:T(8,128)(2,1)S(1)}, bf16[4,512,128]{2,1,0:T(8,128)(2,1)}, u32[]{:S(2)}, u32[]{:S(2)}) collective-permute-start(bf16[4,512,128]{2,1,0:T(8,128)(2,1)S(1)} %collective-permute-done.12.refs_5_), channel_id=1, source_target_pairs={{0,192},{4,60},{8,200},{12,4},{16,208},{20,12},{24,216},{28,20},{3... | collective-permute-start | bytes 1572872 | tf_op jit(solution)/shard_map/while/body/eval_jaxpr/ppermute | solution.py:56
  51.0 1.2 collective-permute-start.17
  54.3 2.9 %collective-permute-done.11.refs_0_ = bf16[4,512,128]{2,1,0:T(8,128)(2,1)} collective-permute-done((bf16[4,512,128]{2,1,0:T(8,128)(2,1)S(1)}, bf16[4,512,128]{2,1,0:T(8,128)(2,1)}, u32[]{:S(2)}, u32[]{:S(2)}) %collective-permute-start.11) | collective-permute-done | bytes 524320 | tf_op jit(solution)/shard_map/while/body/eval_jaxpr/ppermute | solution.py:56
  61.2 6.2 %eval_jaxpr.4.refs_4_ = f32[5,512,128]{2,1,0:T(8,128)S(1)} custom-call(s32[22]{0:T(128)} %get-tuple-element.335.rows, s32[22]{0:T(128)} %get-tuple-element.336.cols, s32[1]{0:T(128)} %get-tuple-element.337.counts, s32[64]{0:T(128)} %get-tuple-element.340.table, bf16[22,512,512]{2,1,0:T(8,128)(2,1)} %get-tuple-element.338.tiles, ...), custom_call_target="tpu_custom_call" | custom-call | flops 1107296256 | bytes 10813440 | tf_op jit(solution)/shard_map/while/body/eval_jaxpr/pallas_call | solution.py:202
  67.5 4.1 %eval_jaxpr.5 = (f32[512,128]{1,0:T(8,128)S(1)}, bf16[512,128]{1,0:T(8,128)(2,1)S(1)}, bf16[512,128]{1,0:T(8,128)(2,1)S(1)}, bf16[512,128]{1,0:T(8,128)(2,1)S(1)}) custom-call(s32[22]{0:T(128)S(1)} %copy-done.7, s32[22]{0:T(128)S(1)} %copy-done.8, s32[1]{0:T(128)} %get-tuple-element.337.counts, s32[64]{0:T(128)S(1)} %copy-done.9, ...), custom_call_target="tpu_custom_call" | custom-call | flops 369098752 | bytes 3604480 | tf_op jit(solution)/shard_map/while/body/eval_jaxpr/pallas_call | solution.py:202
  71.7 3.7 %collective-permute-start.23 = (bf16[512,128]{1,0:T(8,128)(2,1)S(1)}, bf16[512,128]{1,0:T(8,128)(2,1)S(1)}, u32[]{:S(2)}, u32[]{:S(2)}) collective-permute-start(bf16[512,128]{1,0:T(8,128)(2,1)S(1)} %get-tuple-element.301), channel_id=1, source_target_pairs={{0,3},{1,0},{2,1},{3,2},{4,7},{5,4},{6,5},{7,6},{8,11},{9,8},{10,9... | collective-permute-start | bytes 393224 | tf_op jit(solution)/shard_map/while/body/eval_jaxpr/ppermute | solution.py:38
  77.4 2.9 %collective-permute-done.24 = bf16[512,128]{1,0:T(8,128)(2,1)S(1)} collective-permute-done((bf16[512,128]{1,0:T(8,128)(2,1)S(1)}, bf16[512,128]{1,0:T(8,128)(2,1)S(1)}, u32[]{:S(2)}, u32[]{:S(2)}) %collective-permute-start.24) | collective-permute-done | bytes 131104 | tf_op jit(solution)/shard_map/while/body/eval_jaxpr/ppermute | solution.py:38
  80.5 3.4 %collective-permute-start = (bf16[512,128]{1,0:T(8,128)(2,1)S(1)}, bf16[512,128]{1,0:T(8,128)(2,1)S(1)}, u32[]{:S(2)}, u32[]{:S(2)}) collective-permute-start(bf16[512,128]{1,0:T(8,128)(2,1)S(1)} %get-tuple-element.319), channel_id=1, source_target_pairs={{0,16},{4,132},{8,24},{12,140},{16,32},{20,148},{24,40},{28,156},{... | collective-permute-start | bytes 393224 | tf_op jit(solution)/shard_map/while/body/eval_jaxpr/ppermute | solution.py:56
  84.6 3.3 %collective-permute-start.1 = (bf16[512,128]{1,0:T(8,128)(2,1)S(1)}, bf16[512,128]{1,0:T(8,128)(2,1)S(1)}, u32[]{:S(2)}, u32[]{:S(2)}) collective-permute-start(bf16[512,128]{1,0:T(8,128)(2,1)S(1)} %get-tuple-element.319), channel_id=1, source_target_pairs={{0,56},{4,196},{8,0},{12,204},{16,8},{20,212},{24,16},{28,220},{32... | collective-permute-start | bytes 393224 | tf_op jit(solution)/shard_map/while/body/eval_jaxpr/ppermute | solution.py:56
  88.4 2.7 %collective-permute-done.1 = bf16[512,128]{1,0:T(8,128)(2,1)S(1)} collective-permute-done((bf16[512,128]{1,0:T(8,128)(2,1)S(1)}, bf16[512,128]{1,0:T(8,128)(2,1)S(1)}, u32[]{:S(2)}, u32[]{:S(2)}) %collective-permute-start.1) | collective-permute-done | bytes 131104 | tf_op jit(solution)/shard_map/while/body/eval_jaxpr/ppermute | solution.py:56
  91.2 2.1 %collective-permute-done.2 = bf16[512,128]{1,0:T(8,128)(2,1)S(1)} collective-permute-done((bf16[512,128]{1,0:T(8,128)(2,1)S(1)}, bf16[512,128]{1,0:T(8,128)(2,1)S(1)}, u32[]{:S(2)}, u32[]{:S(2)}) %collective-permute-start.2) | collective-permute-done | bytes 131104 | tf_op jit(solution)/shard_map/while/body/eval_jaxpr/ppermute | solution.py:56
  93.5 1.5 collective-permute-start.9
  95.0 2.2 %collective-permute-start.5 = (bf16[512,128]{1,0:T(8,128)(2,1)S(1)}, bf16[512,128]{1,0:T(8,128)(2,1)S(1)}, u32[]{:S(2)}, u32[]{:S(2)}) collective-permute-start(bf16[512,128]{1,0:T(8,128)(2,1)S(1)} %broadcast_select_fusion.10), channel_id=1, source_target_pairs={{0,8},{4,52},{8,16},{12,60},{16,24},{20,4},{24,32},{28,12},{32,40}... | collective-permute-start | bytes 393224 | tf_op jit(solution)/shard_map/while/body/eval_jaxpr/ppermute | solution.py:56
  97.2 7.4 %collective-permute-done.5 = bf16[512,128]{1,0:T(8,128)(2,1)S(1)} collective-permute-done((bf16[512,128]{1,0:T(8,128)(2,1)S(1)}, bf16[512,128]{1,0:T(8,128)(2,1)S(1)}, u32[]{:S(2)}, u32[]{:S(2)}) %collective-permute-start.5) | collective-permute-done | bytes 131104 | tf_op jit(solution)/shard_map/while/body/eval_jaxpr/ppermute | solution.py:56
  107.1 3.1 %collective-permute-done.6 = bf16[512,128]{1,0:T(8,128)(2,1)S(1)} collective-permute-done((bf16[512,128]{1,0:T(8,128)(2,1)S(1)}, bf16[512,128]{1,0:T(8,128)(2,1)S(1)}, u32[]{:S(2)}, u32[]{:S(2)}) %collective-permute-start.6) | collective-permute-done | bytes 131104 | tf_op jit(solution)/shard_map/while/body/eval_jaxpr/ppermute | solution.py:56
  111.2 1.4 collective-permute-start.12
  113.5 6.0 %collective-permute-start.16 = (bf16[4,512,128]{2,1,0:T(8,128)(2,1)S(1)}, bf16[4,512,128]{2,1,0:T(8,128)(2,1)S(1)}, u32[]{:S(2)}, u32[]{:S(2)}) collective-permute-start(bf16[4,512,128]{2,1,0:T(8,128)(2,1)S(1)} %select_select_fusion.4.refs_0_), channel_id=1, source_target_pairs={{0,4},{4,0},{1,5},{5,1},{2,6},{6,2},{3,7},{7,3},{8,12},{12,8},{9,1... | collective-permute-start | bytes 1572872 | tf_op jit(solution)/shard_map/while/body/eval_jaxpr/ppermute | solution.py:38
  119.5 6.2 %collective-permute-start.19 = (bf16[4,512,128]{2,1,0:T(8,128)(2,1)S(1)}, bf16[4,512,128]{2,1,0:T(8,128)(2,1)S(1)}, u32[]{:S(2)}, u32[]{:S(2)}) collective-permute-start(bf16[4,512,128]{2,1,0:T(8,128)(2,1)S(1)} %collective-permute-done.3.refs_3_), channel_id=1, source_target_pairs={{0,4},{4,0},{1,5},{5,1},{2,6},{6,2},{3,7},{7,3},{8,12},{12,8},{9,1... | collective-permute-start | bytes 1572872 | tf_op jit(solution)/shard_map/while/body/eval_jaxpr/ppermute | solution.py:38
  126.0 2.7 %collective-permute-start.13 = (bf16[4,512,128]{2,1,0:T(8,128)(2,1)S(1)}, bf16[4,512,128]{2,1,0:T(8,128)(2,1)}, u32[]{:S(2)}, u32[]{:S(2)}) collective-permute-start(bf16[4,512,128]{2,1,0:T(8,128)(2,1)S(1)} %collective-permute-done.12.refs_5_), channel_id=1, source_target_pairs={{0,192},{4,60},{8,200},{12,4},{16,208},{20,12},{24,216},{28,20},{3... | collective-permute-start | bytes 1572872 | tf_op jit(solution)/shard_map/while/body/eval_jaxpr/ppermute | solution.py:56
  132.8 2.9 %collective-permute-done.11.refs_0_ = bf16[4,512,128]{2,1,0:T(8,128)(2,1)} collective-permute-done((bf16[4,512,128]{2,1,0:T(8,128)(2,1)S(1)}, bf16[4,512,128]{2,1,0:T(8,128)(2,1)}, u32[]{:S(2)}, u32[]{:S(2)}) %collective-permute-start.11) | collective-permute-done | bytes 524320 | tf_op jit(solution)/shard_map/while/body/eval_jaxpr/ppermute | solution.py:56
  139.7 6.2 %eval_jaxpr.4.refs_4_ = f32[5,512,128]{2,1,0:T(8,128)S(1)} custom-call(s32[22]{0:T(128)} %get-tuple-element.335.rows, s32[22]{0:T(128)} %get-tuple-element.336.cols, s32[1]{0:T(128)} %get-tuple-element.337.counts, s32[64]{0:T(128)} %get-tuple-element.340.table, bf16[22,512,512]{2,1,0:T(8,128)(2,1)} %get-tuple-element.338.tiles, ...), custom_call_target="tpu_custom_call" | custom-call | flops 1107296256 | bytes 10813440 | tf_op jit(solution)/shard_map/while/body/eval_jaxpr/pallas_call | solution.py:202
  145.9 4.1 %eval_jaxpr.5 = (f32[512,128]{1,0:T(8,128)S(1)}, bf16[512,128]{1,0:T(8,128)(2,1)S(1)}, bf16[512,128]{1,0:T(8,128)(2,1)S(1)}, bf16[512,128]{1,0:T(8,128)(2,1)S(1)}) custom-call(s32[22]{0:T(128)S(1)} %copy-done.7, s32[22]{0:T(128)S(1)} %copy-done.8, s32[1]{0:T(128)} %get-tuple-element.337.counts, s32[64]{0:T(128)S(1)} %copy-done.9, ...), custom_call_target="tpu_custom_call" | custom-call | flops 369098752 | bytes 3604480 | tf_op jit(solution)/shard_map/while/body/eval_jaxpr/pallas_call | solution.py:202
  150.1 2.7 %collective-permute-start.23 = (bf16[512,128]{1,0:T(8,128)(2,1)S(1)}, bf16[512,128]{1,0:T(8,128)(2,1)S(1)}, u32[]{:S(2)}, u32[]{:S(2)}) collective-permute-start(bf16[512,128]{1,0:T(8,128)(2,1)S(1)} %get-tuple-element.301), channel_id=1, source_target_pairs={{0,3},{1,0},{2,1},{3,2},{4,7},{5,4},{6,5},{7,6},{8,11},{9,8},{10,9... | collective-permute-start | bytes 393224 | tf_op jit(solution)/shard_map/while/body/eval_jaxpr/ppermute | solution.py:38
  153.6 1.9 collective-permute-done.22
  155.4 2.4 %collective-permute-done.24 = bf16[512,128]{1,0:T(8,128)(2,1)S(1)} collective-permute-done((bf16[512,128]{1,0:T(8,128)(2,1)S(1)}, bf16[512,128]{1,0:T(8,128)(2,1)S(1)}, u32[]{:S(2)}, u32[]{:S(2)}) %collective-permute-start.24) | collective-permute-done | bytes 131104 | tf_op jit(solution)/shard_map/while/body/eval_jaxpr/ppermute | solution.py:38
  159.8 3.4 %collective-permute-start.25 = (f32[128,128]{1,0:T(8,128)S(1)}, f32[128,128]{1,0:T(8,128)S(1)}, u32[]{:S(2)}, u32[]{:S(2)}) collective-permute-start(f32[128,128]{1,0:T(8,128)S(1)} %fusion.5), channel_id=1, source_target_pairs={{0,4},{4,0},{1,5},{5,1},{2,6},{6,2},{3,7},{7,3},{8,12},{12,8},{9,1... | collective-permute-start | bytes 196616 | tf_op jit(solution)/shard_map/ppermute | solution.py:43
  164.3 2.7 %collective-permute-start.27 = (f32[128,128]{1,0:T(8,128)S(1)}, f32[128,128]{1,0:T(8,128)S(1)}, u32[]{:S(2)}, u32[]{:S(2)}) collective-permute-start(f32[128,128]{1,0:T(8,128)S(1)} %add.57), channel_id=1, source_target_pairs={{0,3},{1,0},{2,1},{3,2},{4,7},{5,4},{6,5},{7,6},{8,11},{9,8},{10,9... | collective-permute-start | bytes 196616 | tf_op jit(solution)/shard_map/ppermute | solution.py:38
  167.1 1.5 collective-permute-done.26
  169.0 2.5 %collective-permute-done.28 = f32[128,128]{1,0:T(8,128)S(1)} collective-permute-done((f32[128,128]{1,0:T(8,128)S(1)}, f32[128,128]{1,0:T(8,128)S(1)}, u32[]{:S(2)}, u32[]{:S(2)}) %collective-permute-start.28) | collective-permute-done | bytes 65568 | tf_op jit(solution)/shard_map/ppermute | solution.py:38
  171.7 3.8 %collective-permute-start.30 = (f32[128,128]{1,0:T(8,128)S(1)}, f32[128,128]{1,0:T(8,128)S(1)}, u32[]{:S(2)}, u32[]{:S(2)}) collective-permute-start(f32[128,128]{1,0:T(8,128)S(1)} %add_add_fusion.2), channel_id=1, source_target_pairs={{0,192},{64,0},{128,64},{192,128},{1,193},{65,1},{129,65},{193,129... | collective-permute-start | bytes 196616 | tf_op jit(solution)/shard_map/ppermute | solution.py:38
  177.0 3.1 %collective-permute-done.31 = f32[128,128]{1,0:T(8,128)S(1)} collective-permute-done((f32[128,128]{1,0:T(8,128)S(1)}, f32[128,128]{1,0:T(8,128)S(1)}, u32[]{:S(2)}, u32[]{:S(2)}) %collective-permute-start.31) | collective-permute-done | bytes 65568 | tf_op jit(solution)/shard_map/ppermute | solution.py:38
  180.1 1.8 collective-permute-start.32
  182.0 1.8 collective-permute-start.33
  183.8 4.4 %collective-permute-start.34 = (f32[128,128]{1,0:T(8,128)S(1)}, f32[128,128]{1,0:T(8,128)S(1)}, u32[]{:S(2)}, u32[]{:S(2)}) collective-permute-start(f32[128,128]{1,0:T(8,128)S(1)} %add_add_fusion.1), channel_id=1, source_target_pairs={{0,32},{8,40},{16,48},{24,56},{32,0},{40,8},{48,16},{56,24},{1,33}... | collective-permute-start | bytes 196616 | tf_op jit(solution)/shard_map/ppermute | solution.py:38
  188.2 3.8 %collective-permute-done.34 = f32[128,128]{1,0:T(8,128)S(1)} collective-permute-done((f32[128,128]{1,0:T(8,128)S(1)}, f32[128,128]{1,0:T(8,128)S(1)}, u32[]{:S(2)}, u32[]{:S(2)}) %collective-permute-start.34) | collective-permute-done | bytes 65568 | tf_op jit(solution)/shard_map/ppermute | solution.py:38
  192.1 3.5 %collective-permute-done.35 = f32[128,128]{1,0:T(8,128)S(1)} collective-permute-done((f32[128,128]{1,0:T(8,128)S(1)}, f32[128,128]{1,0:T(8,128)S(1)}, u32[]{:S(2)}, u32[]{:S(2)}) %collective-permute-start.35) | collective-permute-done | bytes 65568 | tf_op jit(solution)/shard_map/ppermute | solution.py:43
  196.2 6.7 %orthonormalize.1 = f32[512,128]{1,0:T(8,128)} custom-call(f32[128,128]{1,0:T(8,128)} %add.67.gram_ref, f32[512,128]{1,0:T(8,128)} %copy-done.6), custom_call_target="tpu_custom_call" | custom-call | tf_op jit(solution)/shard_map/orthonormalize/pallas_call | solution.py:281
  (146 shorter events, 37.9 us)
Async XLA Ops:
  1.0 11.3 %collective-permute-start = (bf16[512,128]{1,0:T(8,128)(2,1)S(1)}, bf16[512,128]{1,0:T(8,128)(2,1)S(1)}, u32[]{:S(2)}, u32[]{:S(2)}) collective-permute-start(bf16[512,128]{1,0:T(8,128)(2,1)S(1)} %get-tuple-element.319), channel_id=1, source_target_pairs={{0,16},{4,132},{8,24},{12,140},{16,32},{20,148},{24,40},{28,156},{... | collective-permute-start | bytes 393224 | tf_op jit(solution)/shard_map/while/body/eval_jaxpr/ppermute | solution.py:56
  4.8 13.8 %collective-permute-start.4 = (bf16[512,128]{1,0:T(8,128)(2,1)S(1)}, bf16[512,128]{1,0:T(8,128)(2,1)S(1)}, u32[]{:S(2)}, u32[]{:S(2)}) collective-permute-start(bf16[512,128]{1,0:T(8,128)(2,1)S(1)} %get-tuple-element.319), channel_id=1, source_target_pairs={{0,48},{4,52},{8,56},{12,60},{16,0},{20,4},{24,8},{28,12},{32,16},... | collective-permute-start | bytes 393224 | tf_op jit(solution)/shard_map/while/body/eval_jaxpr/ppermute | solution.py:56
  11.6 5.3 %collective-permute-start.2 = (bf16[512,128]{1,0:T(8,128)(2,1)S(1)}, bf16[512,128]{1,0:T(8,128)(2,1)S(1)}, u32[]{:S(2)}, u32[]{:S(2)}) collective-permute-start(bf16[512,128]{1,0:T(8,128)(2,1)S(1)} %get-tuple-element.319), channel_id=1, source_target_pairs={{0,8},{4,68},{8,16},{12,76},{16,24},{20,84},{24,32},{28,92},{32,40... | collective-permute-start | bytes 393224 | tf_op jit(solution)/shard_map/while/body/eval_jaxpr/ppermute | solution.py:56
  17.1 16.8 %collective-permute-start.3 = (bf16[4,512,128]{2,1,0:T(8,128)(2,1)S(1)}, bf16[4,512,128]{2,1,0:T(8,128)(2,1)S(1)}, u32[]{:S(2)}, u32[]{:S(2)}) collective-permute-start(bf16[4,512,128]{2,1,0:T(8,128)(2,1)S(1)} %select_select_fusion.4.refs_0_), channel_id=1, source_target_pairs={{0,192},{4,60},{8,200},{12,4},{16,208},{20,12},{24,216},{28,20},{3... | collective-permute-start | bytes 1572872 | tf_op jit(solution)/shard_map/while/body/eval_jaxpr/ppermute | solution.py:56
  17.9 12.9 %collective-permute-start.9 = (bf16[4,512,128]{2,1,0:T(8,128)(2,1)S(1)}, bf16[4,512,128]{2,1,0:T(8,128)(2,1)S(1)}, u32[]{:S(2)}, u32[]{:S(2)}) collective-permute-start(bf16[4,512,128]{2,1,0:T(8,128)(2,1)S(1)} %select_select_fusion.4.refs_0_), channel_id=1, source_target_pairs={{0,64},{4,12},{8,72},{12,20},{16,80},{20,28},{24,88},{28,36},{32,9... | collective-permute-start | bytes 1572872 | tf_op jit(solution)/shard_map/while/body/eval_jaxpr/ppermute | solution.py:56
  18.7 9.8 %collective-permute-start.5 = (bf16[512,128]{1,0:T(8,128)(2,1)S(1)}, bf16[512,128]{1,0:T(8,128)(2,1)S(1)}, u32[]{:S(2)}, u32[]{:S(2)}) collective-permute-start(bf16[512,128]{1,0:T(8,128)(2,1)S(1)} %broadcast_select_fusion.10), channel_id=1, source_target_pairs={{0,8},{4,52},{8,16},{12,60},{16,24},{20,4},{24,32},{28,12},{32,40}... | collective-permute-start | bytes 393224 | tf_op jit(solution)/shard_map/while/body/eval_jaxpr/ppermute | solution.py:56
  28.5 5.4 %collective-permute-start.6 = (bf16[512,128]{1,0:T(8,128)(2,1)S(1)}, bf16[512,128]{1,0:T(8,128)(2,1)S(1)}, u32[]{:S(2)}, u32[]{:S(2)}) collective-permute-start(bf16[512,128]{1,0:T(8,128)(2,1)S(1)} %get-tuple-element.294), channel_id=1, source_target_pairs={{0,16},{4,132},{8,24},{12,140},{16,32},{20,148},{24,40},{28,156},{... | collective-permute-start | bytes 393224 | tf_op jit(solution)/shard_map/while/body/eval_jaxpr/ppermute | solution.py:56
  30.7 16.5 %collective-permute-start.10 = (bf16[4,512,128]{2,1,0:T(8,128)(2,1)S(1)}, bf16[4,512,128]{2,1,0:T(8,128)(2,1)S(1)}, u32[]{:S(2)}, u32[]{:S(2)}) collective-permute-start(bf16[4,512,128]{2,1,0:T(8,128)(2,1)S(1)} %collective-permute-done.9.refs_2_), channel_id=1, source_target_pairs={{0,64},{4,12},{8,72},{12,20},{16,80},{20,28},{24,88},{28,36},{32,9... | collective-permute-start | bytes 1572872 | tf_op jit(solution)/shard_map/while/body/eval_jaxpr/ppermute | solution.py:56
  34.1 13.5 %collective-permute-start.12 = (bf16[4,512,128]{2,1,0:T(8,128)(2,1)S(1)}, bf16[4,512,128]{2,1,0:T(8,128)(2,1)S(1)}, u32[]{:S(2)}, u32[]{:S(2)}) collective-permute-start(bf16[4,512,128]{2,1,0:T(8,128)(2,1)S(1)} %get-tuple-element.298), channel_id=1, source_target_pairs={{0,192},{4,60},{8,200},{12,4},{16,208},{20,12},{24,216},{28,20},{3... | collective-permute-start | bytes 1572872 | tf_op jit(solution)/shard_map/while/body/eval_jaxpr/ppermute | solution.py:56
  34.9 6.7 %collective-permute-start.8 = (bf16[512,128]{1,0:T(8,128)(2,1)S(1)}, bf16[512,128]{1,0:T(8,128)(2,1)S(1)}, u32[]{:S(2)}, u32[]{:S(2)}) collective-permute-start(bf16[512,128]{1,0:T(8,128)(2,1)S(1)} %collective-permute-done.5), channel_id=1, source_target_pairs={{0,8},{4,68},{8,16},{12,76},{16,24},{20,84},{24,32},{28,92},{32,40... | collective-permute-start | bytes 393224 | tf_op jit(solution)/shard_map/while/body/eval_jaxpr/ppermute | solution.py:56
  36.0 14.2 %collective-permute-start.16 = (bf16[4,512,128]{2,1,0:T(8,128)(2,1)S(1)}, bf16[4,512,128]{2,1,0:T(8,128)(2,1)S(1)}, u32[]{:S(2)}, u32[]{:S(2)}) collective-permute-start(bf16[4,512,128]{2,1,0:T(8,128)(2,1)S(1)} %select_select_fusion.4.refs_0_), channel_id=1, source_target_pairs={{0,4},{4,0},{1,5},{5,1},{2,6},{6,2},{3,7},{7,3},{8,12},{12,8},{9,1... | collective-permute-start | bytes 1572872 | tf_op jit(solution)/shard_map/while/body/eval_jaxpr/ppermute | solution.py:38
  41.0 11.2 %collective-permute-start.18 = (bf16[4,512,128]{2,1,0:T(8,128)(2,1)S(1)}, bf16[4,512,128]{2,1,0:T(8,128)(2,1)S(1)}, u32[]{:S(2)}, u32[]{:S(2)}) collective-permute-start(bf16[4,512,128]{2,1,0:T(8,128)(2,1)S(1)} %collective-permute-done.9.refs_2_), channel_id=1, source_target_pairs={{0,4},{4,0},{1,5},{5,1},{2,6},{6,2},{3,7},{7,3},{8,12},{12,8},{9,1... | collective-permute-start | bytes 1572872 | tf_op jit(solution)/shard_map/while/body/eval_jaxpr/ppermute | solution.py:38
  41.6 11.4 %collective-permute-start.19 = (bf16[4,512,128]{2,1,0:T(8,128)(2,1)S(1)}, bf16[4,512,128]{2,1,0:T(8,128)(2,1)S(1)}, u32[]{:S(2)}, u32[]{:S(2)}) collective-permute-start(bf16[4,512,128]{2,1,0:T(8,128)(2,1)S(1)} %collective-permute-done.3.refs_3_), channel_id=1, source_target_pairs={{0,4},{4,0},{1,5},{5,1},{2,6},{6,2},{3,7},{7,3},{8,12},{12,8},{9,1... | collective-permute-start | bytes 1572872 | tf_op jit(solution)/shard_map/while/body/eval_jaxpr/ppermute | solution.py:38
  47.5 9.7 %collective-permute-start.11 = (bf16[4,512,128]{2,1,0:T(8,128)(2,1)S(1)}, bf16[4,512,128]{2,1,0:T(8,128)(2,1)}, u32[]{:S(2)}, u32[]{:S(2)}) collective-permute-start(bf16[4,512,128]{2,1,0:T(8,128)(2,1)S(1)} %get-tuple-element.297), channel_id=1, source_target_pairs={{0,64},{4,12},{8,72},{12,20},{16,80},{20,28},{24,88},{28,36},{32,9... | collective-permute-start | bytes 1572872 | tf_op jit(solution)/shard_map/while/body/eval_jaxpr/ppermute | solution.py:56
  47.6 10.5 %collective-permute-start.13 = (bf16[4,512,128]{2,1,0:T(8,128)(2,1)S(1)}, bf16[4,512,128]{2,1,0:T(8,128)(2,1)}, u32[]{:S(2)}, u32[]{:S(2)}) collective-permute-start(bf16[4,512,128]{2,1,0:T(8,128)(2,1)S(1)} %collective-permute-done.12.refs_5_), channel_id=1, source_target_pairs={{0,192},{4,60},{8,200},{12,4},{16,208},{20,12},{24,216},{28,20},{3... | collective-permute-start | bytes 1572872 | tf_op jit(solution)/shard_map/while/body/eval_jaxpr/ppermute | solution.py:56
  51.0 7.1 %collective-permute-start.17 = (bf16[4,512,128]{2,1,0:T(8,128)(2,1)S(1)}, bf16[4,512,128]{2,1,0:T(8,128)(2,1)}, u32[]{:S(2)}, u32[]{:S(2)}) collective-permute-start(bf16[4,512,128]{2,1,0:T(8,128)(2,1)S(1)} %get-tuple-element.299.refs_1_), channel_id=1, source_target_pairs={{0,4},{4,0},{1,5},{5,1},{2,6},{6,2},{3,7},{7,3},{8,12},{12,8},{9,1... | collective-permute-start | bytes 1572872 | tf_op jit(solution)/shard_map/while/body/eval_jaxpr/ppermute | solution.py:38
  53.0 5.1 %collective-permute-start.21 = (bf16[4,512,128]{2,1,0:T(8,128)(2,1)S(1)}, bf16[4,512,128]{2,1,0:T(8,128)(2,1)}, u32[]{:S(2)}, u32[]{:S(2)}) collective-permute-start(bf16[4,512,128]{2,1,0:T(8,128)(2,1)S(1)} %collective-permute-done.12.refs_5_), channel_id=1, source_target_pairs={{0,4},{4,0},{1,5},{5,1},{2,6},{6,2},{3,7},{7,3},{8,12},{12,8},{9,1... | collective-permute-start | bytes 1572872 | tf_op jit(solution)/shard_map/while/body/eval_jaxpr/ppermute | solution.py:38
  57.2 10.2 %collective-permute-start.14 = (bf16[4,512,128]{2,1,0:T(8,128)(2,1)}, bf16[4,512,128]{2,1,0:T(8,128)(2,1)}, u32[]{:S(2)}, u32[]{:S(2)}) collective-permute-start(bf16[4,512,128]{2,1,0:T(8,128)(2,1)} %collective-permute-done.11.refs_0_), channel_id=1, source_target_pairs={{0,4},{4,0},{1,5},{5,1},{2,6},{6,2},{3,7},{7,3},{8,12},{12,8},{9,1... | collective-permute-start | bytes 1572872 | tf_op jit(solution)/shard_map/while/body/eval_jaxpr/ppermute | solution.py:38
  58.1 9.4 %collective-permute-start.15 = (bf16[4,512,128]{2,1,0:T(8,128)(2,1)}, bf16[4,512,128]{2,1,0:T(8,128)(2,1)}, u32[]{:S(2)}, u32[]{:S(2)}) collective-permute-start(bf16[4,512,128]{2,1,0:T(8,128)(2,1)} %collective-permute-done.13.refs_1_), channel_id=1, source_target_pairs={{0,4},{4,0},{1,5},{5,1},{2,6},{6,2},{3,7},{7,3},{8,12},{12,8},{9,1... | collective-permute-start | bytes 1572872 | tf_op jit(solution)/shard_map/while/body/eval_jaxpr/ppermute | solution.py:38
  71.6 5.4 %collective-permute-start.22 = (bf16[512,128]{1,0:T(8,128)(2,1)S(1)}, bf16[512,128]{1,0:T(8,128)(2,1)S(1)}, u32[]{:S(2)}, u32[]{:S(2)}) collective-permute-start(bf16[512,128]{1,0:T(8,128)(2,1)S(1)} %get-tuple-element.300), channel_id=1, source_target_pairs={{0,2},{1,3},{2,0},{3,1},{4,6},{5,7},{6,4},{7,5},{8,10},{9,11},{10,... | collective-permute-start | bytes 393224 | tf_op jit(solution)/shard_map/while/body/eval_jaxpr/ppermute | solution.py:38
  71.7 5.8 %collective-permute-start.23 = (bf16[512,128]{1,0:T(8,128)(2,1)S(1)}, bf16[512,128]{1,0:T(8,128)(2,1)S(1)}, u32[]{:S(2)}, u32[]{:S(2)}) collective-permute-start(bf16[512,128]{1,0:T(8,128)(2,1)S(1)} %get-tuple-element.301), channel_id=1, source_target_pairs={{0,3},{1,0},{2,1},{3,2},{4,7},{5,4},{6,5},{7,6},{8,11},{9,8},{10,9... | collective-permute-start | bytes 393224 | tf_op jit(solution)/shard_map/while/body/eval_jaxpr/ppermute | solution.py:38
  80.5 8.0 %collective-permute-start = (bf16[512,128]{1,0:T(8,128)(2,1)S(1)}, bf16[512,128]{1,0:T(8,128)(2,1)S(1)}, u32[]{:S(2)}, u32[]{:S(2)}) collective-permute-start(bf16[512,128]{1,0:T(8,128)(2,1)S(1)} %get-tuple-element.319), channel_id=1, source_target_pairs={{0,16},{4,132},{8,24},{12,140},{16,32},{20,148},{24,40},{28,156},{... | collective-permute-start | bytes 393224 | tf_op jit(solution)/shard_map/while/body/eval_jaxpr/ppermute | solution.py:56
  83.9 11.1 %collective-permute-start.4 = (bf16[512,128]{1,0:T(8,128)(2,1)S(1)}, bf16[512,128]{1,0:T(8,128)(2,1)S(1)}, u32[]{:S(2)}, u32[]{:S(2)}) collective-permute-start(bf16[512,128]{1,0:T(8,128)(2,1)S(1)} %get-tuple-element.319), channel_id=1, source_target_pairs={{0,48},{4,52},{8,56},{12,60},{16,0},{20,4},{24,8},{28,12},{32,16},... | collective-permute-start | bytes 393224 | tf_op jit(solution)/shard_map/while/body/eval_jaxpr/ppermute | solution.py:56
  84.6 6.5 %collective-permute-start.1 = (bf16[512,128]{1,0:T(8,128)(2,1)S(1)}, bf16[512,128]{1,0:T(8,128)(2,1)S(1)}, u32[]{:S(2)}, u32[]{:S(2)}) collective-permute-start(bf16[512,128]{1,0:T(8,128)(2,1)S(1)} %get-tuple-element.319), channel_id=1, source_target_pairs={{0,56},{4,196},{8,0},{12,204},{16,8},{20,212},{24,16},{28,220},{32... | collective-permute-start | bytes 393224 | tf_op jit(solution)/shard_map/while/body/eval_jaxpr/ppermute | solution.py:56
  87.9 5.3 %collective-permute-start.2 = (bf16[512,128]{1,0:T(8,128)(2,1)S(1)}, bf16[512,128]{1,0:T(8,128)(2,1)S(1)}, u32[]{:S(2)}, u32[]{:S(2)}) collective-permute-start(bf16[512,128]{1,0:T(8,128)(2,1)S(1)} %get-tuple-element.319), channel_id=1, source_target_pairs={{0,8},{4,68},{8,16},{12,76},{16,24},{20,84},{24,32},{28,92},{32,40... | collective-permute-start | bytes 393224 | tf_op jit(solution)/shard_map/while/body/eval_jaxpr/ppermute | solution.py:56
  93.4 17.5 %collective-permute-start.3 = (bf16[4,512,128]{2,1,0:T(8,128)(2,1)S(1)}, bf16[4,512,128]{2,1,0:T(8,128)(2,1)S(1)}, u32[]{:S(2)}, u32[]{:S(2)}) collective-permute-start(bf16[4,512,128]{2,1,0:T(8,128)(2,1)S(1)} %select_select_fusion.4.refs_0_), channel_id=1, source_target_pairs={{0,192},{4,60},{8,200},{12,4},{16,208},{20,12},{24,216},{28,20},{3... | collective-permute-start | bytes 1572872 | tf_op jit(solution)/shard_map/while/body/eval_jaxpr/ppermute | solution.py:56
  93.5 13.1 %collective-permute-start.9 = (bf16[4,512,128]{2,1,0:T(8,128)(2,1)S(1)}, bf16[4,512,128]{2,1,0:T(8,128)(2,1)S(1)}, u32[]{:S(2)}, u32[]{:S(2)}) collective-permute-start(bf16[4,512,128]{2,1,0:T(8,128)(2,1)S(1)} %select_select_fusion.4.refs_0_), channel_id=1, source_target_pairs={{0,64},{4,12},{8,72},{12,20},{16,80},{20,28},{24,88},{28,36},{32,9... | collective-permute-start | bytes 1572872 | tf_op jit(solution)/shard_map/while/body/eval_jaxpr/ppermute | solution.py:56
  95.0 9.7 %collective-permute-start.5 = (bf16[512,128]{1,0:T(8,128)(2,1)S(1)}, bf16[512,128]{1,0:T(8,128)(2,1)S(1)}, u32[]{:S(2)}, u32[]{:S(2)}) collective-permute-start(bf16[512,128]{1,0:T(8,128)(2,1)S(1)} %broadcast_select_fusion.10), channel_id=1, source_target_pairs={{0,8},{4,52},{8,16},{12,60},{16,24},{20,4},{24,32},{28,12},{32,40}... | collective-permute-start | bytes 393224 | tf_op jit(solution)/shard_map/while/body/eval_jaxpr/ppermute | solution.py:56
  104.7 5.5 %collective-permute-start.6 = (bf16[512,128]{1,0:T(8,128)(2,1)S(1)}, bf16[512,128]{1,0:T(8,128)(2,1)S(1)}, u32[]{:S(2)}, u32[]{:S(2)}) collective-permute-start(bf16[512,128]{1,0:T(8,128)(2,1)S(1)} %get-tuple-element.294), channel_id=1, source_target_pairs={{0,16},{4,132},{8,24},{12,140},{16,32},{20,148},{24,40},{28,156},{... | collective-permute-start | bytes 393224 | tf_op jit(solution)/shard_map/while/body/eval_jaxpr/ppermute | solution.py:56
  105.8 5.2 %collective-permute-start.7 = (bf16[512,128]{1,0:T(8,128)(2,1)S(1)}, bf16[512,128]{1,0:T(8,128)(2,1)S(1)}, u32[]{:S(2)}, u32[]{:S(2)}) collective-permute-start(bf16[512,128]{1,0:T(8,128)(2,1)S(1)} %get-tuple-element.295), channel_id=1, source_target_pairs={{0,56},{4,196},{8,0},{12,204},{16,8},{20,212},{24,16},{28,220},{32... | collective-permute-start | bytes 393224 | tf_op jit(solution)/shard_map/while/body/eval_jaxpr/ppermute | solution.py:56
  106.6 19.1 %collective-permute-start.10 = (bf16[4,512,128]{2,1,0:T(8,128)(2,1)S(1)}, bf16[4,512,128]{2,1,0:T(8,128)(2,1)S(1)}, u32[]{:S(2)}, u32[]{:S(2)}) collective-permute-start(bf16[4,512,128]{2,1,0:T(8,128)(2,1)S(1)} %collective-permute-done.9.refs_2_), channel_id=1, source_target_pairs={{0,64},{4,12},{8,72},{12,20},{16,80},{20,28},{24,88},{28,36},{32,9... | collective-permute-start | bytes 1572872 | tf_op jit(solution)/shard_map/while/body/eval_jaxpr/ppermute | solution.py:56
  111.2 14.9 %collective-permute-start.12 = (bf16[4,512,128]{2,1,0:T(8,128)(2,1)S(1)}, bf16[4,512,128]{2,1,0:T(8,128)(2,1)S(1)}, u32[]{:S(2)}, u32[]{:S(2)}) collective-permute-start(bf16[4,512,128]{2,1,0:T(8,128)(2,1)S(1)} %get-tuple-element.298), channel_id=1, source_target_pairs={{0,192},{4,60},{8,200},{12,4},{16,208},{20,12},{24,216},{28,20},{3... | collective-permute-start | bytes 1572872 | tf_op jit(solution)/shard_map/while/body/eval_jaxpr/ppermute | solution.py:56
  112.5 7.0 %collective-permute-start.8 = (bf16[512,128]{1,0:T(8,128)(2,1)S(1)}, bf16[512,128]{1,0:T(8,128)(2,1)S(1)}, u32[]{:S(2)}, u32[]{:S(2)}) collective-permute-start(bf16[512,128]{1,0:T(8,128)(2,1)S(1)} %collective-permute-done.5), channel_id=1, source_target_pairs={{0,8},{4,68},{8,16},{12,76},{16,24},{20,84},{24,32},{28,92},{32,40... | collective-permute-start | bytes 393224 | tf_op jit(solution)/shard_map/while/body/eval_jaxpr/ppermute | solution.py:56
  113.5 15.2 %collective-permute-start.16 = (bf16[4,512,128]{2,1,0:T(8,128)(2,1)S(1)}, bf16[4,512,128]{2,1,0:T(8,128)(2,1)S(1)}, u32[]{:S(2)}, u32[]{:S(2)}) collective-permute-start(bf16[4,512,128]{2,1,0:T(8,128)(2,1)S(1)} %select_select_fusion.4.refs_0_), channel_id=1, source_target_pairs={{0,4},{4,0},{1,5},{5,1},{2,6},{6,2},{3,7},{7,3},{8,12},{12,8},{9,1... | collective-permute-start | bytes 1572872 | tf_op jit(solution)/shard_map/while/body/eval_jaxpr/ppermute | solution.py:38
  119.5 11.2 %collective-permute-start.18 = (bf16[4,512,128]{2,1,0:T(8,128)(2,1)S(1)}, bf16[4,512,128]{2,1,0:T(8,128)(2,1)S(1)}, u32[]{:S(2)}, u32[]{:S(2)}) collective-permute-start(bf16[4,512,128]{2,1,0:T(8,128)(2,1)S(1)} %collective-permute-done.9.refs_2_), channel_id=1, source_target_pairs={{0,4},{4,0},{1,5},{5,1},{2,6},{6,2},{3,7},{7,3},{8,12},{12,8},{9,1... | collective-permute-start | bytes 1572872 | tf_op jit(solution)/shard_map/while/body/eval_jaxpr/ppermute | solution.py:38
  119.5 12.0 %collective-permute-start.19 = (bf16[4,512,128]{2,1,0:T(8,128)(2,1)S(1)}, bf16[4,512,128]{2,1,0:T(8,128)(2,1)S(1)}, u32[]{:S(2)}, u32[]{:S(2)}) collective-permute-start(bf16[4,512,128]{2,1,0:T(8,128)(2,1)S(1)} %collective-permute-done.3.refs_3_), channel_id=1, source_target_pairs={{0,4},{4,0},{1,5},{5,1},{2,6},{6,2},{3,7},{7,3},{8,12},{12,8},{9,1... | collective-permute-start | bytes 1572872 | tf_op jit(solution)/shard_map/while/body/eval_jaxpr/ppermute | solution.py:38
  125.9 9.7 %collective-permute-start.11 = (bf16[4,512,128]{2,1,0:T(8,128)(2,1)S(1)}, bf16[4,512,128]{2,1,0:T(8,128)(2,1)}, u32[]{:S(2)}, u32[]{:S(2)}) collective-permute-start(bf16[4,512,128]{2,1,0:T(8,128)(2,1)S(1)} %get-tuple-element.297), channel_id=1, source_target_pairs={{0,64},{4,12},{8,72},{12,20},{16,80},{20,28},{24,88},{28,36},{32,9... | collective-permute-start | bytes 1572872 | tf_op jit(solution)/shard_map/while/body/eval_jaxpr/ppermute | solution.py:56
  126.0 10.5 %collective-permute-start.13 = (bf16[4,512,128]{2,1,0:T(8,128)(2,1)S(1)}, bf16[4,512,128]{2,1,0:T(8,128)(2,1)}, u32[]{:S(2)}, u32[]{:S(2)}) collective-permute-start(bf16[4,512,128]{2,1,0:T(8,128)(2,1)S(1)} %collective-permute-done.12.refs_5_), channel_id=1, source_target_pairs={{0,192},{4,60},{8,200},{12,4},{16,208},{20,12},{24,216},{28,20},{3... | collective-permute-start | bytes 1572872 | tf_op jit(solution)/shard_map/while/body/eval_jaxpr/ppermute | solution.py:56
  129.5 7.1 %collective-permute-start.17 = (bf16[4,512,128]{2,1,0:T(8,128)(2,1)S(1)}, bf16[4,512,128]{2,1,0:T(8,128)(2,1)}, u32[]{:S(2)}, u32[]{:S(2)}) collective-permute-start(bf16[4,512,128]{2,1,0:T(8,128)(2,1)S(1)} %get-tuple-element.299.refs_1_), channel_id=1, source_target_pairs={{0,4},{4,0},{1,5},{5,1},{2,6},{6,2},{3,7},{7,3},{8,12},{12,8},{9,1... | collective-permute-start | bytes 1572872 | tf_op jit(solution)/shard_map/while/body/eval_jaxpr/ppermute | solution.py:38
  135.6 10.2 %collective-permute-start.14 = (bf16[4,512,128]{2,1,0:T(8,128)(2,1)}, bf16[4,512,128]{2,1,0:T(8,128)(2,1)}, u32[]{:S(2)}, u32[]{:S(2)}) collective-permute-start(bf16[4,512,128]{2,1,0:T(8,128)(2,1)} %collective-permute-done.11.refs_0_), channel_id=1, source_target_pairs={{0,4},{4,0},{1,5},{5,1},{2,6},{6,2},{3,7},{7,3},{8,12},{12,8},{9,1... | collective-permute-start | bytes 1572872 | tf_op jit(solution)/shard_map/while/body/eval_jaxpr/ppermute | solution.py:38
  136.5 9.4 %collective-permute-start.15 = (bf16[4,512,128]{2,1,0:T(8,128)(2,1)}, bf16[4,512,128]{2,1,0:T(8,128)(2,1)}, u32[]{:S(2)}, u32[]{:S(2)}) collective-permute-start(bf16[4,512,128]{2,1,0:T(8,128)(2,1)} %collective-permute-done.13.refs_1_), channel_id=1, source_target_pairs={{0,4},{4,0},{1,5},{5,1},{2,6},{6,2},{3,7},{7,3},{8,12},{12,8},{9,1... | collective-permute-start | bytes 1572872 | tf_op jit(solution)/shard_map/while/body/eval_jaxpr/ppermute | solution.py:38
  150.0 5.4 %collective-permute-start.22 = (bf16[512,128]{1,0:T(8,128)(2,1)S(1)}, bf16[512,128]{1,0:T(8,128)(2,1)S(1)}, u32[]{:S(2)}, u32[]{:S(2)}) collective-permute-start(bf16[512,128]{1,0:T(8,128)(2,1)S(1)} %get-tuple-element.300), channel_id=1, source_target_pairs={{0,2},{1,3},{2,0},{3,1},{4,6},{5,7},{6,4},{7,5},{8,10},{9,11},{10,... | collective-permute-start | bytes 393224 | tf_op jit(solution)/shard_map/while/body/eval_jaxpr/ppermute | solution.py:38
  150.1 5.3 %collective-permute-start.23 = (bf16[512,128]{1,0:T(8,128)(2,1)S(1)}, bf16[512,128]{1,0:T(8,128)(2,1)S(1)}, u32[]{:S(2)}, u32[]{:S(2)}) collective-permute-start(bf16[512,128]{1,0:T(8,128)(2,1)S(1)} %get-tuple-element.301), channel_id=1, source_target_pairs={{0,3},{1,0},{2,1},{3,2},{4,7},{5,4},{6,5},{7,6},{8,11},{9,8},{10,9... | collective-permute-start | bytes 393224 | tf_op jit(solution)/shard_map/while/body/eval_jaxpr/ppermute | solution.py:38
  171.6 5.4 %collective-permute-start.29 = (f32[128,128]{1,0:T(8,128)S(1)}, f32[128,128]{1,0:T(8,128)S(1)}, u32[]{:S(2)}, u32[]{:S(2)}) collective-permute-start(f32[128,128]{1,0:T(8,128)S(1)} %add_add_fusion.2), channel_id=1, source_target_pairs={{0,64},{64,128},{128,192},{192,0},{1,65},{65,129},{129,193},{193,1... | collective-permute-start | bytes 196616 | tf_op jit(solution)/shard_map/ppermute | solution.py:38
  171.7 5.3 %collective-permute-start.30 = (f32[128,128]{1,0:T(8,128)S(1)}, f32[128,128]{1,0:T(8,128)S(1)}, u32[]{:S(2)}, u32[]{:S(2)}) collective-permute-start(f32[128,128]{1,0:T(8,128)S(1)} %add_add_fusion.2), channel_id=1, source_target_pairs={{0,192},{64,0},{128,64},{192,128},{1,193},{65,1},{129,65},{193,129... | collective-permute-start | bytes 196616 | tf_op jit(solution)/shard_map/ppermute | solution.py:38
  180.1 8.1 %collective-permute-start.32 = (f32[128,128]{1,0:T(8,128)S(1)}, f32[128,128]{1,0:T(8,128)S(1)}, u32[]{:S(2)}, u32[]{:S(2)}) collective-permute-start(f32[128,128]{1,0:T(8,128)S(1)} %add_add_fusion.1), channel_id=1, source_target_pairs={{0,16},{8,24},{16,32},{24,40},{32,48},{40,56},{48,0},{56,8},{1,17}... | collective-permute-start | bytes 196616 | tf_op jit(solution)/shard_map/ppermute | solution.py:38
  182.0 6.2 %collective-permute-start.33 = (f32[128,128]{1,0:T(8,128)S(1)}, f32[128,128]{1,0:T(8,128)S(1)}, u32[]{:S(2)}, u32[]{:S(2)}) collective-permute-start(f32[128,128]{1,0:T(8,128)S(1)} %add_add_fusion.1), channel_id=1, source_target_pairs={{0,48},{8,56},{16,0},{24,8},{32,16},{40,24},{48,32},{56,40},{1,49}... | collective-permute-start | bytes 196616 | tf_op jit(solution)/shard_map/ppermute | solution.py:38
  183.8 8.2 %collective-permute-start.34 = (f32[128,128]{1,0:T(8,128)S(1)}, f32[128,128]{1,0:T(8,128)S(1)}, u32[]{:S(2)}, u32[]{:S(2)}) collective-permute-start(f32[128,128]{1,0:T(8,128)S(1)} %add_add_fusion.1), channel_id=1, source_target_pairs={{0,32},{8,40},{16,48},{24,56},{32,0},{40,8},{48,16},{56,24},{1,33}... | collective-permute-start | bytes 196616 | tf_op jit(solution)/shard_map/ppermute | solution.py:38
  (32 other events, 342.8 us)

commit v3 on v1

--- a/solution.py
+++ b/solution.py
@@ -34,14 +34,18 @@
     return second
 
 
+def side_pairs(hop):
+    pairs = []
+    for y in range(NY):
+        for z in range(NZ):
+            pairs.append((plane_index(y, z, 0), plane_index(y, z + hop, 0)))
+            pairs.append((plane_index(y, z, 1), plane_index(y, z - hop, 1)))
+    return pairs
+
+
 def axis_shift(value, axis, hop):
     n = lax.axis_size(axis)
     return lax.ppermute(value, axis, [(i, (i + hop) % n) for i in range(n)])
-
-
-def axis_swap(value, axis, bit):
-    n = lax.axis_size(axis)
-    return lax.ppermute(value, axis, [(i, i ^ bit) for i in range(n)])
 
 
 def stack_blocks(parts):
@@ -217,7 +221,7 @@
             + [vmem] * (len(ids) + len(extra)),
             out_specs=[vmem] * len(out_shape),
             scratch_shapes=([pltpu.VMEM(sums.shape, sums.dtype)] if final else []) + scratch,
-            compiler_params=pltpu.CompilerParams(vmem_limit_bytes=40 << 20),
+            compiler_params=pltpu.CompilerParams(vmem_limit_bytes=(49 if final else 40) << 20),
             cost_estimate=pl.CostEstimate(
                 flops=int(share * 2 * slots * tile * tile * width),
                 bytes_accessed=int(share * slots * tile * (tile + width) * 2),
@@ -238,12 +242,18 @@
     return own + one.astype(f32) + three.astype(f32) + two.astype(f32)
 
 
-def sum_over_devices(gram):
-    gram = gram + axis_swap(gram, "c", 1)
+def sum_over_devices(gram, core):
+    gram = gram + axis_shift(gram, "c", 1)
     for axis in ("x", "y"):
         gram = gram + axis_shift(gram, axis, 1) + axis_shift(gram, axis, 3) + axis_shift(gram, axis, 2)
-    gram = gram + axis_shift(gram, "z", 2) + axis_shift(gram, "z", 6) + axis_shift(gram, "z", 4)
-    return gram + axis_swap(gram, "z", 1)
+    zero = core == 0
+    half = gram.shape[0] // 2
+    side = [lax.ppermute(gram, PLANE, side_pairs(hop)) for hop in (1, 2, 3)]
+    far = axis_shift(jnp.where(zero, gram[:half], gram[half:]), "z", 4)
+    none = jnp.zeros_like(far)
+    far = jnp.concatenate([jnp.where(zero, far, none), jnp.where(zero, none, far)], axis=0)
+    part = side[0] + side[1] + side[2] + far
+    return gram + (part + axis_shift(part, "c", 1))
 
 
 STEP = 16
@@ -305,7 +315,8 @@
         applied = apply_operator(block, tiles, lists, core)
         return applied.astype(jnp.bfloat16), latest, applied
 
-    start = (embedding.astype(jnp.bfloat16), jnp.zeros_like(embedding), embedding)
+    unread = 2.0 * embedding
+    start = (embedding.astype(jnp.bfloat16), jnp.zeros_like(embedding), unread)
     _, first_order, applied = lax.fori_loop(0, 2, apply_once, start)
     second = 2.0 * applied - embedding
     spectral = 1.2661 * embedding - 1.1303 * first_order + 0.2715 * second
@@ -313,7 +324,7 @@
         spectral, spectral, (((0,), (0,)), ((), ())), precision=lax.Precision.HIGHEST
     )
     node_total = embedding.shape[0] * NY * NZ * NC * NX
-    return finish(sum_over_devices(gram), spectral, float(np.sqrt(node_total)))
+    return finish(sum_over_devices(gram, core), spectral, float(np.sqrt(node_total)))
 
 
 def solution(mesh):

time: 200 us -> 198 us (0.990); the launches traced: 197 us -> 198 us
  starting transfers between devices: 107 us -> 112 us
  waiting for transfers between devices: 58.1 us -> 55.9 us
    ppermute x31, starting transfers between devices: 39.8 us -> 45.5 us  [axis_shift(): return lax.ppermute(value, axis, [(i, (i + hop) % n) for i in range(n)])]
    ppermute x31, waiting for transfers between devices: 21.7 us -> 18.6 us  [axis_shift(): return lax.ppermute(value, axis, [(i, (i + hop) % n) for i in range(n)])]
    ppermute x2 -> x3, starting transfers between devices: 5.65 us -> 5.58 us  [sum_over_devices(): side = [lax.ppermute(gram, PLANE, side_pairs(hop)) for hop in (1, 2, 3)]]
  transfers between devices with their start and end apart: 59 -> 60, of which waited for: 28 -> 30; matrix products, arithmetic and copies ran while one was open for 1% -> 1% of each run, Pallas kernels for 6% -> 6%
where the time goes in v3:
time: 198 us
  starting transfers between devices  112 us (57%)
  waiting for transfers between devices  55.9 us (28%)
  Pallas kernels  23.9 us (12%)
  other arithmetic  3.77 us (2%)
    ppermute x26, starting transfers between devices, send(): return lax.ppermute(value, PLANE, pairs)  60.8 us
    ppermute x31, starting transfers between devices, axis_shift(): return lax.ppermute(value, axis, [(i, (i + hop) % n) for i in range(n)])  45.5 us
    ppermute x26, waiting for transfers between devices, send(): return lax.ppermute(value, PLANE, pairs)  34.5 us
    ppermute x31, waiting for transfers between devices, axis_shift(): return lax.ppermute(value, axis, [(i, (i + hop) % n) for i in range(n)])  18.6 us
    pallas_call x4, Pallas kernels, call(): pl.pallas_call(functools.partial(tile_kernel, ids, final), out_shape=out_...  17.2 us
    pallas_call x1, Pallas kernels, finish(): pl.pallas_call(functools.partial(finish_kernel, scale), out_shape=jax.Sha...  6.67 us
    ppermute x3, starting transfers between devices, sum_over_devices(): side = [lax.ppermute(gram, PLANE, side_pairs(hop)) for hop in (1, 2, 3)]  5.58 us
  transfers between devices with their start and end apart: 60, of which 30 were waited for; matrix products, arithmetic and copies ran while one was open for 1% of the time, Pallas kernels for 6%

profile of v3, /device:TPU:1, one launch (start us, length us, event | category | flops | bytes accessed | tf_op | source)
XLA Modules:
  0.0 198.1 jit_solution(5561759805214570596)
XLA Ops:
  1.1 148.0 %while.17 = (s32[]{:T(128)}, bf16[512,128]{1,0:T(8,128)(2,1)S(1)}, f32[512,128]{1,0:T(8,128)}, f32[512,128]{1,0:T(8,128)S(1)}, pred[]{:T(512)}, /*index=5*/s32[2...) while((s32[]{:T(128)}, bf16[512,128]{1,0:T(8,128)(2,1)S(1)}, ...), condition=%wide.region_1.2_spmd.clone, body=%wide.region_0.1_spmd.sunk.clone.sunk | while | flops 1479016448 | bytes 55708520 | solution.py:320
  1.1 3.8 %collective-permute-start = (bf16[512,128]{1,0:T(8,128)(2,1)S(1)}, bf16[512,128]{1,0:T(8,128)(2,1)S(1)}, u32[]{:S(2)}, u32[]{:S(2)}) collective-permute-start(bf16[512,128]{1,0:T(8,128)(2,1)S(1)} %get-tuple-element.275), channel_id=1, source_target_pairs={{0,16},{4,132},{8,24},{12,140},{16,32},{20,148},{24,40},{28,156},{... | collective-permute-start | bytes 393224 | tf_op jit(solution)/shard_map/while/body/eval_jaxpr/ppermute | solution.py:70
  7.3 2.1 %collective-permute-done.1 = bf16[512,128]{1,0:T(8,128)(2,1)S(1)} collective-permute-done((bf16[512,128]{1,0:T(8,128)(2,1)S(1)}, bf16[512,128]{1,0:T(8,128)(2,1)S(1)}, u32[]{:S(2)}, u32[]{:S(2)}) %collective-permute-start.1) | collective-permute-done | bytes 131104 | tf_op jit(solution)/shard_map/while/body/eval_jaxpr/ppermute | solution.py:70
  9.4 1.7 collective-permute-done.2
  11.2 1.7 collective-permute-start.8
  12.9 3.7 %collective-permute-start.3 = (bf16[4,512,128]{2,1,0:T(8,128)(2,1)S(1)}, bf16[4,512,128]{2,1,0:T(8,128)(2,1)S(1)}, u32[]{:S(2)}, u32[]{:S(2)}) collective-permute-start(bf16[4,512,128]{2,1,0:T(8,128)(2,1)S(1)} %select_select_fusion.4.refs_0_), channel_id=1, source_target_pairs={{0,192},{4,60},{8,200},{12,4},{16,208},{20,12},{24,216},{28,20},{3... | collective-permute-start | bytes 1572872 | tf_op jit(solution)/shard_map/while/body/eval_jaxpr/ppermute | solution.py:70
  16.6 4.2 %collective-permute-start.4 = (bf16[512,128]{1,0:T(8,128)(2,1)S(1)}, bf16[512,128]{1,0:T(8,128)(2,1)S(1)}, u32[]{:S(2)}, u32[]{:S(2)}) collective-permute-start(bf16[512,128]{1,0:T(8,128)(2,1)S(1)} %get-tuple-element.275), channel_id=1, source_target_pairs={{0,48},{4,36},{8,56},{12,44},{16,0},{20,52},{24,8},{28,60},{32,16}... | collective-permute-start | bytes 393224 | tf_op jit(solution)/shard_map/while/body/eval_jaxpr/ppermute | solution.py:70
  20.8 7.2 %collective-permute-done.4 = bf16[512,128]{1,0:T(8,128)(2,1)S(1)} collective-permute-done((bf16[512,128]{1,0:T(8,128)(2,1)S(1)}, bf16[512,128]{1,0:T(8,128)(2,1)S(1)}, u32[]{:S(2)}, u32[]{:S(2)}) %collective-permute-start.4) | collective-permute-done | bytes 131104 | tf_op jit(solution)/shard_map/while/body/eval_jaxpr/ppermute | solution.py:70
  29.7 2.3 %collective-permute-start.6 = (bf16[512,128]{1,0:T(8,128)(2,1)S(1)}, bf16[512,128]{1,0:T(8,128)(2,1)S(1)}, u32[]{:S(2)}, u32[]{:S(2)}) collective-permute-start(bf16[512,128]{1,0:T(8,128)(2,1)S(1)} %collective-permute-done.4), channel_id=1, source_target_pairs={{0,56},{4,196},{8,0},{12,204},{16,8},{20,212},{24,16},{28,220},{32... | collective-permute-start | bytes 393224 | tf_op jit(solution)/shard_map/while/body/eval_jaxpr/ppermute | solution.py:70
  32.0 2.9 %collective-permute-start.9 = (bf16[4,512,128]{2,1,0:T(8,128)(2,1)S(1)}, bf16[4,512,128]{2,1,0:T(8,128)(2,1)S(1)}, u32[]{:S(2)}, u32[]{:S(2)}) collective-permute-start(bf16[4,512,128]{2,1,0:T(8,128)(2,1)S(1)} %collective-permute-done.8.refs_2_), channel_id=1, source_target_pairs={{0,64},{4,12},{8,72},{12,20},{16,80},{20,28},{24,88},{28,36},{32,9... | collective-permute-start | bytes 1572872 | tf_op jit(solution)/shard_map/while/body/eval_jaxpr/ppermute | solution.py:70
  35.3 6.5 %collective-permute-start.11 = (bf16[4,512,128]{2,1,0:T(8,128)(2,1)S(1)}, bf16[4,512,128]{2,1,0:T(8,128)(2,1)S(1)}, u32[]{:S(2)}, u32[]{:S(2)}) collective-permute-start(bf16[4,512,128]{2,1,0:T(8,128)(2,1)S(1)} %get-tuple-element.256), channel_id=1, source_target_pairs={{0,192},{4,60},{8,200},{12,4},{16,208},{20,12},{24,216},{28,20},{3... | collective-permute-start | bytes 1572872 | tf_op jit(solution)/shard_map/while/body/eval_jaxpr/ppermute | solution.py:70
  43.6 4.4 %collective-permute-done.11.refs_5_ = bf16[4,512,128]{2,1,0:T(8,128)(2,1)S(1)} collective-permute-done((bf16[4,512,128]{2,1,0:T(8,128)(2,1)S(1)}, bf16[4,512,128]{2,1,0:T(8,128)(2,1)S(1)}, u32[]{:S(2)}, u32[]{:S(2)}) %collective-permute-start.11) | collective-permute-done | bytes 524320 | tf_op jit(solution)/shard_map/while/body/eval_jaxpr/ppermute | solution.py:70
  48.0 3.4 %collective-permute-start.12 = (bf16[4,512,128]{2,1,0:T(8,128)(2,1)S(1)}, bf16[4,512,128]{2,1,0:T(8,128)(2,1)S(1)}, u32[]{:S(2)}, u32[]{:S(2)}) collective-permute-start(bf16[4,512,128]{2,1,0:T(8,128)(2,1)S(1)} %collective-permute-done.11.refs_5_), channel_id=1, source_target_pairs={{0,192},{4,60},{8,200},{12,4},{16,208},{20,12},{24,216},{28,20},{3... | collective-permute-start | bytes 1572872 | tf_op jit(solution)/shard_map/while/body/eval_jaxpr/ppermute | solution.py:70
  53.1 1.5 collective-permute-start.13
  54.6 2.9 %collective-permute-done.12.refs_1_ = bf16[4,512,128]{2,1,0:T(8,128)(2,1)S(1)} collective-permute-done((bf16[4,512,128]{2,1,0:T(8,128)(2,1)S(1)}, bf16[4,512,128]{2,1,0:T(8,128)(2,1)S(1)}, u32[]{:S(2)}, u32[]{:S(2)}) %collective-permute-start.12) | collective-permute-done | bytes 524320 | tf_op jit(solution)/shard_map/while/body/eval_jaxpr/ppermute | solution.py:70
  57.5 5.5 %eval_jaxpr.4.refs_4_ = f32[5,512,128]{2,1,0:T(8,128)S(1)} custom-call(s32[22]{0:T(128)} %get-tuple-element.290.rows, s32[22]{0:T(128)} %get-tuple-element.291.cols, s32[1]{0:T(128)} %get-tuple-element.292.counts, s32[64]{0:T(128)} %get-tuple-element.295.table, bf16[22,512,512]{2,1,0:T(8,128)(2,1)} %get-tuple-element.293.tiles, ...), custom_call_target="tpu_custom_call" | custom-call | flops 1107296256 | bytes 10813440 | tf_op jit(solution)/shard_map/while/body/eval_jaxpr/pallas_call | solution.py:216
  63.1 3.1 %eval_jaxpr.5 = (f32[512,128]{1,0:T(8,128)S(1)}, bf16[512,128]{1,0:T(8,128)(2,1)S(1)}, bf16[512,128]{1,0:T(8,128)(2,1)S(1)}, bf16[512,128]{1,0:T(8,128)(2,1)S(1)}) custom-call(s32[22]{0:T(128)S(1)} %copy-done.2, s32[22]{0:T(128)S(1)} %copy-done.3, s32[1]{0:T(128)} %get-tuple-element.292.counts, s32[64]{0:T(128)S(1)} %copy-done.4, ...), custom_call_target="tpu_custom_call" | custom-call | flops 369098752 | bytes 3604480 | tf_op jit(solution)/shard_map/while/body/eval_jaxpr/pallas_call | solution.py:216
  66.3 3.7 %collective-permute-start.22 = (bf16[512,128]{1,0:T(8,128)(2,1)S(1)}, bf16[512,128]{1,0:T(8,128)(2,1)S(1)}, u32[]{:S(2)}, u32[]{:S(2)}) collective-permute-start(bf16[512,128]{1,0:T(8,128)(2,1)S(1)} %get-tuple-element.258), channel_id=1, source_target_pairs={{0,3},{1,0},{2,1},{3,2},{4,7},{5,4},{6,5},{7,6},{8,11},{9,8},{10,9... | collective-permute-start | bytes 393224 | tf_op jit(solution)/shard_map/while/body/eval_jaxpr/ppermute | solution.py:48
  72.1 2.9 %collective-permute-done.23 = bf16[512,128]{1,0:T(8,128)(2,1)S(1)} collective-permute-done((bf16[512,128]{1,0:T(8,128)(2,1)S(1)}, bf16[512,128]{1,0:T(8,128)(2,1)S(1)}, u32[]{:S(2)}, u32[]{:S(2)}) %collective-permute-start.23) | collective-permute-done | bytes 131104 | tf_op jit(solution)/shard_map/while/body/eval_jaxpr/ppermute | solution.py:48
  75.1 2.5 %collective-permute-start = (bf16[512,128]{1,0:T(8,128)(2,1)S(1)}, bf16[512,128]{1,0:T(8,128)(2,1)S(1)}, u32[]{:S(2)}, u32[]{:S(2)}) collective-permute-start(bf16[512,128]{1,0:T(8,128)(2,1)S(1)} %get-tuple-element.275), channel_id=1, source_target_pairs={{0,16},{4,132},{8,24},{12,140},{16,32},{20,148},{24,40},{28,156},{... | collective-permute-start | bytes 393224 | tf_op jit(solution)/shard_map/while/body/eval_jaxpr/ppermute | solution.py:70
  77.6 2.3 %collective-permute-start.1 = (bf16[512,128]{1,0:T(8,128)(2,1)S(1)}, bf16[512,128]{1,0:T(8,128)(2,1)S(1)}, u32[]{:S(2)}, u32[]{:S(2)}) collective-permute-start(bf16[512,128]{1,0:T(8,128)(2,1)S(1)} %get-tuple-element.275), channel_id=1, source_target_pairs={{0,56},{4,196},{8,0},{12,204},{16,8},{20,212},{24,16},{28,220},{32... | collective-permute-start | bytes 393224 | tf_op jit(solution)/shard_map/while/body/eval_jaxpr/ppermute | solution.py:70
  80.5 4.0 %collective-permute-done.1 = bf16[512,128]{1,0:T(8,128)(2,1)S(1)} collective-permute-done((bf16[512,128]{1,0:T(8,128)(2,1)S(1)}, bf16[512,128]{1,0:T(8,128)(2,1)S(1)}, u32[]{:S(2)}, u32[]{:S(2)}) %collective-permute-start.1) | collective-permute-done | bytes 131104 | tf_op jit(solution)/shard_map/while/body/eval_jaxpr/ppermute | solution.py:70
  86.8 2.2 %collective-permute-start.3 = (bf16[4,512,128]{2,1,0:T(8,128)(2,1)S(1)}, bf16[4,512,128]{2,1,0:T(8,128)(2,1)S(1)}, u32[]{:S(2)}, u32[]{:S(2)}) collective-permute-start(bf16[4,512,128]{2,1,0:T(8,128)(2,1)S(1)} %select_select_fusion.4.refs_0_), channel_id=1, source_target_pairs={{0,192},{4,60},{8,200},{12,4},{16,208},{20,12},{24,216},{28,20},{3... | collective-permute-start | bytes 1572872 | tf_op jit(solution)/shard_map/while/body/eval_jaxpr/ppermute | solution.py:70
  89.0 4.0 %collective-permute-start.4 = (bf16[512,128]{1,0:T(8,128)(2,1)S(1)}, bf16[512,128]{1,0:T(8,128)(2,1)S(1)}, u32[]{:S(2)}, u32[]{:S(2)}) collective-permute-start(bf16[512,128]{1,0:T(8,128)(2,1)S(1)} %get-tuple-element.275), channel_id=1, source_target_pairs={{0,48},{4,36},{8,56},{12,44},{16,0},{20,52},{24,8},{28,60},{32,16}... | collective-permute-start | bytes 393224 | tf_op jit(solution)/shard_map/while/body/eval_jaxpr/ppermute | solution.py:70
  93.0 5.5 %collective-permute-done.4 = bf16[512,128]{1,0:T(8,128)(2,1)S(1)} collective-permute-done((bf16[512,128]{1,0:T(8,128)(2,1)S(1)}, bf16[512,128]{1,0:T(8,128)(2,1)S(1)}, u32[]{:S(2)}, u32[]{:S(2)}) %collective-permute-start.4) | collective-permute-done | bytes 131104 | tf_op jit(solution)/shard_map/while/body/eval_jaxpr/ppermute | solution.py:70
  102.2 2.2 %collective-permute-start.9 = (bf16[4,512,128]{2,1,0:T(8,128)(2,1)S(1)}, bf16[4,512,128]{2,1,0:T(8,128)(2,1)S(1)}, u32[]{:S(2)}, u32[]{:S(2)}) collective-permute-start(bf16[4,512,128]{2,1,0:T(8,128)(2,1)S(1)} %collective-permute-done.8.refs_2_), channel_id=1, source_target_pairs={{0,64},{4,12},{8,72},{12,20},{16,80},{20,28},{24,88},{28,36},{32,9... | collective-permute-start | bytes 1572872 | tf_op jit(solution)/shard_map/while/body/eval_jaxpr/ppermute | solution.py:70
  105.6 6.6 %collective-permute-start.11 = (bf16[4,512,128]{2,1,0:T(8,128)(2,1)S(1)}, bf16[4,512,128]{2,1,0:T(8,128)(2,1)S(1)}, u32[]{:S(2)}, u32[]{:S(2)}) collective-permute-start(bf16[4,512,128]{2,1,0:T(8,128)(2,1)S(1)} %get-tuple-element.256), channel_id=1, source_target_pairs={{0,192},{4,60},{8,200},{12,4},{16,208},{20,12},{24,216},{28,20},{3... | collective-permute-start | bytes 1572872 | tf_op jit(solution)/shard_map/while/body/eval_jaxpr/ppermute | solution.py:70
  112.2 3.4 %collective-permute-start.15 = (bf16[4,512,128]{2,1,0:T(8,128)(2,1)S(1)}, bf16[4,512,128]{2,1,0:T(8,128)(2,1)S(1)}, u32[]{:S(2)}, u32[]{:S(2)}) collective-permute-start(bf16[4,512,128]{2,1,0:T(8,128)(2,1)S(1)} %select_select_fusion.4.refs_0_), channel_id=1, source_target_pairs={{0,4},{4,0},{1,5},{5,1},{2,6},{6,2},{3,7},{7,3},{8,12},{12,8},{9,1... | collective-permute-start | bytes 1572872 | tf_op jit(solution)/shard_map/while/body/eval_jaxpr/ppermute | solution.py:48
  118.3 3.1 %collective-permute-start.12 = (bf16[4,512,128]{2,1,0:T(8,128)(2,1)S(1)}, bf16[4,512,128]{2,1,0:T(8,128)(2,1)S(1)}, u32[]{:S(2)}, u32[]{:S(2)}) collective-permute-start(bf16[4,512,128]{2,1,0:T(8,128)(2,1)S(1)} %collective-permute-done.11.refs_5_), channel_id=1, source_target_pairs={{0,192},{4,60},{8,200},{12,4},{16,208},{20,12},{24,216},{28,20},{3... | collective-permute-start | bytes 1572872 | tf_op jit(solution)/shard_map/while/body/eval_jaxpr/ppermute | solution.py:70
  121.4 4.5 %collective-permute-start.18 = (bf16[4,512,128]{2,1,0:T(8,128)(2,1)S(1)}, bf16[4,512,128]{2,1,0:T(8,128)(2,1)S(1)}, u32[]{:S(2)}, u32[]{:S(2)}) collective-permute-start(bf16[4,512,128]{2,1,0:T(8,128)(2,1)S(1)} %collective-permute-done.3.refs_3_), channel_id=1, source_target_pairs={{0,4},{4,0},{1,5},{5,1},{2,6},{6,2},{3,7},{7,3},{8,12},{12,8},{9,1... | collective-permute-start | bytes 1572872 | tf_op jit(solution)/shard_map/while/body/eval_jaxpr/ppermute | solution.py:48
  126.5 3.8 %collective-permute-start.13 = (bf16[4,512,128]{2,1,0:T(8,128)(2,1)S(1)}, bf16[4,512,128]{2,1,0:T(8,128)(2,1)S(1)}, u32[]{:S(2)}, u32[]{:S(2)}) collective-permute-start(bf16[4,512,128]{2,1,0:T(8,128)(2,1)S(1)} %collective-permute-done.10.refs_0_), channel_id=1, source_target_pairs={{0,4},{4,0},{1,5},{5,1},{2,6},{6,2},{3,7},{7,3},{8,12},{12,8},{9,1... | collective-permute-start | bytes 1572872 | tf_op jit(solution)/shard_map/while/body/eval_jaxpr/ppermute | solution.py:48
  130.3 2.3 %collective-permute-start.14 = (bf16[4,512,128]{2,1,0:T(8,128)(2,1)S(1)}, bf16[4,512,128]{2,1,0:T(8,128)(2,1)S(1)}, u32[]{:S(2)}, u32[]{:S(2)}) collective-permute-start(bf16[4,512,128]{2,1,0:T(8,128)(2,1)S(1)} %collective-permute-done.12.refs_1_), channel_id=1, source_target_pairs={{0,4},{4,0},{1,5},{5,1},{2,6},{6,2},{3,7},{7,3},{8,12},{12,8},{9,1... | collective-permute-start | bytes 1572872 | tf_op jit(solution)/shard_map/while/body/eval_jaxpr/ppermute | solution.py:48
  132.6 5.5 %eval_jaxpr.4.refs_4_ = f32[5,512,128]{2,1,0:T(8,128)S(1)} custom-call(s32[22]{0:T(128)} %get-tuple-element.290.rows, s32[22]{0:T(128)} %get-tuple-element.291.cols, s32[1]{0:T(128)} %get-tuple-element.292.counts, s32[64]{0:T(128)} %get-tuple-element.295.table, bf16[22,512,512]{2,1,0:T(8,128)(2,1)} %get-tuple-element.293.tiles, ...), custom_call_target="tpu_custom_call" | custom-call | flops 1107296256 | bytes 10813440 | tf_op jit(solution)/shard_map/while/body/eval_jaxpr/pallas_call | solution.py:216
  138.2 3.1 %eval_jaxpr.5 = (f32[512,128]{1,0:T(8,128)S(1)}, bf16[512,128]{1,0:T(8,128)(2,1)S(1)}, bf16[512,128]{1,0:T(8,128)(2,1)S(1)}, bf16[512,128]{1,0:T(8,128)(2,1)S(1)}) custom-call(s32[22]{0:T(128)S(1)} %copy-done.2, s32[22]{0:T(128)S(1)} %copy-done.3, s32[1]{0:T(128)} %get-tuple-element.292.counts, s32[64]{0:T(128)S(1)} %copy-done.4, ...), custom_call_target="tpu_custom_call" | custom-call | flops 369098752 | bytes 3604480 | tf_op jit(solution)/shard_map/while/body/eval_jaxpr/pallas_call | solution.py:216
  141.4 2.4 %collective-permute-start.22 = (bf16[512,128]{1,0:T(8,128)(2,1)S(1)}, bf16[512,128]{1,0:T(8,128)(2,1)S(1)}, u32[]{:S(2)}, u32[]{:S(2)}) collective-permute-start(bf16[512,128]{1,0:T(8,128)(2,1)S(1)} %get-tuple-element.258), channel_id=1, source_target_pairs={{0,3},{1,0},{2,1},{3,2},{4,7},{5,4},{6,5},{7,6},{8,11},{9,8},{10,9... | collective-permute-start | bytes 393224 | tf_op jit(solution)/shard_map/while/body/eval_jaxpr/ppermute | solution.py:48
  144.5 2.2 %collective-permute-done.21 = bf16[512,128]{1,0:T(8,128)(2,1)S(1)} collective-permute-done((bf16[512,128]{1,0:T(8,128)(2,1)S(1)}, bf16[512,128]{1,0:T(8,128)(2,1)S(1)}, u32[]{:S(2)}, u32[]{:S(2)}) %collective-permute-start.21) | collective-permute-done | bytes 131104 | tf_op jit(solution)/shard_map/while/body/eval_jaxpr/ppermute | solution.py:48
  146.7 2.1 %collective-permute-done.23 = bf16[512,128]{1,0:T(8,128)(2,1)S(1)} collective-permute-done((bf16[512,128]{1,0:T(8,128)(2,1)S(1)}, bf16[512,128]{1,0:T(8,128)(2,1)S(1)}, u32[]{:S(2)}, u32[]{:S(2)}) %collective-permute-start.23) | collective-permute-done | bytes 131104 | tf_op jit(solution)/shard_map/while/body/eval_jaxpr/ppermute | solution.py:48
  150.7 3.8 %collective-permute-start.24 = (f32[128,128]{1,0:T(8,128)S(1)}, f32[128,128]{1,0:T(8,128)S(1)}, u32[]{:S(2)}, u32[]{:S(2)}) collective-permute-start(f32[128,128]{1,0:T(8,128)S(1)} %fusion.1), channel_id=1, source_target_pairs={{0,4},{4,0},{1,5},{5,1},{2,6},{6,2},{3,7},{7,3},{8,12},{12,8},{9,1... | collective-permute-start | bytes 196616 | tf_op jit(solution)/shard_map/ppermute | solution.py:48
  155.5 2.7 %collective-permute-start.26 = (f32[128,128]{1,0:T(8,128)S(1)}, f32[128,128]{1,0:T(8,128)S(1)}, u32[]{:S(2)}, u32[]{:S(2)}) collective-permute-start(f32[128,128]{1,0:T(8,128)S(1)} %add.60), channel_id=1, source_target_pairs={{0,3},{1,0},{2,1},{3,2},{4,7},{5,4},{6,5},{7,6},{8,11},{9,8},{10,9... | collective-permute-start | bytes 196616 | tf_op jit(solution)/shard_map/ppermute | solution.py:48
  158.3 1.5 collective-permute-done.25
  160.2 2.5 %collective-permute-done.27 = f32[128,128]{1,0:T(8,128)S(1)} collective-permute-done((f32[128,128]{1,0:T(8,128)S(1)}, f32[128,128]{1,0:T(8,128)S(1)}, u32[]{:S(2)}, u32[]{:S(2)}) %collective-permute-start.27) | collective-permute-done | bytes 65568 | tf_op jit(solution)/shard_map/ppermute | solution.py:48
  162.9 3.7 %collective-permute-start.29 = (f32[128,128]{1,0:T(8,128)S(1)}, f32[128,128]{1,0:T(8,128)S(1)}, u32[]{:S(2)}, u32[]{:S(2)}) collective-permute-start(f32[128,128]{1,0:T(8,128)S(1)} %add_add_fusion.2), channel_id=1, source_target_pairs={{0,192},{64,0},{128,64},{192,128},{1,193},{65,1},{129,65},{193,129... | collective-permute-start | bytes 196616 | tf_op jit(solution)/shard_map/ppermute | solution.py:48
  168.2 3.1 %collective-permute-done.30 = f32[128,128]{1,0:T(8,128)S(1)} collective-permute-done((f32[128,128]{1,0:T(8,128)S(1)}, f32[128,128]{1,0:T(8,128)S(1)}, u32[]{:S(2)}, u32[]{:S(2)}) %collective-permute-start.30) | collective-permute-done | bytes 65568 | tf_op jit(solution)/shard_map/ppermute | solution.py:48
  171.3 3.4 %collective-permute-start.34 = (f32[64,128]{1,0:T(8,128)S(1)}, f32[64,128]{1,0:T(8,128)S(1)}, u32[]{:S(2)}, u32[]{:S(2)}) collective-permute-start(f32[64,128]{1,0:T(8,128)S(1)} %slice_select_fusion), channel_id=1, source_target_pairs={{0,32},{8,40},{16,48},{24,56},{32,0},{40,8},{48,16},{56,24},{1,33}... | collective-permute-start | bytes 98312 | tf_op jit(solution)/shard_map/ppermute | solution.py:48
  175.1 3.0 %collective-permute-start.32 = (f32[128,128]{1,0:T(8,128)S(1)}, f32[128,128]{1,0:T(8,128)S(1)}, u32[]{:S(2)}, u32[]{:S(2)}) collective-permute-start(f32[128,128]{1,0:T(8,128)S(1)} %add_add_fusion.1), channel_id=1, source_target_pairs={{0,16},{4,52},{8,24},{12,60},{16,32},{20,4},{24,40},{28,12},{32,48... | collective-permute-start | bytes 196616 | tf_op jit(solution)/shard_map/ppermute | solution.py:251
  178.1 2.3 %collective-permute-start.33 = (f32[128,128]{1,0:T(8,128)S(1)}, f32[128,128]{1,0:T(8,128)S(1)}, u32[]{:S(2)}, u32[]{:S(2)}) collective-permute-start(f32[128,128]{1,0:T(8,128)S(1)} %add_add_fusion.1), channel_id=1, source_target_pairs={{0,24},{4,44},{8,32},{12,52},{16,40},{20,60},{24,48},{28,4},{32,56... | collective-permute-start | bytes 196616 | tf_op jit(solution)/shard_map/ppermute | solution.py:251
  183.2 6.7 %collective-permute-start.35 = (f32[128,128]{1,0:T(8,128)S(1)}, f32[128,128]{1,0:T(8,128)S(1)}, u32[]{:S(2)}, u32[]{:S(2)}) collective-permute-start(f32[128,128]{1,0:T(8,128)S(1)} %maximum_add_fusion), channel_id=1, source_target_pairs={{0,4},{4,0},{1,5},{5,1},{2,6},{6,2},{3,7},{7,3},{8,12},{12,8},{9,1... | collective-permute-start | bytes 196616 | tf_op jit(solution)/shard_map/ppermute | solution.py:48
  191.4 6.7 %orthonormalize.1 = f32[512,128]{1,0:T(8,128)} custom-call(f32[128,128]{1,0:T(8,128)} %add_add_fusion.gram_ref, f32[512,128]{1,0:T(8,128)} %copy-done), custom_call_target="tpu_custom_call" | custom-call | tf_op jit(solution)/shard_map/orthonormalize/pallas_call | solution.py:301
  (121 shorter events, 32.8 us)
Async XLA Ops:
  1.1 6.2 %collective-permute-start = (bf16[512,128]{1,0:T(8,128)(2,1)S(1)}, bf16[512,128]{1,0:T(8,128)(2,1)S(1)}, u32[]{:S(2)}, u32[]{:S(2)}) collective-permute-start(bf16[512,128]{1,0:T(8,128)(2,1)S(1)} %get-tuple-element.275), channel_id=1, source_target_pairs={{0,16},{4,132},{8,24},{12,140},{16,32},{20,148},{24,40},{28,156},{... | collective-permute-start | bytes 393224 | tf_op jit(solution)/shard_map/while/body/eval_jaxpr/ppermute | solution.py:70
  5.7 5.3 %collective-permute-start.2 = (bf16[512,128]{1,0:T(8,128)(2,1)S(1)}, bf16[512,128]{1,0:T(8,128)(2,1)S(1)}, u32[]{:S(2)}, u32[]{:S(2)}) collective-permute-start(bf16[512,128]{1,0:T(8,128)(2,1)S(1)} %get-tuple-element.275), channel_id=1, source_target_pairs={{0,8},{4,68},{8,16},{12,76},{16,24},{20,84},{24,32},{28,92},{32,40... | collective-permute-start | bytes 393224 | tf_op jit(solution)/shard_map/while/body/eval_jaxpr/ppermute | solution.py:70
  11.2 20.8 %collective-permute-start.8 = (bf16[4,512,128]{2,1,0:T(8,128)(2,1)S(1)}, bf16[4,512,128]{2,1,0:T(8,128)(2,1)S(1)}, u32[]{:S(2)}, u32[]{:S(2)}) collective-permute-start(bf16[4,512,128]{2,1,0:T(8,128)(2,1)S(1)} %select_select_fusion.4.refs_0_), channel_id=1, source_target_pairs={{0,64},{4,12},{8,72},{12,20},{16,80},{20,28},{24,88},{28,36},{32,9... | collective-permute-start | bytes 1572872 | tf_op jit(solution)/shard_map/while/body/eval_jaxpr/ppermute | solution.py:70
  12.9 22.3 %collective-permute-start.3 = (bf16[4,512,128]{2,1,0:T(8,128)(2,1)S(1)}, bf16[4,512,128]{2,1,0:T(8,128)(2,1)S(1)}, u32[]{:S(2)}, u32[]{:S(2)}) collective-permute-start(bf16[4,512,128]{2,1,0:T(8,128)(2,1)S(1)} %select_select_fusion.4.refs_0_), channel_id=1, source_target_pairs={{0,192},{4,60},{8,200},{12,4},{16,208},{20,12},{24,216},{28,20},{3... | collective-permute-start | bytes 1572872 | tf_op jit(solution)/shard_map/while/body/eval_jaxpr/ppermute | solution.py:70
  16.6 11.4 %collective-permute-start.4 = (bf16[512,128]{1,0:T(8,128)(2,1)S(1)}, bf16[512,128]{1,0:T(8,128)(2,1)S(1)}, u32[]{:S(2)}, u32[]{:S(2)}) collective-permute-start(bf16[512,128]{1,0:T(8,128)(2,1)S(1)} %get-tuple-element.275), channel_id=1, source_target_pairs={{0,48},{4,36},{8,56},{12,44},{16,0},{20,52},{24,8},{28,60},{32,16}... | collective-permute-start | bytes 393224 | tf_op jit(solution)/shard_map/while/body/eval_jaxpr/ppermute | solution.py:70
  28.1 6.8 %collective-permute-start.5 = (bf16[512,128]{1,0:T(8,128)(2,1)S(1)}, bf16[512,128]{1,0:T(8,128)(2,1)S(1)}, u32[]{:S(2)}, u32[]{:S(2)}) collective-permute-start(bf16[512,128]{1,0:T(8,128)(2,1)S(1)} %broadcast_select_fusion.8), channel_id=1, source_target_pairs={{0,16},{4,132},{8,24},{12,140},{16,32},{20,148},{24,40},{28,156},{... | collective-permute-start | bytes 393224 | tf_op jit(solution)/shard_map/while/body/eval_jaxpr/ppermute | solution.py:70
  29.3 5.8 %collective-permute-start.7 = (bf16[512,128]{1,0:T(8,128)(2,1)S(1)}, bf16[512,128]{1,0:T(8,128)(2,1)S(1)}, u32[]{:S(2)}, u32[]{:S(2)}) collective-permute-start(bf16[512,128]{1,0:T(8,128)(2,1)S(1)} %broadcast_select_fusion.8), channel_id=1, source_target_pairs={{0,8},{4,68},{8,16},{12,76},{16,24},{20,84},{24,32},{28,92},{32,40... | collective-permute-start | bytes 393224 | tf_op jit(solution)/shard_map/while/body/eval_jaxpr/ppermute | solution.py:70
  29.7 5.5 %collective-permute-start.6 = (bf16[512,128]{1,0:T(8,128)(2,1)S(1)}, bf16[512,128]{1,0:T(8,128)(2,1)S(1)}, u32[]{:S(2)}, u32[]{:S(2)}) collective-permute-start(bf16[512,128]{1,0:T(8,128)(2,1)S(1)} %collective-permute-done.4), channel_id=1, source_target_pairs={{0,56},{4,196},{8,0},{12,204},{16,8},{20,212},{24,16},{28,220},{32... | collective-permute-start | bytes 393224 | tf_op jit(solution)/shard_map/while/body/eval_jaxpr/ppermute | solution.py:70
  32.0 11.4 %collective-permute-start.9 = (bf16[4,512,128]{2,1,0:T(8,128)(2,1)S(1)}, bf16[4,512,128]{2,1,0:T(8,128)(2,1)S(1)}, u32[]{:S(2)}, u32[]{:S(2)}) collective-permute-start(bf16[4,512,128]{2,1,0:T(8,128)(2,1)S(1)} %collective-permute-done.8.refs_2_), channel_id=1, source_target_pairs={{0,64},{4,12},{8,72},{12,20},{16,80},{20,28},{24,88},{28,36},{32,9... | collective-permute-start | bytes 1572872 | tf_op jit(solution)/shard_map/while/body/eval_jaxpr/ppermute | solution.py:70
  35.3 12.6 %collective-permute-start.11 = (bf16[4,512,128]{2,1,0:T(8,128)(2,1)S(1)}, bf16[4,512,128]{2,1,0:T(8,128)(2,1)S(1)}, u32[]{:S(2)}, u32[]{:S(2)}) collective-permute-start(bf16[4,512,128]{2,1,0:T(8,128)(2,1)S(1)} %get-tuple-element.256), channel_id=1, source_target_pairs={{0,192},{4,60},{8,200},{12,4},{16,208},{20,12},{24,216},{28,20},{3... | collective-permute-start | bytes 1572872 | tf_op jit(solution)/shard_map/while/body/eval_jaxpr/ppermute | solution.py:70
  41.8 9.5 %collective-permute-start.15 = (bf16[4,512,128]{2,1,0:T(8,128)(2,1)S(1)}, bf16[4,512,128]{2,1,0:T(8,128)(2,1)S(1)}, u32[]{:S(2)}, u32[]{:S(2)}) collective-permute-start(bf16[4,512,128]{2,1,0:T(8,128)(2,1)S(1)} %select_select_fusion.4.refs_0_), channel_id=1, source_target_pairs={{0,4},{4,0},{1,5},{5,1},{2,6},{6,2},{3,7},{7,3},{8,12},{12,8},{9,1... | collective-permute-start | bytes 1572872 | tf_op jit(solution)/shard_map/while/body/eval_jaxpr/ppermute | solution.py:48
  41.8 9.5 %collective-permute-start.16 = (bf16[4,512,128]{2,1,0:T(8,128)(2,1)S(1)}, bf16[4,512,128]{2,1,0:T(8,128)(2,1)S(1)}, u32[]{:S(2)}, u32[]{:S(2)}) collective-permute-start(bf16[4,512,128]{2,1,0:T(8,128)(2,1)S(1)} %get-tuple-element.255.refs_1_), channel_id=1, source_target_pairs={{0,4},{4,0},{1,5},{5,1},{2,6},{6,2},{3,7},{7,3},{8,12},{12,8},{9,1... | collective-permute-start | bytes 1572872 | tf_op jit(solution)/shard_map/while/body/eval_jaxpr/ppermute | solution.py:48
  42.3 9.5 %collective-permute-start.17 = (bf16[4,512,128]{2,1,0:T(8,128)(2,1)S(1)}, bf16[4,512,128]{2,1,0:T(8,128)(2,1)S(1)}, u32[]{:S(2)}, u32[]{:S(2)}) collective-permute-start(bf16[4,512,128]{2,1,0:T(8,128)(2,1)S(1)} %collective-permute-done.8.refs_2_), channel_id=1, source_target_pairs={{0,4},{4,0},{1,5},{5,1},{2,6},{6,2},{3,7},{7,3},{8,12},{12,8},{9,1... | collective-permute-start | bytes 1572872 | tf_op jit(solution)/shard_map/while/body/eval_jaxpr/ppermute | solution.py:48
  43.5 9.6 %collective-permute-start.10 = (bf16[4,512,128]{2,1,0:T(8,128)(2,1)S(1)}, bf16[4,512,128]{2,1,0:T(8,128)(2,1)S(1)}, u32[]{:S(2)}, u32[]{:S(2)}) collective-permute-start(bf16[4,512,128]{2,1,0:T(8,128)(2,1)S(1)} %broadcast_select_fusion.10), channel_id=1, source_target_pairs={{0,64},{4,12},{8,72},{12,20},{16,80},{20,28},{24,88},{28,36},{32,9... | collective-permute-start | bytes 1572872 | tf_op jit(solution)/shard_map/while/body/eval_jaxpr/ppermute | solution.py:70
  48.0 9.5 %collective-permute-start.12 = (bf16[4,512,128]{2,1,0:T(8,128)(2,1)S(1)}, bf16[4,512,128]{2,1,0:T(8,128)(2,1)S(1)}, u32[]{:S(2)}, u32[]{:S(2)}) collective-permute-start(bf16[4,512,128]{2,1,0:T(8,128)(2,1)S(1)} %collective-permute-done.11.refs_5_), channel_id=1, source_target_pairs={{0,192},{4,60},{8,200},{12,4},{16,208},{20,12},{24,216},{28,20},{3... | collective-permute-start | bytes 1572872 | tf_op jit(solution)/shard_map/while/body/eval_jaxpr/ppermute | solution.py:70
  51.4 6.1 %collective-permute-start.18 = (bf16[4,512,128]{2,1,0:T(8,128)(2,1)S(1)}, bf16[4,512,128]{2,1,0:T(8,128)(2,1)S(1)}, u32[]{:S(2)}, u32[]{:S(2)}) collective-permute-start(bf16[4,512,128]{2,1,0:T(8,128)(2,1)S(1)} %collective-permute-done.3.refs_3_), channel_id=1, source_target_pairs={{0,4},{4,0},{1,5},{5,1},{2,6},{6,2},{3,7},{7,3},{8,12},{12,8},{9,1... | collective-permute-start | bytes 1572872 | tf_op jit(solution)/shard_map/while/body/eval_jaxpr/ppermute | solution.py:48
  51.4 6.1 %collective-permute-start.20 = (bf16[4,512,128]{2,1,0:T(8,128)(2,1)S(1)}, bf16[4,512,128]{2,1,0:T(8,128)(2,1)S(1)}, u32[]{:S(2)}, u32[]{:S(2)}) collective-permute-start(bf16[4,512,128]{2,1,0:T(8,128)(2,1)S(1)} %collective-permute-done.11.refs_5_), channel_id=1, source_target_pairs={{0,4},{4,0},{1,5},{5,1},{2,6},{6,2},{3,7},{7,3},{8,12},{12,8},{9,1... | collective-permute-start | bytes 1572872 | tf_op jit(solution)/shard_map/while/body/eval_jaxpr/ppermute | solution.py:48
  51.9 5.6 %collective-permute-start.19 = (bf16[4,512,128]{2,1,0:T(8,128)(2,1)S(1)}, bf16[4,512,128]{2,1,0:T(8,128)(2,1)S(1)}, u32[]{:S(2)}, u32[]{:S(2)}) collective-permute-start(bf16[4,512,128]{2,1,0:T(8,128)(2,1)S(1)} %collective-permute-done.9.refs_4_), channel_id=1, source_target_pairs={{0,4},{4,0},{1,5},{5,1},{2,6},{6,2},{3,7},{7,3},{8,12},{12,8},{9,1... | collective-permute-start | bytes 1572872 | tf_op jit(solution)/shard_map/while/body/eval_jaxpr/ppermute | solution.py:48
  53.1 10.0 %collective-permute-start.13 = (bf16[4,512,128]{2,1,0:T(8,128)(2,1)S(1)}, bf16[4,512,128]{2,1,0:T(8,128)(2,1)S(1)}, u32[]{:S(2)}, u32[]{:S(2)}) collective-permute-start(bf16[4,512,128]{2,1,0:T(8,128)(2,1)S(1)} %collective-permute-done.10.refs_0_), channel_id=1, source_target_pairs={{0,4},{4,0},{1,5},{5,1},{2,6},{6,2},{3,7},{7,3},{8,12},{12,8},{9,1... | collective-permute-start | bytes 1572872 | tf_op jit(solution)/shard_map/while/body/eval_jaxpr/ppermute | solution.py:48
  57.5 5.5 %collective-permute-start.14 = (bf16[4,512,128]{2,1,0:T(8,128)(2,1)S(1)}, bf16[4,512,128]{2,1,0:T(8,128)(2,1)S(1)}, u32[]{:S(2)}, u32[]{:S(2)}) collective-permute-start(bf16[4,512,128]{2,1,0:T(8,128)(2,1)S(1)} %collective-permute-done.12.refs_1_), channel_id=1, source_target_pairs={{0,4},{4,0},{1,5},{5,1},{2,6},{6,2},{3,7},{7,3},{8,12},{12,8},{9,1... | collective-permute-start | bytes 1572872 | tf_op jit(solution)/shard_map/while/body/eval_jaxpr/ppermute | solution.py:48
  66.2 5.4 %collective-permute-start.21 = (bf16[512,128]{1,0:T(8,128)(2,1)S(1)}, bf16[512,128]{1,0:T(8,128)(2,1)S(1)}, u32[]{:S(2)}, u32[]{:S(2)}) collective-permute-start(bf16[512,128]{1,0:T(8,128)(2,1)S(1)} %get-tuple-element.257), channel_id=1, source_target_pairs={{0,2},{1,3},{2,0},{3,1},{4,6},{5,7},{6,4},{7,5},{8,10},{9,11},{10,... | collective-permute-start | bytes 393224 | tf_op jit(solution)/shard_map/while/body/eval_jaxpr/ppermute | solution.py:48
  66.3 5.7 %collective-permute-start.22 = (bf16[512,128]{1,0:T(8,128)(2,1)S(1)}, bf16[512,128]{1,0:T(8,128)(2,1)S(1)}, u32[]{:S(2)}, u32[]{:S(2)}) collective-permute-start(bf16[512,128]{1,0:T(8,128)(2,1)S(1)} %get-tuple-element.258), channel_id=1, source_target_pairs={{0,3},{1,0},{2,1},{3,2},{4,7},{5,4},{6,5},{7,6},{8,11},{9,8},{10,9... | collective-permute-start | bytes 393224 | tf_op jit(solution)/shard_map/while/body/eval_jaxpr/ppermute | solution.py:48
  75.1 5.4 %collective-permute-start = (bf16[512,128]{1,0:T(8,128)(2,1)S(1)}, bf16[512,128]{1,0:T(8,128)(2,1)S(1)}, u32[]{:S(2)}, u32[]{:S(2)}) collective-permute-start(bf16[512,128]{1,0:T(8,128)(2,1)S(1)} %get-tuple-element.275), channel_id=1, source_target_pairs={{0,16},{4,132},{8,24},{12,140},{16,32},{20,148},{24,40},{28,156},{... | collective-permute-start | bytes 393224 | tf_op jit(solution)/shard_map/while/body/eval_jaxpr/ppermute | solution.py:70
  77.6 6.9 %collective-permute-start.1 = (bf16[512,128]{1,0:T(8,128)(2,1)S(1)}, bf16[512,128]{1,0:T(8,128)(2,1)S(1)}, u32[]{:S(2)}, u32[]{:S(2)}) collective-permute-start(bf16[512,128]{1,0:T(8,128)(2,1)S(1)} %get-tuple-element.275), channel_id=1, source_target_pairs={{0,56},{4,196},{8,0},{12,204},{16,8},{20,212},{24,16},{28,220},{32... | collective-permute-start | bytes 393224 | tf_op jit(solution)/shard_map/while/body/eval_jaxpr/ppermute | solution.py:70
  79.9 5.3 %collective-permute-start.2 = (bf16[512,128]{1,0:T(8,128)(2,1)S(1)}, bf16[512,128]{1,0:T(8,128)(2,1)S(1)}, u32[]{:S(2)}, u32[]{:S(2)}) collective-permute-start(bf16[512,128]{1,0:T(8,128)(2,1)S(1)} %get-tuple-element.275), channel_id=1, source_target_pairs={{0,8},{4,68},{8,16},{12,76},{16,24},{20,84},{24,32},{28,92},{32,40... | collective-permute-start | bytes 393224 | tf_op jit(solution)/shard_map/while/body/eval_jaxpr/ppermute | solution.py:70
  85.4 16.8 %collective-permute-start.8 = (bf16[4,512,128]{2,1,0:T(8,128)(2,1)S(1)}, bf16[4,512,128]{2,1,0:T(8,128)(2,1)S(1)}, u32[]{:S(2)}, u32[]{:S(2)}) collective-permute-start(bf16[4,512,128]{2,1,0:T(8,128)(2,1)S(1)} %select_select_fusion.4.refs_0_), channel_id=1, source_target_pairs={{0,64},{4,12},{8,72},{12,20},{16,80},{20,28},{24,88},{28,36},{32,9... | collective-permute-start | bytes 1572872 | tf_op jit(solution)/shard_map/while/body/eval_jaxpr/ppermute | solution.py:70
  86.8 18.6 %collective-permute-start.3 = (bf16[4,512,128]{2,1,0:T(8,128)(2,1)S(1)}, bf16[4,512,128]{2,1,0:T(8,128)(2,1)S(1)}, u32[]{:S(2)}, u32[]{:S(2)}) collective-permute-start(bf16[4,512,128]{2,1,0:T(8,128)(2,1)S(1)} %select_select_fusion.4.refs_0_), channel_id=1, source_target_pairs={{0,192},{4,60},{8,200},{12,4},{16,208},{20,12},{24,216},{28,20},{3... | collective-permute-start | bytes 1572872 | tf_op jit(solution)/shard_map/while/body/eval_jaxpr/ppermute | solution.py:70
  89.0 9.5 %collective-permute-start.4 = (bf16[512,128]{1,0:T(8,128)(2,1)S(1)}, bf16[512,128]{1,0:T(8,128)(2,1)S(1)}, u32[]{:S(2)}, u32[]{:S(2)}) collective-permute-start(bf16[512,128]{1,0:T(8,128)(2,1)S(1)} %get-tuple-element.275), channel_id=1, source_target_pairs={{0,48},{4,36},{8,56},{12,44},{16,0},{20,52},{24,8},{28,60},{32,16}... | collective-permute-start | bytes 393224 | tf_op jit(solution)/shard_map/while/body/eval_jaxpr/ppermute | solution.py:70
  98.6 5.9 %collective-permute-start.5 = (bf16[512,128]{1,0:T(8,128)(2,1)S(1)}, bf16[512,128]{1,0:T(8,128)(2,1)S(1)}, u32[]{:S(2)}, u32[]{:S(2)}) collective-permute-start(bf16[512,128]{1,0:T(8,128)(2,1)S(1)} %broadcast_select_fusion.8), channel_id=1, source_target_pairs={{0,16},{4,132},{8,24},{12,140},{16,32},{20,148},{24,40},{28,156},{... | collective-permute-start | bytes 393224 | tf_op jit(solution)/shard_map/while/body/eval_jaxpr/ppermute | solution.py:70
  99.6 5.8 %collective-permute-start.7 = (bf16[512,128]{1,0:T(8,128)(2,1)S(1)}, bf16[512,128]{1,0:T(8,128)(2,1)S(1)}, u32[]{:S(2)}, u32[]{:S(2)}) collective-permute-start(bf16[512,128]{1,0:T(8,128)(2,1)S(1)} %broadcast_select_fusion.8), channel_id=1, source_target_pairs={{0,8},{4,68},{8,16},{12,76},{16,24},{20,84},{24,32},{28,92},{32,40... | collective-permute-start | bytes 393224 | tf_op jit(solution)/shard_map/while/body/eval_jaxpr/ppermute | solution.py:70
  102.2 14.6 %collective-permute-start.9 = (bf16[4,512,128]{2,1,0:T(8,128)(2,1)S(1)}, bf16[4,512,128]{2,1,0:T(8,128)(2,1)S(1)}, u32[]{:S(2)}, u32[]{:S(2)}) collective-permute-start(bf16[4,512,128]{2,1,0:T(8,128)(2,1)S(1)} %collective-permute-done.8.refs_2_), channel_id=1, source_target_pairs={{0,64},{4,12},{8,72},{12,20},{16,80},{20,28},{24,88},{28,36},{32,9... | collective-permute-start | bytes 1572872 | tf_op jit(solution)/shard_map/while/body/eval_jaxpr/ppermute | solution.py:70
  105.6 12.7 %collective-permute-start.11 = (bf16[4,512,128]{2,1,0:T(8,128)(2,1)S(1)}, bf16[4,512,128]{2,1,0:T(8,128)(2,1)S(1)}, u32[]{:S(2)}, u32[]{:S(2)}) collective-permute-start(bf16[4,512,128]{2,1,0:T(8,128)(2,1)S(1)} %get-tuple-element.256), channel_id=1, source_target_pairs={{0,192},{4,60},{8,200},{12,4},{16,208},{20,12},{24,216},{28,20},{3... | collective-permute-start | bytes 1572872 | tf_op jit(solution)/shard_map/while/body/eval_jaxpr/ppermute | solution.py:70
  112.2 9.2 %collective-permute-start.15 = (bf16[4,512,128]{2,1,0:T(8,128)(2,1)S(1)}, bf16[4,512,128]{2,1,0:T(8,128)(2,1)S(1)}, u32[]{:S(2)}, u32[]{:S(2)}) collective-permute-start(bf16[4,512,128]{2,1,0:T(8,128)(2,1)S(1)} %select_select_fusion.4.refs_0_), channel_id=1, source_target_pairs={{0,4},{4,0},{1,5},{5,1},{2,6},{6,2},{3,7},{7,3},{8,12},{12,8},{9,1... | collective-permute-start | bytes 1572872 | tf_op jit(solution)/shard_map/while/body/eval_jaxpr/ppermute | solution.py:48
  115.5 10.4 %collective-permute-start.16 = (bf16[4,512,128]{2,1,0:T(8,128)(2,1)S(1)}, bf16[4,512,128]{2,1,0:T(8,128)(2,1)S(1)}, u32[]{:S(2)}, u32[]{:S(2)}) collective-permute-start(bf16[4,512,128]{2,1,0:T(8,128)(2,1)S(1)} %get-tuple-element.255.refs_1_), channel_id=1, source_target_pairs={{0,4},{4,0},{1,5},{5,1},{2,6},{6,2},{3,7},{7,3},{8,12},{12,8},{9,1... | collective-permute-start | bytes 1572872 | tf_op jit(solution)/shard_map/while/body/eval_jaxpr/ppermute | solution.py:48
  115.5 10.5 %collective-permute-start.17 = (bf16[4,512,128]{2,1,0:T(8,128)(2,1)S(1)}, bf16[4,512,128]{2,1,0:T(8,128)(2,1)S(1)}, u32[]{:S(2)}, u32[]{:S(2)}) collective-permute-start(bf16[4,512,128]{2,1,0:T(8,128)(2,1)S(1)} %collective-permute-done.8.refs_2_), channel_id=1, source_target_pairs={{0,4},{4,0},{1,5},{5,1},{2,6},{6,2},{3,7},{7,3},{8,12},{12,8},{9,1... | collective-permute-start | bytes 1572872 | tf_op jit(solution)/shard_map/while/body/eval_jaxpr/ppermute | solution.py:48
  116.9 9.6 %collective-permute-start.10 = (bf16[4,512,128]{2,1,0:T(8,128)(2,1)S(1)}, bf16[4,512,128]{2,1,0:T(8,128)(2,1)S(1)}, u32[]{:S(2)}, u32[]{:S(2)}) collective-permute-start(bf16[4,512,128]{2,1,0:T(8,128)(2,1)S(1)} %broadcast_select_fusion.10), channel_id=1, source_target_pairs={{0,64},{4,12},{8,72},{12,20},{16,80},{20,28},{24,88},{28,36},{32,9... | collective-permute-start | bytes 1572872 | tf_op jit(solution)/shard_map/while/body/eval_jaxpr/ppermute | solution.py:70
  118.3 12.0 %collective-permute-start.12 = (bf16[4,512,128]{2,1,0:T(8,128)(2,1)S(1)}, bf16[4,512,128]{2,1,0:T(8,128)(2,1)S(1)}, u32[]{:S(2)}, u32[]{:S(2)}) collective-permute-start(bf16[4,512,128]{2,1,0:T(8,128)(2,1)S(1)} %collective-permute-done.11.refs_5_), channel_id=1, source_target_pairs={{0,192},{4,60},{8,200},{12,4},{16,208},{20,12},{24,216},{28,20},{3... | collective-permute-start | bytes 1572872 | tf_op jit(solution)/shard_map/while/body/eval_jaxpr/ppermute | solution.py:70
  121.4 11.2 %collective-permute-start.18 = (bf16[4,512,128]{2,1,0:T(8,128)(2,1)S(1)}, bf16[4,512,128]{2,1,0:T(8,128)(2,1)S(1)}, u32[]{:S(2)}, u32[]{:S(2)}) collective-permute-start(bf16[4,512,128]{2,1,0:T(8,128)(2,1)S(1)} %collective-permute-done.3.refs_3_), channel_id=1, source_target_pairs={{0,4},{4,0},{1,5},{5,1},{2,6},{6,2},{3,7},{7,3},{8,12},{12,8},{9,1... | collective-permute-start | bytes 1572872 | tf_op jit(solution)/shard_map/while/body/eval_jaxpr/ppermute | solution.py:48
  125.9 6.7 %collective-permute-start.20 = (bf16[4,512,128]{2,1,0:T(8,128)(2,1)S(1)}, bf16[4,512,128]{2,1,0:T(8,128)(2,1)S(1)}, u32[]{:S(2)}, u32[]{:S(2)}) collective-permute-start(bf16[4,512,128]{2,1,0:T(8,128)(2,1)S(1)} %collective-permute-done.11.refs_5_), channel_id=1, source_target_pairs={{0,4},{4,0},{1,5},{5,1},{2,6},{6,2},{3,7},{7,3},{8,12},{12,8},{9,1... | collective-permute-start | bytes 1572872 | tf_op jit(solution)/shard_map/while/body/eval_jaxpr/ppermute | solution.py:48
  126.0 6.6 %collective-permute-start.19 = (bf16[4,512,128]{2,1,0:T(8,128)(2,1)S(1)}, bf16[4,512,128]{2,1,0:T(8,128)(2,1)S(1)}, u32[]{:S(2)}, u32[]{:S(2)}) collective-permute-start(bf16[4,512,128]{2,1,0:T(8,128)(2,1)S(1)} %collective-permute-done.9.refs_4_), channel_id=1, source_target_pairs={{0,4},{4,0},{1,5},{5,1},{2,6},{6,2},{3,7},{7,3},{8,12},{12,8},{9,1... | collective-permute-start | bytes 1572872 | tf_op jit(solution)/shard_map/while/body/eval_jaxpr/ppermute | solution.py:48
  126.5 11.6 %collective-permute-start.13 = (bf16[4,512,128]{2,1,0:T(8,128)(2,1)S(1)}, bf16[4,512,128]{2,1,0:T(8,128)(2,1)S(1)}, u32[]{:S(2)}, u32[]{:S(2)}) collective-permute-start(bf16[4,512,128]{2,1,0:T(8,128)(2,1)S(1)} %collective-permute-done.10.refs_0_), channel_id=1, source_target_pairs={{0,4},{4,0},{1,5},{5,1},{2,6},{6,2},{3,7},{7,3},{8,12},{12,8},{9,1... | collective-permute-start | bytes 1572872 | tf_op jit(solution)/shard_map/while/body/eval_jaxpr/ppermute | solution.py:48
  130.3 7.8 %collective-permute-start.14 = (bf16[4,512,128]{2,1,0:T(8,128)(2,1)S(1)}, bf16[4,512,128]{2,1,0:T(8,128)(2,1)S(1)}, u32[]{:S(2)}, u32[]{:S(2)}) collective-permute-start(bf16[4,512,128]{2,1,0:T(8,128)(2,1)S(1)} %collective-permute-done.12.refs_1_), channel_id=1, source_target_pairs={{0,4},{4,0},{1,5},{5,1},{2,6},{6,2},{3,7},{7,3},{8,12},{12,8},{9,1... | collective-permute-start | bytes 1572872 | tf_op jit(solution)/shard_map/while/body/eval_jaxpr/ppermute | solution.py:48
  141.3 5.4 %collective-permute-start.21 = (bf16[512,128]{1,0:T(8,128)(2,1)S(1)}, bf16[512,128]{1,0:T(8,128)(2,1)S(1)}, u32[]{:S(2)}, u32[]{:S(2)}) collective-permute-start(bf16[512,128]{1,0:T(8,128)(2,1)S(1)} %get-tuple-element.257), channel_id=1, source_target_pairs={{0,2},{1,3},{2,0},{3,1},{4,6},{5,7},{6,4},{7,5},{8,10},{9,11},{10,... | collective-permute-start | bytes 393224 | tf_op jit(solution)/shard_map/while/body/eval_jaxpr/ppermute | solution.py:48
  162.8 5.4 %collective-permute-start.28 = (f32[128,128]{1,0:T(8,128)S(1)}, f32[128,128]{1,0:T(8,128)S(1)}, u32[]{:S(2)}, u32[]{:S(2)}) collective-permute-start(f32[128,128]{1,0:T(8,128)S(1)} %add_add_fusion.2), channel_id=1, source_target_pairs={{0,64},{64,128},{128,192},{192,0},{1,65},{65,129},{129,193},{193,1... | collective-permute-start | bytes 196616 | tf_op jit(solution)/shard_map/ppermute | solution.py:48
  171.3 9.0 %collective-permute-start.34 = (f32[64,128]{1,0:T(8,128)S(1)}, f32[64,128]{1,0:T(8,128)S(1)}, u32[]{:S(2)}, u32[]{:S(2)}) collective-permute-start(f32[64,128]{1,0:T(8,128)S(1)} %slice_select_fusion), channel_id=1, source_target_pairs={{0,32},{8,40},{16,48},{24,56},{32,0},{40,8},{48,16},{56,24},{1,33}... | collective-permute-start | bytes 98312 | tf_op jit(solution)/shard_map/ppermute | solution.py:48
  174.8 5.6 %collective-permute-start.31 = (f32[128,128]{1,0:T(8,128)S(1)}, f32[128,128]{1,0:T(8,128)S(1)}, u32[]{:S(2)}, u32[]{:S(2)}) collective-permute-start(f32[128,128]{1,0:T(8,128)S(1)} %add_add_fusion.1), channel_id=1, source_target_pairs={{0,8},{4,60},{8,16},{12,4},{16,24},{20,12},{24,32},{28,20},{32,40}... | collective-permute-start | bytes 196616 | tf_op jit(solution)/shard_map/ppermute | solution.py:251
  175.1 6.7 %collective-permute-start.32 = (f32[128,128]{1,0:T(8,128)S(1)}, f32[128,128]{1,0:T(8,128)S(1)}, u32[]{:S(2)}, u32[]{:S(2)}) collective-permute-start(f32[128,128]{1,0:T(8,128)S(1)} %add_add_fusion.1), channel_id=1, source_target_pairs={{0,16},{4,52},{8,24},{12,60},{16,32},{20,4},{24,40},{28,12},{32,48... | collective-permute-start | bytes 196616 | tf_op jit(solution)/shard_map/ppermute | solution.py:251
  183.2 7.6 %collective-permute-start.35 = (f32[128,128]{1,0:T(8,128)S(1)}, f32[128,128]{1,0:T(8,128)S(1)}, u32[]{:S(2)}, u32[]{:S(2)}) collective-permute-start(f32[128,128]{1,0:T(8,128)S(1)} %maximum_add_fusion), channel_id=1, source_target_pairs={{0,4},{4,0},{1,5},{5,1},{2,6},{6,2},{3,7},{7,3},{8,12},{12,8},{9,1... | collective-permute-start | bytes 196616 | tf_op jit(solution)/shard_map/ppermute | solution.py:48
  (20 other events, 471.3 us)
